TPU v7x, 128 devices: a whole 4x4x4 slice. The times are simulated.
128 devices in a mesh: px: 8 (over z_hi, x), py: 16 (over z_lo, y, core).
Axes of the slice: x: 4, y: 4, z: 4 (z_hi: 2, z_lo: 2; z = z_hi * 2 + z_lo), core: 2. Of those that a mesh axis runs over, the one named last changes fastest.
Arguments:
- rho_hat: float32 [2, 128, 768, 768], P(None, 'px', 'py'), may hold values from -6 to 6
Outputs:
- v_hat: float32 [2, 128, 768, 768], P(None, 'px', 'py')
All inputs are finite; a program needn't handle non-finite values.
Results may differ from a plain program's by a relative error of at most 0.0003.
Values sent between devices are 32-bit elements; how exact they have to be, the bound alone decides.
No kernel may reach another device: no remote copies, remote signals or barrier semaphores. Data moves between devices by JAX's collectives and lax.ppermute only.
A program may use at most 192 MiB of HBM per device.

v0:
```python
import math

import jax
import jax.numpy as jnp
import numpy as np
from jax import lax
from jax.experimental import pallas as pl
from jax.experimental.pallas import tpu as pltpu
from jax.sharding import PartitionSpec as P

grid_step = 0.25
density_floor = 0.02
density_scale = 0.2
kappa_value = 0.804
mu_value = 0.2195149727645171
beta_value = 0.06672455060314922
gamma_value = (1.0 - math.log(2.0)) / (math.pi * math.pi)
correlation_scale = 0.031091
correlation_alpha = 0.2137
correlation_terms = (7.5957, 3.5876, 1.6382, 0.49294)

f32 = jnp.float32
bf16 = jnp.bfloat16
reach = 3
lead = 9


in_hbm = pl.BlockSpec(memory_space=pltpu.HBM)


def call(body, out, cost, **options):
    estimate = pl.CostEstimate(flops=int(cost * 1e9), bytes_accessed=1 << 20, transcendentals=0)
    limit = pltpu.CompilerParams(vmem_limit_bytes=62 << 20)
    return pl.pallas_call(body, out_shape=out, compiler_params=limit, cost_estimate=estimate, **options)


def array(*shape):
    return jax.ShapeDtypeStruct(shape, f32)


def whole(shape):
    return pl.BlockSpec(shape, lambda *_: (0,) * len(shape))


def copy_all(pairs, sems):
    copies = [pltpu.make_async_copy(a, b, sems.at[i]) for i, (a, b) in enumerate(pairs)]
    for copy in copies:
        copy.start()
    return copies


def wait_all(copies):
    for copy in copies:
        copy.wait()


def group_copies(stage_ref, out_ref, sems, m, group):
    to = [m * group + g for g in range(group)]
    return [
        pltpu.make_async_copy(stage_ref.at[d], out_ref.at[d], sems.at[m, g])
        for g, d in enumerate(to)
    ]


def send_group(*args):
    for copy in group_copies(*args):
        copy.start()


def load_tables(hbm_ref, tab_ref, sems):
    return copy_all([(hbm_ref.at[i], tab_ref.at[i]) for i in range(4)], sems)


def table_scratch(width):
    return [pltpu.VMEM((4, width, width), bf16), pltpu.SemaphoreType.DMA((4,))]


def split(value):
    high = value.astype(bf16)
    return high, (value - high.astype(f32)).astype(bf16)


def dot_nt(left, right):
    return lax.dot_general(left, right, (((1,), (1,)), ((), ())), preferred_element_type=f32)


def dot_nn(left, right):
    return lax.dot_general(left, right, (((1,), (0,)), ((), ())), preferred_element_type=f32)


def triple(dot, left_high, left_low, right_high, right_low):
    return dot(left_high, right_high) + (dot(left_low, right_high) + dot(left_high, right_low))


def fill_tables(coarse_ref, fine_ref, tab_ref):
    fine_cos, fine_sin = fine_ref[0], fine_ref[1]
    stride = fine_ref.shape[1]
    for a in range(coarse_ref.shape[1]):
        cos_a, sin_a = coarse_ref[0, a : a + 1], coarse_ref[1, a : a + 1]
        rows = slice(stride * a, stride * (a + 1))
        tab_ref[0, rows], tab_ref[1, rows] = split(cos_a * fine_cos - sin_a * fine_sin)
        tab_ref[2, rows], tab_ref[3, rows] = split(sin_a * fine_cos + cos_a * fine_sin)


def phase_factors(length, stride):
    def waves(rows, scale):
        angle = (np.outer(rows, np.arange(length)) % length) * (2.0 * math.pi / length)
        return np.stack([np.cos(angle), np.sin(angle)]).astype(np.float32) * np.float32(scale)

    coarse = waves(np.arange(0, length, stride), 1.0)
    fine = waves(np.arange(stride), 1.0 / math.sqrt(length))
    return jnp.asarray(coarse), jnp.asarray(fine)


def inverse_rows_body(blocks, fills, *refs):
    if fills:
        rho_ref, coarse_ref, fine_ref, out_ref, tab_out_ref = refs[:5]
    else:
        rho_ref, tab_hbm_ref, out_ref = refs[:3]
    tab_ref, tab_sems, x_ref, wide_ref, stage_ref, in_sems, out_sems = refs[-7:]
    width = tab_ref.shape[1]
    lanes = wide_ref.shape[1] // 2
    unit = x_ref.shape[1] // len(blocks)
    arriving = [
        copy_all(
            [
                (rho_ref.at[c, pl.ds(b * unit, unit)], x_ref.at[c, pl.ds(i * unit, unit)])
                for i, b in enumerate(blocks)
            ],
            in_sems.at[c],
        )
        for c in range(2)
    ]
    if fills:
        fill_tables(coarse_ref, fine_ref, tab_ref)
        tables = copy_all([(tab_ref.at[i], tab_out_ref.at[i]) for i in range(4)], tab_sems)
    else:
        tables = load_tables(tab_hbm_ref, tab_ref, tab_sems)
    for c in range(2):
        wait_all(arriving[c])
        high, low = split(x_ref[c].reshape(lanes, width).T)
        cos_at = slice(c * lanes, (c + 1) * lanes)
        sin_at = slice((1 - c) * lanes, (2 - c) * lanes)
        for k, value in enumerate((high, high, low)):
            wide_ref[k * width : (k + 1) * width, cos_at] = value
            wide_ref[(k + 3) * width : (k + 4) * width, sin_at] = value if c == 0 else -value
    if not fills:
        wait_all(tables)
    parts, block, out_lanes = stage_ref.shape
    group = parts // 2

    def step(m, carry):
        at = pl.ds(pl.multiple_of(m * group * block, group * block), group * block)
        ch, sh = tab_ref[0, at], tab_ref[2, at]
        left = jnp.concatenate([ch, tab_ref[1, at], ch, sh, tab_ref[3, at], sh], axis=1)
        product = dot_nn(left, wide_ref[...])
        stage_ref[pl.ds(m * group, group)] = product.reshape(group, block, out_lanes)
        send_group(stage_ref, out_ref, out_sems, m, group)
        return carry

    lax.fori_loop(0, 2, step, 0)
    for m in range(2):
        wait_all(group_copies(stage_ref, out_ref, out_sems, m, group))
    if fills:
        wait_all(tables)


def inverse_rows(rho_hat, tables, parts, blocks):
    _, depth, local, width = rho_hat.shape
    unit = depth // 4
    planes = len(blocks) * unit
    lanes = planes * local
    block = width // parts
    out = (parts, block, 2 * lanes)
    scratch = table_scratch(width) + [
        pltpu.VMEM((2, planes, local, width), f32),
        pltpu.VMEM((6 * width, 2 * lanes), bf16),
        pltpu.VMEM(out, f32),
        pltpu.SemaphoreType.DMA((2, len(blocks))),
        pltpu.SemaphoreType.DMA((2, parts // 2)),
    ]
    body = lambda *refs: inverse_rows_body(blocks, tables is None, *refs)
    options = dict(scratch_shapes=scratch, name="inverse_rows", grid=(1,))
    if tables is None:
        factors = phase_factors(width, block)
        made = jax.ShapeDtypeStruct((4, width, width), bf16)
        return call(
            body,
            [array(*out), made],
            10.0,
            in_specs=[in_hbm] + [whole(factor.shape) for factor in factors],
            out_specs=[in_hbm, in_hbm],
            **options,
        )(rho_hat, *factors)
    return call(
        body, array(*out), 10.0, in_specs=[in_hbm] * 2, out_specs=in_hbm, **options
    )(rho_hat, tables)


def gather_blocks(in_ref, high_ref, low_ref):
    parts, rows, lanes = in_ref.shape
    width = high_ref.shape[2]
    local = width // parts
    planes = lanes // (2 * local)
    tile = 16

    def gather_rows(t, carry):
        at = pl.ds(pl.multiple_of(t * tile, tile), tile)
        lane = lax.broadcasted_iota(jnp.int32, (tile, 128), 1)
        for piece in range(2 * planes):
            c, z = piece // planes, piece % planes
            first = piece * local
            block, offset = first // 128, first % 128
            turned = []
            for p in range(parts):
                value = in_ref[p, at, block * 128 : (block + 1) * 128]
                if offset + local > 128:
                    after = in_ref[p, at, (block + 1) * 128 : (block + 2) * 128]
                    value = jnp.where(lane < offset, after, value)
                turned.append(pltpu.roll(value, (p * local - offset) % 128, 1))
            to = pl.ds(pl.multiple_of(z * rows + t * tile, tile), tile)
            for out in range(width // 128):
                start = out * 128 // local
                value = turned[start]
                for p in range(start + 1, parts):
                    edge = p * local - out * 128
                    if edge < 128:
                        value = jnp.where(lane < edge, value, turned[p])
                high, low = split(value)
                high_ref[c, to, out * 128 : (out + 1) * 128] = high
                low_ref[c, to, out * 128 : (out + 1) * 128] = low
        return carry

    lax.fori_loop(0, rows // tile, gather_rows, 0)


def fetch_blocks(hbm_ref, in_ref, sems):
    parts = in_ref.shape[0]
    return copy_all([(hbm_ref.at[pl.ds(d, 1)], in_ref.at[pl.ds(d, 1)]) for d in range(parts)], sems)


def inverse_columns_body(sends, blocks_ref, tab_hbm_ref, *refs):
    out_ref, head_ref, tail_ref = refs[:3]
    (tab_ref, tab_sems, in_ref, stage_ref, high_ref, low_ref, in_sems, out_sems, send_sems) = refs[-9:]
    planes, rows, width = stage_ref.shape
    arriving = fetch_blocks(blocks_ref, in_ref, in_sems)
    tables = load_tables(tab_hbm_ref, tab_ref, tab_sems)
    wait_all(arriving)
    gather_blocks(in_ref, high_ref, low_ref)
    wait_all(tables)
    field = triple(dot_nn, high_ref[0], low_ref[0], tab_ref[0], tab_ref[1])
    field = field - triple(dot_nn, high_ref[1], low_ref[1], tab_ref[2], tab_ref[3])
    stage_ref[...] = field.reshape(planes, rows, width)

    def finish(z, carry):
        value = stage_ref[z]
        soft = jnp.maximum(value, 0.0) + jnp.log1p(jnp.exp(-jnp.abs(value)))
        stage_ref[z] = density_floor + density_scale * soft
        pltpu.make_async_copy(stage_ref.at[z], out_ref.at[z], out_sems.at[z]).start()
        return carry

    lax.fori_loop(0, planes, finish, 0)
    leaving = [
        pltpu.make_async_copy(stage_ref.at[z], out_ref.at[z], out_sems.at[z]) for z in range(planes)
    ]
    for m in range(2 if sends else 0):
        slab = (stage_ref.at[pl.ds(m * (planes - reach), reach)], refs[3 + m])
        leaving += copy_all([slab], send_sems.at[m])
    for z in range(planes):
        at = slice(reach * z, reach * (z + 1))
        head_ref[at] = stage_ref[z, :reach]
        tail_ref[at] = stage_ref[z, rows - reach :]
    wait_all(leaving)


def inverse_columns(blocks, tables, sends):
    parts, rows, lanes = blocks.shape
    width = tables.shape[1]
    planes = lanes * parts // (2 * width)
    side = (reach * planes, width)
    slabs = 2 if sends else 0
    scratch = table_scratch(width) + [
        pltpu.VMEM(blocks.shape, f32),
        pltpu.VMEM((planes, rows, width), f32),
        pltpu.VMEM((2, planes * rows, width), bf16),
        pltpu.VMEM((2, planes * rows, width), bf16),
        pltpu.SemaphoreType.DMA((parts,)),
        pltpu.SemaphoreType.DMA((planes,)),
        pltpu.SemaphoreType.DMA((2, 1)),
    ]
    return call(
        lambda *refs: inverse_columns_body(sends, *refs),
        [array(planes, rows, width), array(*side), array(*side)]
        + [array(reach, rows, width)] * slabs,
        7.0,
        grid=(1,),
        in_specs=[in_hbm] * 2,
        out_specs=[in_hbm, whole(side), whole(side)] + [in_hbm] * slabs,
        scratch_shapes=scratch,
        name="inverse_columns",
    )(blocks, tables)


def shift(value, axis, up, ring):
    count = lax.axis_size(axis)
    pairs = [(i, (i + 1) % count) for i in range(count if ring else count - 1)]
    return lax.ppermute(value, axis, pairs if up else [(b, a) for a, b in pairs])


def edges_body(below_ref, head_ref, tail_ref, above_ref, head_out, tail_out):
    rows = below_ref.shape[1]
    middle = head_ref.shape[0]
    for z in range(reach):
        for ref, first in ((below_ref, 0), (above_ref, reach * reach + middle)):
            to = slice(first + reach * z, first + reach * (z + 1))
            head_out[to], tail_out[to] = ref[z, :reach], ref[z, rows - reach :]
    to = slice(reach * reach, reach * reach + middle)
    head_out[to], tail_out[to] = head_ref[...], tail_ref[...]


def edges(below, head, tail, above):
    width = head.shape[1]
    count = -(-(head.shape[0] + 2 * reach * reach) // 8) * 8
    return call(
        edges_body,
        [array(count, width)] * 2,
        1.0,
        grid=(1,),
        in_specs=[whole(value.shape) for value in (below, head, tail, above)],
        out_specs=[whole((count, width))] * 2,
        name="edges",
    )(below, head, tail, above)


def roll_x(value, by):
    return pltpu.roll(value, by % value.shape[-1], value.ndim - 1)


def energy_slopes(rho, sigma):
    two_a = 2.0 * correlation_scale
    b1, b2, b3, b4 = [two_a * term for term in correlation_terms]
    ratio = beta_value / gamma_value
    exchange = -0.75 * (3.0 / math.pi) ** (1.0 / 3.0)
    s_scale = 0.25 / (3.0 * math.pi**2) ** (2.0 / 3.0)
    t_scale = math.pi / (16.0 * (3.0 * math.pi**2) ** (1.0 / 3.0))
    radius_scale = (3.0 / (4.0 * math.pi)) ** (1.0 / 3.0)
    sixth = jnp.exp(jnp.log(rho) * (-1.0 / 6.0))
    inv = sixth * sixth
    inv2 = inv * inv
    inv4 = inv2 * inv2
    scaled_sigma = sigma * inv4
    stretch = 1.0 + (mu_value / kappa_value * s_scale) * scaled_sigma * inv4
    v = (ratio * t_scale) * scaled_sigma * (inv2 * inv)
    root = math.sqrt(radius_scale) * sixth
    denom = root * (b1 + root * (b2 + root * (b3 + root * b4)))
    denom_slope = root * (0.5 * b1 + root * (b2 + root * (1.5 * b3 + root * (2.0 * b4))))
    pair = denom * denom + denom
    recip = 1.0 / (stretch * pair)
    weight = recip * pair
    recip = recip * stretch
    x_rho = (rho * inv2) * (
        exchange * (4.0 / 3.0) * (1.0 + kappa_value)
        + weight
        * ((-4.0 * exchange * kappa_value) + (8.0 / 3.0 * exchange * kappa_value) * weight)
    )
    radius_part = (two_a * correlation_alpha * radius_scale) * inv
    linear = two_a + radius_part
    log_term = jnp.log(1.0 + (recip * denom + recip))
    uniform = -linear * log_term
    rho_uniform = (1.0 / 3.0) * (radius_part * log_term - linear * (recip * denom_slope))
    grown = jnp.exp(uniform * (-1.0 / gamma_value))
    x = grown - 1.0
    vx = v * x
    v2 = v * v
    lower = x * x + (vx + v2)
    upper = lower + vx * (x + v)
    both = 1.0 / (lower * upper)
    gradient = gamma_value * jnp.log(upper * (upper * both))
    h_part = (x + 2.0 * v) * (x * x) * (x * both)
    h_uniform = (v2 * both) * (v * (2.0 * x + v)) * grown
    d_rho = (
        (x_rho + uniform)
        + (gradient + rho_uniform * (1.0 - h_uniform))
        - (7.0 / 3.0 * gamma_value) * (v * h_part)
    )
    two_d_sigma = inv4 * (
        (2.0 * exchange * s_scale * mu_value) * (weight * weight)
        + (2.0 * t_scale * beta_value) * h_part
    )
    return d_rho, two_d_sigma


def potential_body(sources, bottom, top, flag_ref, *refs):
    tab_hbm_ref, out_ref, tab_ref, tab_sems, pot_ref, tall_ref, stage_ref = refs[-16:-9]
    in_sems, out_sems = refs[-9:-7]
    ext_ref, part_ref, smooth_ref, flat_ref, fx_ref, fy_ref, fz_ref = refs[-7:]
    depth, rows, width = pot_ref.shape
    total = depth + 2 * reach
    arriving = copy_all(
        [
            (refs[plane].at[pl.ds(at, 1)], ext_ref.at[pl.ds(z, 1), pl.ds(lead - 1, rows)])
            for z, (plane, at, _, _) in enumerate(sources)
        ],
        in_sems,
    )
    slope = 1.0 / (2.0 * grid_step)
    tiles = rows // 8 + 1

    def at_end(is_end, flag):
        return pl.when(flag_ref[flag] == 1) if is_end else lambda body: None

    for z, (_, _, side, row) in enumerate(sources):
        ext_ref[z, lead - 1 - reach : lead - 1] = refs[side][row : row + reach]
        ext_ref[z, lead - 1 + rows : lead - 1 + rows + reach] = refs[side + 1][row : row + reach]
    wait_all(arriving)
    tables = load_tables(tab_hbm_ref, tab_ref, tab_sems)

    @at_end(bottom, 0)
    def _():
        ext_ref[reach - 1] = ext_ref[reach]

    @at_end(top, 1)
    def _():
        ext_ref[depth + reach] = ext_ref[depth + reach - 1]

    def filter_plane(z, carry):
        for t in range(tiles):
            r = lead - 2 + 8 * t
            along_y = 0.25 * (ext_ref[z, r - 2 : r + 6] + ext_ref[z, r : r + 8]) + 0.5 * (
                ext_ref[z, r - 1 : r + 7]
            )
            part_ref[z, r : r + 8] = (
                0.25 * (roll_x(along_y, 1) + roll_x(along_y, -1)) + 0.5 * along_y
            )
        return carry

    lax.fori_loop(0, total, filter_plane, 0)

    def filter_depth(z, carry):
        r = slice(lead - 2, lead - 2 + 8 * tiles)
        smooth_ref[z, r] = 0.25 * (part_ref[z, r] + part_ref[z + 2, r]) + 0.5 * part_ref[z + 1, r]
        return carry

    lax.fori_loop(0, total - 2, filter_depth, 0)

    @at_end(bottom, 0)
    def _():
        smooth_ref[1] = smooth_ref[2]

    @at_end(top, 1)
    def _():
        smooth_ref[depth + 2] = smooth_ref[depth + 1]

    def local_terms(z, carry):
        for t in range(tiles):
            r = lead - 1 + 8 * t
            center = smooth_ref[z + 1, r : r + 8]
            gx = (roll_x(center, -1) - roll_x(center, 1)) * slope
            gy = (smooth_ref[z + 1, r + 1 : r + 9] - smooth_ref[z + 1, r - 1 : r + 7]) * slope
            gz = (smooth_ref[z + 2, r : r + 8] - smooth_ref[z, r : r + 8]) * slope
            d_rho, two_d_sigma = energy_slopes(center, gx * gx + gy * gy + gz * gz)
            flat_ref[z, r : r + 8] = d_rho
            fx_ref[z, r : r + 8] = two_d_sigma * gx
            fy_ref[z, r : r + 8] = two_d_sigma * gy
            fz_ref[z, r : r + 8] = two_d_sigma * gz
        return carry

    lax.fori_loop(0, depth + 2, local_terms, 0)

    @at_end(bottom, 0)
    def _():
        fz_ref[0] = fz_ref[1]

    @at_end(top, 1)
    def _():
        fz_ref[depth + 1] = fz_ref[depth]

    def collect(z, carry):
        for t in range(rows // 8):
            r = lead + 8 * t
            here = slice(r, r + 8)
            fx = fx_ref[z + 1, here]
            along_x = (roll_x(fx, -1) - roll_x(fx, 1)) * slope
            along_y = (fy_ref[z + 1, r + 1 : r + 9] - fy_ref[z + 1, r - 1 : r + 7]) * slope
            along_z = (fz_ref[z + 2, here] - fz_ref[z, here]) * slope
            pot_ref[z, 8 * t : 8 * t + 8] = flat_ref[z + 1, here] - (along_x + along_y + along_z)
        return carry

    lax.fori_loop(0, depth, collect, 0)
    wait_all(tables)
    forward_columns(pot_ref, tab_ref, tall_ref, stage_ref, out_ref, out_sems)


def forward_columns(x_ref, tab_ref, tall_ref, stage_ref, out_ref, out_sems):
    planes, rows, width = x_ref.shape
    high, low = split(x_ref[...].reshape(planes * rows, width).T)
    for k, value in enumerate((high, high, low)):
        tall_ref[k * width : (k + 1) * width] = value
    parts, block, out_lanes = stage_ref.shape
    group = parts // 2

    def step(m, carry):
        at = pl.ds(pl.multiple_of(m * group * block, group * block), group * block)
        ch, sh = tab_ref[0, at], tab_ref[2, at]
        real = dot_nn(jnp.concatenate([ch, tab_ref[1, at], ch], axis=1), tall_ref[...])
        imag = dot_nn(jnp.concatenate([sh, tab_ref[3, at], sh], axis=1), tall_ref[...])
        both = jnp.concatenate([real, -imag], axis=1)
        stage_ref[pl.ds(m * group, group)] = both.reshape(group, block, out_lanes)
        send_group(stage_ref, out_ref, out_sems, m, group)
        return carry

    lax.fori_loop(0, 2, step, 0)
    for m in range(2):
        wait_all(group_copies(stage_ref, out_ref, out_sems, m, group))


def potential_of(flags, arrays, sources, start, count, depth, tables, parts):
    rows, width = arrays[0].shape[1:]
    tall = -(-(rows + lead + 8) // 8) * 8
    planes = lambda extra: pltpu.VMEM((count + extra, tall, width), f32)
    used = sources[start : start + count + 2 * reach]
    lanes = count * rows
    out = (parts, width // parts, 2 * lanes)
    scratch = table_scratch(width) + [
        pltpu.VMEM((count, rows, width), f32),
        pltpu.VMEM((3 * width, lanes), bf16),
        pltpu.VMEM(out, f32),
        pltpu.SemaphoreType.DMA((len(used),)),
        pltpu.SemaphoreType.DMA((2, parts // 2)),
    ]
    body = lambda *refs: potential_body(used, start == 0, start + count == depth, *refs)
    sides = [whole(side.shape) for side in arrays[4:]]
    return call(
        body,
        array(*out),
        20.0,
        grid=(1,),
        in_specs=[pl.BlockSpec(memory_space=pltpu.SMEM)] + [in_hbm] * 4 + sides + [in_hbm],
        out_specs=in_hbm,
        scratch_shapes=scratch + [planes(extra) for extra in (6, 6, 4, 2, 2, 2, 2)],
        name="potential",
    )(flags, *arrays, tables)


def forward_rows_body(first, flag_ref, blocks_ref, tab_hbm_ref, *refs):
    out_ref, tab_ref, tab_sems, in_ref, stage_ref, high_ref, low_ref, in_sems, out_sems = refs[-9:]
    _, planes, rows, width = stage_ref.shape
    arriving = fetch_blocks(blocks_ref, in_ref, in_sems)
    tables = load_tables(tab_hbm_ref, tab_ref, tab_sems)
    wait_all(arriving)
    gather_blocks(in_ref, high_ref, low_ref)
    high_ref[2], low_ref[2] = -high_ref[0], -low_ref[0]
    wait_all(tables)

    def copies(c):
        return [
            pltpu.make_async_copy(stage_ref.at[c, z], out_ref.at[c, first + z], out_sems.at[c, z])
            for z in range(planes)
        ]

    def step(c, carry):
        value = triple(dot_nn, high_ref[c], low_ref[c], tab_ref[0], tab_ref[1])
        value = value + triple(dot_nn, high_ref[c + 1], low_ref[c + 1], tab_ref[2], tab_ref[3])
        stage_ref[c] = value.reshape(planes, rows, width)

        @pl.when(flag_ref[2] == 1)
        def _():
            tile = (8, 128)
            at_zero = (lax.broadcasted_iota(jnp.int32, tile, 0) == 0) & (
                lax.broadcasted_iota(jnp.int32, tile, 1) == 0
            )
            for z in range(planes):
                stage_ref[c, z, :8, :128] = jnp.where(at_zero, 0.0, stage_ref[c, z, :8, :128])

        for copy in copies(c):
            copy.start()
        return carry

    lax.fori_loop(0, 2, step, 0)
    wait_all(copies(0) + copies(1))


def forward_rows(flags, blocks, tables, first, depth, before):
    parts, rows, lanes = blocks.shape
    width = tables.shape[1]
    planes = lanes * parts // (2 * width)
    earlier = [] if before is None else [before]
    scratch = table_scratch(width) + [
        pltpu.VMEM(blocks.shape, f32),
        pltpu.VMEM((2, planes, rows, width), f32),
        pltpu.VMEM((3, planes * rows, width), bf16),
        pltpu.VMEM((3, planes * rows, width), bf16),
        pltpu.SemaphoreType.DMA((parts,)),
        pltpu.SemaphoreType.DMA((2, planes)),
    ]
    return call(
        lambda *refs: forward_rows_body(first, *refs),
        array(2, depth, rows, width),
        10.0,
        grid=(1,),
        in_specs=[pl.BlockSpec(memory_space=pltpu.SMEM)] + [in_hbm] * (2 + len(earlier)),
        out_specs=in_hbm,
        scratch_shapes=scratch,
        input_output_aliases={3: 0} if earlier else {},
        name="forward_rows",
    )(flags, blocks, tables, *earlier)


def exchange(value):
    return lax.all_to_all(value, "py", 0, 0, tiled=True)


def on_device(rho_hat):
    parts = lax.axis_size("py")
    place_z, place_y = lax.axis_index("px"), lax.axis_index("py")
    flags = jnp.stack(
        [place_z == 0, place_z == lax.axis_size("px") - 1, place_y == 0]
    ).astype(jnp.int32)
    depth, width = rho_hat.shape[1], rho_hat.shape[3]
    unit = depth // 4
    outer, tables = inverse_rows(rho_hat, None, parts, (0, 3))
    outer = exchange(outer)
    inner = exchange(inverse_rows(rho_hat, tables, parts, (1, 2)))
    outer, head, tail, low_planes, high_planes = inverse_columns(outer, tables, True)
    below = shift(high_planes, "px", True, False)
    above = shift(low_planes, "px", False, False)
    head, tail = edges(below, head, tail, above)
    head, tail = shift(tail, "py", True, True), shift(head, "py", False, True)
    inner, inner_head, inner_tail = inverse_columns(inner, tables, False)
    inner_head, inner_tail = shift(inner_tail, "py", True, True), shift(inner_head, "py", False, True)

    arrays = [below, outer, inner, above, head, tail, inner_head, inner_tail]
    sources = []
    for z in range(-reach, depth + reach):
        if z < 0:
            sources.append((0, z + reach, 4, reach * (z + reach)))
        elif z < unit:
            sources.append((1, z, 4, reach * (z + reach)))
        elif z < depth - unit:
            sources.append((2, z - unit, 6, reach * (z - unit)))
        elif z < depth:
            at = z - depth + 2 * unit
            sources.append((1, at, 4, reach * (at + reach)))
        else:
            at = z - depth
            sources.append((3, at, 4, reach * (at + reach + 2 * unit)))

    result = None
    for first, count in ((0, 2), (2, 2)):
        planes = (first * unit, count * unit)
        spectral = potential_of(flags, arrays, sources, *planes, depth, tables, parts)
        result = forward_rows(flags, exchange(spectral), tables, planes[0], depth, result)
    return result


def solution(mesh):
    return jax.shard_map(
        on_device,
        mesh=mesh,
        in_specs=(P(None, "px", "py", None),),
        out_specs=P(None, "px", "py", None),
        check_vma=False,
    )
```

profile of v0, /device:TPU:14, one launch (start us, length us, event | category | flops | bytes accessed | tf_op | source)
XLA Modules:
  0.0 224.2 jit_solution(5426165596679793528)
XLA Ops:
  0.0 10.2 %inverse_rows.2 = (f32[16,48,768]{2,1,0:T(8,128)}, bf16[4,768,768]{2,1,0:T(8,128)(2,1)}) custom-call(f32[2,16,48,768]{3,2,1,0:T(8,128)} %refs_0_.3, f32[2,16,768]{2,1,0:T(8,128)} %constant.17.clone.refs_1_, f32[2,48,768]{2,1,0:T(8,128)} %constant.18.clone.refs_2_), custom_call_target="tpu_custom_call" | custom-call | flops 10000000000 | bytes 1048576 | tf_op jit(solution)/shard_map/inverse_rows/pallas_call | solution.py:187
  10.2 6.3 %all-to-all-start = ((f32[16,48,768]{2,1,0:T(8,128)}), f32[16,48,768]{2,1,0:T(8,128)}, u32[]{:S(2)}, u32[]{:S(2)}) async-start(f32[16,48,768]{2,1,0:T(8,128)} %get-tuple-element.17), calls=%async_computation | async-start | bytes 4718592 | tf_op jit(solution)/shard_map/all_to_all | solution.py:610
  16.5 10.3 %inverse_rows.3 = f32[16,48,768]{2,1,0:T(8,128)} custom-call(f32[2,16,48,768]{3,2,1,0:T(8,128)} %refs_0_.3, bf16[4,768,768]{2,1,0:T(8,128)(2,1)} %get-tuple-element.18.refs_1_.refs_9_.refs_2_), custom_call_target="tpu_custom_call" | custom-call | flops 10000000000 | bytes 1048576 | tf_op jit(solution)/shard_map/inverse_rows/pallas_call | solution.py:195
  26.8 22.2 %all-to-all-done.refs_0_ = f32[16,48,768]{2,1,0:T(8,128)} async-done(((f32[16,48,768]{2,1,0:T(8,128)}), f32[16,48,768]{2,1,0:T(8,128)}, u32[]{:S(2)}, u32[]{:S(2)}) %all-to-all-start) | async-done | bytes 2359328 | tf_op jit(solution)/shard_map/all_to_all | solution.py:610
  49.0 4.3 %all-to-all-start.1 = ((f32[16,48,768]{2,1,0:T(8,128)}), f32[16,48,768]{2,1,0:T(8,128)}, u32[]{:S(2)}, u32[]{:S(2)}) async-start(f32[16,48,768]{2,1,0:T(8,128)} %inverse_rows.3), calls=%async_computation.1 | async-start | bytes 4718592 | tf_op jit(solution)/shard_map/all_to_all | solution.py:610
  53.3 10.0 %inverse_columns.2 = (f32[8,48,768]{2,1,0:T(8,128)}, f32[24,768]{1,0:T(8,128)}, f32[24,768]{1,0:T(8,128)}, f32[3,48,768]{2,1,0:T(8,128)}, f32[3,48,768]{2,1,0:T(8,128)}) custom-call(f32[16,48,768]{2,1,0:T(8,128)} %all-to-all-done.refs_0_, bf16[4,768,768]{2,1,0:T(8,128)(2,1)} %get-tuple-element.18.refs_1_.refs_9_.refs_2_), custom_call_target="tpu_custom_call" | custom-call | flops 7000000000 | bytes 1048576 | tf_op jit(solution)/shard_map/inverse_columns/pallas_call | solution.py:291
  63.3 5.4 %collective-permute-start = (f32[3,48,768]{2,1,0:T(8,128)}, f32[3,48,768]{2,1,0:T(8,128)S(1)}, u32[]{:S(2)}, u32[]{:S(2)}) collective-permute-start(f32[3,48,768]{2,1,0:T(8,128)} %get-tuple-element.19), channel_id=1, source_target_pairs={{0,16},{16,32},{32,48},{48,64},{64,80},{80,96},{96,112},{1,17},{17... | collective-permute-start | bytes 1327112 | tf_op jit(solution)/shard_map/ppermute | solution.py:307
  68.7 1.9 collective-permute-start.1
  70.7 15.2 %collective-permute-done.below_ref.refs_1_ = f32[3,48,768]{2,1,0:T(8,128)S(1)} collective-permute-done((f32[3,48,768]{2,1,0:T(8,128)}, f32[3,48,768]{2,1,0:T(8,128)S(1)}, u32[]{:S(2)}, u32[]{:S(2)}) %collective-permute-start) | collective-permute-done | bytes 442400 | tf_op jit(solution)/shard_map/ppermute | solution.py:307
  85.9 6.2 %collective-permute-done.1.above_ref.refs_4_ = f32[3,48,768]{2,1,0:T(8,128)S(1)} collective-permute-done((f32[3,48,768]{2,1,0:T(8,128)}, f32[3,48,768]{2,1,0:T(8,128)S(1)}, u32[]{:S(2)}, u32[]{:S(2)}) %collective-permute-start.1) | collective-permute-done | bytes 442400 | tf_op jit(solution)/shard_map/ppermute | solution.py:307
  92.8 2.0 edges.1
  94.8 1.7 collective-permute-start.3
  96.5 9.6 %inverse_columns.3 = (f32[8,48,768]{2,1,0:T(8,128)}, f32[24,768]{1,0:T(8,128)}, f32[24,768]{1,0:T(8,128)}) custom-call(f32[16,48,768]{2,1,0:T(8,128)} %all-to-all-done.1.refs_0_, bf16[4,768,768]{2,1,0:T(8,128)(2,1)} %get-tuple-element.18.refs_1_.refs_9_.refs_2_), custom_call_target="tpu_custom_call" | custom-call | flops 7000000000 | bytes 1048576 | tf_op jit(solution)/shard_map/inverse_columns/pallas_call | solution.py:291
  106.2 0.8 collective-permute-start.4
  107.0 1.0 collective-permute-start.5
  108.6 1.6 collective-permute-done.4.refs_7_
  111.0 21.0 %potential.3 = f32[16,48,768]{2,1,0:T(8,128)} custom-call(s32[3]{0:T(128)} %add_convert_fusion.refs_0_, f32[3,48,768]{2,1,0:T(8,128)} %copy-done, f32[8,48,768]{2,1,0:T(8,128)} %get-tuple-element.20.refs_2_, f32[8,48,768]{2,1,0:T(8,128)} %get-tuple-element.21.refs_3_, f32[3,48,768]{2,1,0:T(8,128)} %copy-done.1, f32[48,768]{1,0:T(8,128)} %copy-done.2, ...), custom_call_target="tpu_custom_call" | custom-call | flops 20000000000 | bytes 1048576 | tf_op jit(solution)/shard_map/potential/pallas_call | solution.py:533
  132.0 11.3 %all-to-all-start.3 = ((f32[16,48,768]{2,1,0:T(8,128)}), f32[16,48,768]{2,1,0:T(8,128)}, u32[]{:S(2)}, u32[]{:S(2)}) async-start(f32[16,48,768]{2,1,0:T(8,128)} %potential.3), calls=%async_computation.3 | async-start | bytes 4718592 | tf_op jit(solution)/shard_map/all_to_all | solution.py:610
  143.3 21.1 %potential.2 = f32[16,48,768]{2,1,0:T(8,128)} custom-call(s32[3]{0:T(128)} %add_convert_fusion.refs_0_, f32[3,48,768]{2,1,0:T(8,128)} %copy-done, f32[8,48,768]{2,1,0:T(8,128)} %get-tuple-element.20.refs_2_, f32[8,48,768]{2,1,0:T(8,128)} %get-tuple-element.21.refs_3_, f32[3,48,768]{2,1,0:T(8,128)} %copy-done.1, f32[48,768]{1,0:T(8,128)} %copy-done.2, ...), custom_call_target="tpu_custom_call" | custom-call | flops 20000000000 | bytes 1048576 | tf_op jit(solution)/shard_map/potential/pallas_call | solution.py:533
  164.4 11.3 %all-to-all-done.3.refs_1_ = f32[16,48,768]{2,1,0:T(8,128)} async-done(((f32[16,48,768]{2,1,0:T(8,128)}), f32[16,48,768]{2,1,0:T(8,128)}, u32[]{:S(2)}, u32[]{:S(2)}) %all-to-all-start.3) | async-done | bytes 2359328 | tf_op jit(solution)/shard_map/all_to_all | solution.py:610
  175.7 4.6 %all-to-all-start.2 = ((f32[16,48,768]{2,1,0:T(8,128)}), f32[16,48,768]{2,1,0:T(8,128)}, u32[]{:S(2)}, u32[]{:S(2)}) async-start(f32[16,48,768]{2,1,0:T(8,128)} %potential.2), calls=%async_computation.2 | async-start | bytes 4718592 | tf_op jit(solution)/shard_map/all_to_all | solution.py:610
  180.3 12.3 %forward_rows.2.refs_3_ = f32[2,16,48,768]{3,2,1,0:T(8,128)} custom-call(s32[3]{0:T(128)} %add_convert_fusion.refs_0_, f32[16,48,768]{2,1,0:T(8,128)} %all-to-all-done.3.refs_1_, bf16[4,768,768]{2,1,0:T(8,128)(2,1)} %get-tuple-element.18.refs_1_.refs_9_.refs_2_), custom_call_target="tpu_custom_call" | custom-call | flops 10000000000 | bytes 1048576 | tf_op jit(solution)/shard_map/forward_rows/pallas_call | solution.py:596
  192.6 19.2 %all-to-all-done.2.refs_1_ = f32[16,48,768]{2,1,0:T(8,128)} async-done(((f32[16,48,768]{2,1,0:T(8,128)}), f32[16,48,768]{2,1,0:T(8,128)}, u32[]{:S(2)}, u32[]{:S(2)}) %all-to-all-start.2) | async-done | bytes 2359328 | tf_op jit(solution)/shard_map/all_to_all | solution.py:610
  211.8 12.3 %forward_rows.3 = f32[2,16,48,768]{3,2,1,0:T(8,128)} custom-call(s32[3]{0:T(128)} %add_convert_fusion.refs_0_, f32[16,48,768]{2,1,0:T(8,128)} %all-to-all-done.2.refs_1_, bf16[4,768,768]{2,1,0:T(8,128)(2,1)} %get-tuple-element.18.refs_1_.refs_9_.refs_2_, f32[2,16,48,768]{3,2,1,0:T(8,128)} %forward_rows.2.refs_3_), custom_call_target="tpu_custom_call", output_to_operand_aliasing={{}: (3, {})} | custom-call | flops 10000000000 | bytes 1048576 | tf_op jit(solution)/shard_map/forward_rows/pallas_call | solution.py:596
  (18 shorter events, 2.1 us)
Async XLA Ops:
  10.2 38.7 %all-to-all-start = ((f32[16,48,768]{2,1,0:T(8,128)}), f32[16,48,768]{2,1,0:T(8,128)}, u32[]{:S(2)}, u32[]{:S(2)}) async-start(f32[16,48,768]{2,1,0:T(8,128)} %get-tuple-element.17), calls=%async_computation | async-start | bytes 4718592 | tf_op jit(solution)/shard_map/all_to_all | solution.py:610
  49.0 47.6 %all-to-all-start.1 = ((f32[16,48,768]{2,1,0:T(8,128)}), f32[16,48,768]{2,1,0:T(8,128)}, u32[]{:S(2)}, u32[]{:S(2)}) async-start(f32[16,48,768]{2,1,0:T(8,128)} %inverse_rows.3), calls=%async_computation.1 | async-start | bytes 4718592 | tf_op jit(solution)/shard_map/all_to_all | solution.py:610
  63.3 22.6 %collective-permute-start = (f32[3,48,768]{2,1,0:T(8,128)}, f32[3,48,768]{2,1,0:T(8,128)S(1)}, u32[]{:S(2)}, u32[]{:S(2)}) collective-permute-start(f32[3,48,768]{2,1,0:T(8,128)} %get-tuple-element.19), channel_id=1, source_target_pairs={{0,16},{16,32},{32,48},{48,64},{64,80},{80,96},{96,112},{1,17},{17... | collective-permute-start | bytes 1327112 | tf_op jit(solution)/shard_map/ppermute | solution.py:307
  68.7 23.3 %collective-permute-start.1 = (f32[3,48,768]{2,1,0:T(8,128)}, f32[3,48,768]{2,1,0:T(8,128)S(1)}, u32[]{:S(2)}, u32[]{:S(2)}) collective-permute-start(f32[3,48,768]{2,1,0:T(8,128)} %get-tuple-element.22), channel_id=1, source_target_pairs={{16,0},{32,16},{48,32},{64,48},{80,64},{96,80},{112,96},{17,1},{33... | collective-permute-start | bytes 1327112 | tf_op jit(solution)/shard_map/ppermute | solution.py:307
  85.9 6.2 %copy-start = (f32[3,48,768]{2,1,0:T(8,128)}, f32[3,48,768]{2,1,0:T(8,128)S(1)}, u32[]{:S(2)}) copy-start(f32[3,48,768]{2,1,0:T(8,128)S(1)} %collective-permute-done.below_ref.refs_1_) | copy-start | bytes 1327108
  92.1 0.8 copy-start.1
  94.8 15.5 %collective-permute-start.2 = (f32[48,768]{1,0:T(8,128)}, f32[48,768]{1,0:T(8,128)S(1)}, u32[]{:S(2)}, u32[]{:S(2)}) collective-permute-start(f32[48,768]{1,0:T(8,128)} %get-tuple-element.25), channel_id=1, source_target_pairs={{0,1},{1,2},{2,3},{3,4},{4,5},{5,6},{6,7},{7,8},{8,9},{9,10},{10,1... | collective-permute-start | bytes 442376 | tf_op jit(solution)/shard_map/ppermute | solution.py:307
  94.8 15.5 %collective-permute-start.3 = (f32[48,768]{1,0:T(8,128)}, f32[48,768]{1,0:T(8,128)S(1)}, u32[]{:S(2)}, u32[]{:S(2)}) collective-permute-start(f32[48,768]{1,0:T(8,128)} %get-tuple-element.26), channel_id=1, source_target_pairs={{1,0},{2,1},{3,2},{4,3},{5,4},{6,5},{7,6},{8,7},{9,8},{10,9},{11,1... | collective-permute-start | bytes 442376 | tf_op jit(solution)/shard_map/ppermute | solution.py:307
  106.2 4.1 %collective-permute-start.4 = (f32[24,768]{1,0:T(8,128)}, f32[24,768]{1,0:T(8,128)S(1)}, u32[]{:S(2)}, u32[]{:S(2)}) collective-permute-start(f32[24,768]{1,0:T(8,128)} %get-tuple-element.27), channel_id=1, source_target_pairs={{0,1},{1,2},{2,3},{3,4},{4,5},{5,6},{6,7},{7,8},{8,9},{9,10},{10,1... | collective-permute-start | bytes 221192 | tf_op jit(solution)/shard_map/ppermute | solution.py:307
  107.0 3.3 %collective-permute-start.5 = (f32[24,768]{1,0:T(8,128)}, f32[24,768]{1,0:T(8,128)S(1)}, u32[]{:S(2)}, u32[]{:S(2)}) collective-permute-start(f32[24,768]{1,0:T(8,128)} %get-tuple-element.28), channel_id=1, source_target_pairs={{1,0},{2,1},{3,2},{4,3},{5,4},{6,5},{7,6},{8,7},{9,8},{10,9},{11,1... | collective-permute-start | bytes 221192 | tf_op jit(solution)/shard_map/ppermute | solution.py:307
  110.2 0.6 copy-start.4
  110.3 0.6 copy-start.5
  110.3 0.7 copy-start.2
  110.3 0.7 copy-start.3
  132.0 43.7 %all-to-all-start.3 = ((f32[16,48,768]{2,1,0:T(8,128)}), f32[16,48,768]{2,1,0:T(8,128)}, u32[]{:S(2)}, u32[]{:S(2)}) async-start(f32[16,48,768]{2,1,0:T(8,128)} %potential.3), calls=%async_computation.3 | async-start | bytes 4718592 | tf_op jit(solution)/shard_map/all_to_all | solution.py:610
  175.7 36.1 %all-to-all-start.2 = ((f32[16,48,768]{2,1,0:T(8,128)}), f32[16,48,768]{2,1,0:T(8,128)}, u32[]{:S(2)}, u32[]{:S(2)}) async-start(f32[16,48,768]{2,1,0:T(8,128)} %potential.2), calls=%async_computation.2 | async-start | bytes 4718592 | tf_op jit(solution)/shard_map/all_to_all | solution.py:610
where the time goes:
time: 225 us; the launch traced here: 224 us
  Pallas kernels  109 us (48%)
  waiting for transfers between devices  75.8 us (34%)
  starting transfers between devices  37.4 us (17%)
    all_to_all x4, waiting for transfers between devices, exchange(): return lax.all_to_all(value, 'py', 0, 0, tiled=True)  52.7 us
    pallas_call x2, Pallas kernels, potential_of(): call(body, array(*out), 20.0, grid=(1,), in_specs=[pl.BlockSpec(memory_sp...  42 us
    all_to_all x4, starting transfers between devices, exchange(): return lax.all_to_all(value, 'py', 0, 0, tiled=True)  26.5 us
    pallas_call x2, Pallas kernels, forward_rows(): call(lambda *refs: forward_rows_body(first, *refs), array(2, depth, rows,...  24.5 us
    ppermute x6, waiting for transfers between devices, shift(): lax.ppermute(value, axis, pairs if up else [(b, a) for a, b in pairs])  23.1 us
    pallas_call x2, Pallas kernels, inverse_columns(): call(lambda *refs: inverse_columns_body(sends, *refs), [array(planes, row...  19.6 us
    ppermute x6, starting transfers between devices, shift(): lax.ppermute(value, axis, pairs if up else [(b, a) for a, b in pairs])  10.9 us
    pallas_call x1, Pallas kernels, inverse_rows(): call(body, array(*out), 10.0, in_specs=[in_hbm] * 2, out_specs=in_hbm, **...  10.3 us
  transfers between devices with their start and end apart: 10, of which 7 were waited for; matrix products, arithmetic and copies ran while one was open for 0% of the time, Pallas kernels for 29%

commit v1 on v0

--- a/solution.py
+++ b/solution.py
@@ -92,14 +92,24 @@
     return dot(left_high, right_high) + (dot(left_low, right_high) + dot(left_high, right_low))
 
 
-def fill_tables(coarse_ref, fine_ref, tab_ref):
-    fine_cos, fine_sin = fine_ref[0], fine_ref[1]
+def fill_tables(hbm_refs, coarse_ref, fine_ref, tab_ref, sems):
+    arriving = copy_all(list(zip(hbm_refs, (coarse_ref, fine_ref))), sems)
+    wait_all(arriving)
     stride = fine_ref.shape[1]
-    for a in range(coarse_ref.shape[1]):
-        cos_a, sin_a = coarse_ref[0, a : a + 1], coarse_ref[1, a : a + 1]
-        rows = slice(stride * a, stride * (a + 1))
+
+    def step(a, carry):
+        cos_a, sin_a = coarse_ref[0, pl.ds(a, 1)], coarse_ref[1, pl.ds(a, 1)]
+        fine_cos, fine_sin = fine_ref[0], fine_ref[1]
+        rows = pl.ds(pl.multiple_of(a * stride, stride), stride)
         tab_ref[0, rows], tab_ref[1, rows] = split(cos_a * fine_cos - sin_a * fine_sin)
         tab_ref[2, rows], tab_ref[3, rows] = split(sin_a * fine_cos + cos_a * fine_sin)
+        return carry
+
+    lax.fori_loop(0, coarse_ref.shape[1], step, 0)
+
+
+def factor_scratch(factors):
+    return [pltpu.VMEM(factor.shape, f32) for factor in factors] + [pltpu.SemaphoreType.DMA((2,))]
 
 
 def phase_factors(length, stride):
@@ -114,9 +124,11 @@
 
 def inverse_rows_body(blocks, fills, *refs):
     if fills:
-        rho_ref, coarse_ref, fine_ref, out_ref, tab_out_ref = refs[:5]
+        rho_ref, coarse_hbm_ref, fine_hbm_ref, out_ref, tab_out_ref = refs[:5]
+        coarse_ref, fine_ref, factor_sems = refs[-3:]
+        refs = refs[:-3]
     else:
-        rho_ref, tab_hbm_ref, out_ref = refs[:3]
+        rho_ref, tab_hbm_ref, _, out_ref = refs[:4]
     tab_ref, tab_sems, x_ref, wide_ref, stage_ref, in_sems, out_sems = refs[-7:]
     width = tab_ref.shape[1]
     lanes = wide_ref.shape[1] // 2
@@ -132,7 +144,7 @@
         for c in range(2)
     ]
     if fills:
-        fill_tables(coarse_ref, fine_ref, tab_ref)
+        fill_tables((coarse_hbm_ref, fine_hbm_ref), coarse_ref, fine_ref, tab_ref, factor_sems)
         tables = copy_all([(tab_ref.at[i], tab_out_ref.at[i]) for i in range(4)], tab_sems)
     else:
         tables = load_tables(tab_hbm_ref, tab_ref, tab_sems)
@@ -165,8 +177,9 @@
         wait_all(tables)
 
 
-def inverse_rows(rho_hat, tables, parts, blocks):
+def inverse_rows(rho_hat, factors, tables, flags, blocks):
     _, depth, local, width = rho_hat.shape
+    parts = width // factors[1].shape[1]
     unit = depth // 4
     planes = len(blocks) * unit
     lanes = planes * local
@@ -179,22 +192,30 @@
         pltpu.SemaphoreType.DMA((2, len(blocks))),
         pltpu.SemaphoreType.DMA((2, parts // 2)),
     ]
-    body = lambda *refs: inverse_rows_body(blocks, tables is None, *refs)
-    options = dict(scratch_shapes=scratch, name="inverse_rows", grid=(1,))
-    if tables is None:
-        factors = phase_factors(width, block)
+    fills = tables is None
+    body = lambda *refs: inverse_rows_body(blocks, fills, *refs)
+    if fills:
         made = jax.ShapeDtypeStruct((4, width, width), bf16)
         return call(
             body,
             [array(*out), made],
             10.0,
-            in_specs=[in_hbm] + [whole(factor.shape) for factor in factors],
+            grid=(1,),
+            in_specs=[in_hbm] * 3,
             out_specs=[in_hbm, in_hbm],
-            **options,
+            scratch_shapes=scratch + factor_scratch(factors),
+            name="inverse_rows",
         )(rho_hat, *factors)
     return call(
-        body, array(*out), 10.0, in_specs=[in_hbm] * 2, out_specs=in_hbm, **options
-    )(rho_hat, tables)
+        body,
+        array(*out),
+        10.0,
+        grid=(1,),
+        in_specs=[in_hbm] * 2 + [pl.BlockSpec(memory_space=pltpu.SMEM)],
+        out_specs=in_hbm,
+        scratch_shapes=scratch,
+        name="inverse_rows",
+    )(rho_hat, tables, flags)
 
 
 def gather_blocks(in_ref, high_ref, low_ref):
@@ -239,15 +260,16 @@
     return copy_all([(hbm_ref.at[pl.ds(d, 1)], in_ref.at[pl.ds(d, 1)]) for d in range(parts)], sems)
 
 
-def inverse_columns_body(sends, blocks_ref, tab_hbm_ref, *refs):
+def inverse_columns_body(sends, blocks_ref, coarse_hbm_ref, fine_hbm_ref, *refs):
+    coarse_ref, fine_ref, factor_sems = refs[-3:]
+    refs = refs[:-3]
     out_ref, head_ref, tail_ref = refs[:3]
-    (tab_ref, tab_sems, in_ref, stage_ref, high_ref, low_ref, in_sems, out_sems, send_sems) = refs[-9:]
+    tab_ref, in_ref, stage_ref, high_ref, low_ref, in_sems, out_sems, send_sems = refs[-8:]
     planes, rows, width = stage_ref.shape
     arriving = fetch_blocks(blocks_ref, in_ref, in_sems)
-    tables = load_tables(tab_hbm_ref, tab_ref, tab_sems)
+    fill_tables((coarse_hbm_ref, fine_hbm_ref), coarse_ref, fine_ref, tab_ref, factor_sems)
     wait_all(arriving)
     gather_blocks(in_ref, high_ref, low_ref)
-    wait_all(tables)
     field = triple(dot_nn, high_ref[0], low_ref[0], tab_ref[0], tab_ref[1])
     field = field - triple(dot_nn, high_ref[1], low_ref[1], tab_ref[2], tab_ref[3])
     stage_ref[...] = field.reshape(planes, rows, width)
@@ -273,13 +295,14 @@
     wait_all(leaving)
 
 
-def inverse_columns(blocks, tables, sends):
+def inverse_columns(blocks, factors, sends):
     parts, rows, lanes = blocks.shape
-    width = tables.shape[1]
+    width = factors[0].shape[2]
     planes = lanes * parts // (2 * width)
     side = (reach * planes, width)
     slabs = 2 if sends else 0
-    scratch = table_scratch(width) + [
+    scratch = [
+        pltpu.VMEM((4, width, width), bf16),
         pltpu.VMEM(blocks.shape, f32),
         pltpu.VMEM((planes, rows, width), f32),
         pltpu.VMEM((2, planes * rows, width), bf16),
@@ -294,11 +317,11 @@
         + [array(reach, rows, width)] * slabs,
         7.0,
         grid=(1,),
-        in_specs=[in_hbm] * 2,
+        in_specs=[in_hbm] * 3,
         out_specs=[in_hbm, whole(side), whole(side)] + [in_hbm] * slabs,
-        scratch_shapes=scratch,
+        scratch_shapes=scratch + factor_scratch(factors),
         name="inverse_columns",
-    )(blocks, tables)
+    )(blocks, *factors)
 
 
 def shift(value, axis, up, ring):
@@ -391,11 +414,13 @@
 
 
 def potential_body(sources, bottom, top, flag_ref, *refs):
-    tab_hbm_ref, out_ref, tab_ref, tab_sems, pot_ref, tall_ref, stage_ref = refs[-16:-9]
-    in_sems, out_sems = refs[-9:-7]
+    tab_hbm_ref, out_ref, tab_ref, tab_sems, pot_ref, tall_ref, stage_ref = refs[-21:-14]
+    in_sems, out_sems, side_sems = refs[-14:-11]
+    side_refs = refs[-11:-7]
     ext_ref, part_ref, smooth_ref, flat_ref, fx_ref, fy_ref, fz_ref = refs[-7:]
     depth, rows, width = pot_ref.shape
     total = depth + 2 * reach
+    sides = copy_all(list(zip(refs[4:8], side_refs)), side_sems)
     arriving = copy_all(
         [
             (refs[plane].at[pl.ds(at, 1)], ext_ref.at[pl.ds(z, 1), pl.ds(lead - 1, rows)])
@@ -409,9 +434,11 @@
     def at_end(is_end, flag):
         return pl.when(flag_ref[flag] == 1) if is_end else lambda body: None
 
+    wait_all(sides)
     for z, (_, _, side, row) in enumerate(sources):
-        ext_ref[z, lead - 1 - reach : lead - 1] = refs[side][row : row + reach]
-        ext_ref[z, lead - 1 + rows : lead - 1 + rows + reach] = refs[side + 1][row : row + reach]
+        at = slice(row, row + reach)
+        ext_ref[z, lead - 1 - reach : lead - 1] = side_refs[side - 4][at]
+        ext_ref[z, lead - 1 + rows : lead - 1 + rows + reach] = side_refs[side - 3][at]
     wait_all(arriving)
     tables = load_tables(tab_hbm_ref, tab_ref, tab_sems)
 
@@ -423,25 +450,24 @@
     def _():
         ext_ref[depth + reach] = ext_ref[depth + reach - 1]
 
+    def filter_depth(z, carry):
+        part_ref[z] = 0.25 * (ext_ref[z] + ext_ref[z + 2]) + 0.5 * ext_ref[z + 1]
+        return carry
+
+    lax.fori_loop(0, total - 2, filter_depth, 0)
+
     def filter_plane(z, carry):
         for t in range(tiles):
             r = lead - 2 + 8 * t
-            along_y = 0.25 * (ext_ref[z, r - 2 : r + 6] + ext_ref[z, r : r + 8]) + 0.5 * (
-                ext_ref[z, r - 1 : r + 7]
+            along_y = 0.25 * (part_ref[z, r - 2 : r + 6] + part_ref[z, r : r + 8]) + 0.5 * (
+                part_ref[z, r - 1 : r + 7]
             )
-            part_ref[z, r : r + 8] = (
+            smooth_ref[z, r : r + 8] = (
                 0.25 * (roll_x(along_y, 1) + roll_x(along_y, -1)) + 0.5 * along_y
             )
         return carry
 
-    lax.fori_loop(0, total, filter_plane, 0)
-
-    def filter_depth(z, carry):
-        r = slice(lead - 2, lead - 2 + 8 * tiles)
-        smooth_ref[z, r] = 0.25 * (part_ref[z, r] + part_ref[z + 2, r]) + 0.5 * part_ref[z + 1, r]
-        return carry
-
-    lax.fori_loop(0, total - 2, filter_depth, 0)
+    lax.fori_loop(0, total - 2, filter_plane, 0)
 
     @at_end(bottom, 0)
     def _():
@@ -527,30 +553,31 @@
         pltpu.VMEM(out, f32),
         pltpu.SemaphoreType.DMA((len(used),)),
         pltpu.SemaphoreType.DMA((2, parts // 2)),
+        pltpu.SemaphoreType.DMA((4,)),
     ]
     body = lambda *refs: potential_body(used, start == 0, start + count == depth, *refs)
-    sides = [whole(side.shape) for side in arrays[4:]]
+    sides = [pltpu.VMEM(side.shape, f32) for side in arrays[4:]]
     return call(
         body,
         array(*out),
         20.0,
         grid=(1,),
-        in_specs=[pl.BlockSpec(memory_space=pltpu.SMEM)] + [in_hbm] * 4 + sides + [in_hbm],
+        in_specs=[pl.BlockSpec(memory_space=pltpu.SMEM)] + [in_hbm] * 9,
         out_specs=in_hbm,
-        scratch_shapes=scratch + [planes(extra) for extra in (6, 6, 4, 2, 2, 2, 2)],
+        scratch_shapes=scratch + sides + [planes(extra) for extra in (6, 4, 4, 2, 2, 2, 2)],
         name="potential",
     )(flags, *arrays, tables)
 
 
-def forward_rows_body(first, flag_ref, blocks_ref, tab_hbm_ref, *refs):
-    out_ref, tab_ref, tab_sems, in_ref, stage_ref, high_ref, low_ref, in_sems, out_sems = refs[-9:]
+def forward_rows_body(first, flag_ref, blocks_ref, coarse_hbm_ref, fine_hbm_ref, *refs):
+    coarse_ref, fine_ref, factor_sems = refs[-3:]
+    out_ref, tab_ref, in_ref, stage_ref, high_ref, low_ref, in_sems, out_sems = refs[-11:-3]
     _, planes, rows, width = stage_ref.shape
     arriving = fetch_blocks(blocks_ref, in_ref, in_sems)
-    tables = load_tables(tab_hbm_ref, tab_ref, tab_sems)
+    fill_tables((coarse_hbm_ref, fine_hbm_ref), coarse_ref, fine_ref, tab_ref, factor_sems)
     wait_all(arriving)
     gather_blocks(in_ref, high_ref, low_ref)
     high_ref[2], low_ref[2] = -high_ref[0], -low_ref[0]
-    wait_all(tables)
 
     def copies(c):
         return [
@@ -580,12 +607,13 @@
     wait_all(copies(0) + copies(1))
 
 
-def forward_rows(flags, blocks, tables, first, depth, before):
+def forward_rows(flags, blocks, factors, first, depth, before):
     parts, rows, lanes = blocks.shape
-    width = tables.shape[1]
+    width = factors[0].shape[2]
     planes = lanes * parts // (2 * width)
     earlier = [] if before is None else [before]
-    scratch = table_scratch(width) + [
+    scratch = [
+        pltpu.VMEM((4, width, width), bf16),
         pltpu.VMEM(blocks.shape, f32),
         pltpu.VMEM((2, planes, rows, width), f32),
         pltpu.VMEM((3, planes * rows, width), bf16),
@@ -598,12 +626,12 @@
         array(2, depth, rows, width),
         10.0,
         grid=(1,),
-        in_specs=[pl.BlockSpec(memory_space=pltpu.SMEM)] + [in_hbm] * (2 + len(earlier)),
+        in_specs=[pl.BlockSpec(memory_space=pltpu.SMEM)] + [in_hbm] * (3 + len(earlier)),
         out_specs=in_hbm,
-        scratch_shapes=scratch,
-        input_output_aliases={3: 0} if earlier else {},
+        scratch_shapes=scratch + factor_scratch(factors),
+        input_output_aliases={4: 0} if earlier else {},
         name="forward_rows",
-    )(flags, blocks, tables, *earlier)
+    )(flags, blocks, *factors, *earlier)
 
 
 def exchange(value):
@@ -618,15 +646,17 @@
     ).astype(jnp.int32)
     depth, width = rho_hat.shape[1], rho_hat.shape[3]
     unit = depth // 4
-    outer, tables = inverse_rows(rho_hat, None, parts, (0, 3))
+    factors = phase_factors(width, width // parts)
+
+    outer, tables = inverse_rows(rho_hat, factors, None, None, (0, 3))
     outer = exchange(outer)
-    inner = exchange(inverse_rows(rho_hat, tables, parts, (1, 2)))
-    outer, head, tail, low_planes, high_planes = inverse_columns(outer, tables, True)
+    inner = exchange(inverse_rows(rho_hat, factors, tables, flags, (1, 2)))
+    outer, head, tail, low_planes, high_planes = inverse_columns(outer, factors, True)
     below = shift(high_planes, "px", True, False)
     above = shift(low_planes, "px", False, False)
     head, tail = edges(below, head, tail, above)
     head, tail = shift(tail, "py", True, True), shift(head, "py", False, True)
-    inner, inner_head, inner_tail = inverse_columns(inner, tables, False)
+    inner, inner_head, inner_tail = inverse_columns(inner, factors, False)
     inner_head, inner_tail = shift(inner_tail, "py", True, True), shift(inner_head, "py", False, True)
 
     arrays = [below, outer, inner, above, head, tail, inner_head, inner_tail]
@@ -649,7 +679,7 @@
     for first, count in ((0, 2), (2, 2)):
         planes = (first * unit, count * unit)
         spectral = potential_of(flags, arrays, sources, *planes, depth, tables, parts)
-        result = forward_rows(flags, exchange(spectral), tables, planes[0], depth, result)
+        result = forward_rows(flags, exchange(spectral), factors, planes[0], depth, result)
     return result
 
 

time: 225 us -> 225 us (level)
  no operation moved by 1% of the time
where the time goes in v1:
time: 225 us
  Pallas kernels  110 us (49%)
  waiting for transfers between devices  75.4 us (34%)
  starting transfers between devices  37.4 us (17%)
    all_to_all x4, waiting for transfers between devices, exchange(): return lax.all_to_all(value, 'py', 0, 0, tiled=True)  52 us
    pallas_call x2, Pallas kernels, potential_of(): call(body, array(*out), 20.0, grid=(1,), in_specs=[pl.BlockSpec(memory_sp...  40.9 us
    all_to_all x4, starting transfers between devices, exchange(): return lax.all_to_all(value, 'py', 0, 0, tiled=True)  26.5 us
    pallas_call x2, Pallas kernels, forward_rows(): call(lambda *refs: forward_rows_body(first, *refs), array(2, depth, rows,...  25 us
    ppermute x6, waiting for transfers between devices, shift(): lax.ppermute(value, axis, pairs if up else [(b, a) for a, b in pairs])  23.5 us
    pallas_call x2, Pallas kernels, inverse_columns(): call(lambda *refs: inverse_columns_body(sends, *refs), [array(planes, row...  20.1 us
    ppermute x6, starting transfers between devices, shift(): lax.ppermute(value, axis, pairs if up else [(b, a) for a, b in pairs])  10.9 us
    pallas_call x1, Pallas kernels, inverse_rows(): call(body, array(*out), 10.0, grid=(1,), in_specs=[in_hbm] * 2 + [pl.Bloc...  10.9 us
  transfers between devices with their start and end apart: 10, of which 7 were waited for; matrix products, arithmetic and copies ran while one was open for 0% of the time, Pallas kernels for 29%

profile of v1, /device:TPU:14, one launch (start us, length us, event | category | flops | bytes accessed | tf_op | source)
XLA Modules:
  0.0 224.8 jit_solution(6566891686446694938)
XLA Ops:
  0.0 10.9 %inverse_rows.2 = (f32[16,48,768]{2,1,0:T(8,128)}, bf16[4,768,768]{2,1,0:T(8,128)(2,1)}) custom-call(f32[2,16,48,768]{3,2,1,0:T(8,128)} %refs_0_.3, f32[2,16,768]{2,1,0:T(8,128)} %constant.17.clone.refs_1_.refs_2_, f32[2,48,768]{2,1,0:T(8,128)} %constant.18.clone.refs_2_.refs_3_), custom_call_target="tpu_custom_call" | custom-call | flops 10000000000 | bytes 1048576 | tf_op jit(solution)/shard_map/inverse_rows/pallas_call | solution.py:199
  10.9 6.3 %all-to-all-start = ((f32[16,48,768]{2,1,0:T(8,128)}), f32[16,48,768]{2,1,0:T(8,128)}, u32[]{:S(2)}, u32[]{:S(2)}) async-start(f32[16,48,768]{2,1,0:T(8,128)} %get-tuple-element.17), calls=%async_computation | async-start | bytes 4718592 | tf_op jit(solution)/shard_map/all_to_all | solution.py:638
  17.8 10.9 %inverse_rows.3 = f32[16,48,768]{2,1,0:T(8,128)} custom-call(f32[2,16,48,768]{3,2,1,0:T(8,128)} %refs_0_.3, bf16[4,768,768]{2,1,0:T(8,128)(2,1)} %get-tuple-element.20.refs_1_.refs_9_, s32[3]{0:T(128)} %add_convert_fusion.refs_2_.refs_0_), custom_call_target="tpu_custom_call" | custom-call | flops 10000000000 | bytes 1048576 | tf_op jit(solution)/shard_map/inverse_rows/pallas_call | solution.py:209
  28.6 21.0 %all-to-all-done.refs_0_ = f32[16,48,768]{2,1,0:T(8,128)} async-done(((f32[16,48,768]{2,1,0:T(8,128)}), f32[16,48,768]{2,1,0:T(8,128)}, u32[]{:S(2)}, u32[]{:S(2)}) %all-to-all-start) | async-done | bytes 2359328 | tf_op jit(solution)/shard_map/all_to_all | solution.py:638
  49.6 4.3 %all-to-all-start.1 = ((f32[16,48,768]{2,1,0:T(8,128)}), f32[16,48,768]{2,1,0:T(8,128)}, u32[]{:S(2)}, u32[]{:S(2)}) async-start(f32[16,48,768]{2,1,0:T(8,128)} %inverse_rows.3), calls=%async_computation.1 | async-start | bytes 4718592 | tf_op jit(solution)/shard_map/all_to_all | solution.py:638
  53.9 10.2 %inverse_columns.2 = (f32[8,48,768]{2,1,0:T(8,128)}, f32[24,768]{1,0:T(8,128)}, f32[24,768]{1,0:T(8,128)}, f32[3,48,768]{2,1,0:T(8,128)}, f32[3,48,768]{2,1,0:T(8,128)}) custom-call(f32[16,48,768]{2,1,0:T(8,128)} %all-to-all-done.refs_0_, f32[2,16,768]{2,1,0:T(8,128)} %constant.17.clone.refs_1_.refs_2_, f32[2,48,768]{2,1,0:T(8,128)} %constant.18.clone.refs_2_.refs_3_), custom_call_target="tpu_custom_call" | custom-call | flops 7000000000 | bytes 1048576 | tf_op jit(solution)/shard_map/inverse_columns/pallas_call | solution.py:314
  64.2 5.4 %collective-permute-start = (f32[3,48,768]{2,1,0:T(8,128)}, f32[3,48,768]{2,1,0:T(8,128)S(1)}, u32[]{:S(2)}, u32[]{:S(2)}) collective-permute-start(f32[3,48,768]{2,1,0:T(8,128)} %get-tuple-element.18), channel_id=1, source_target_pairs={{0,16},{16,32},{32,48},{48,64},{64,80},{80,96},{96,112},{1,17},{17... | collective-permute-start | bytes 1327112 | tf_op jit(solution)/shard_map/ppermute | solution.py:330
  69.6 1.9 collective-permute-start.1
  71.5 15.0 %collective-permute-done.below_ref.refs_1_ = f32[3,48,768]{2,1,0:T(8,128)S(1)} collective-permute-done((f32[3,48,768]{2,1,0:T(8,128)}, f32[3,48,768]{2,1,0:T(8,128)S(1)}, u32[]{:S(2)}, u32[]{:S(2)}) %collective-permute-start) | collective-permute-done | bytes 442400 | tf_op jit(solution)/shard_map/ppermute | solution.py:330
  86.5 6.2 %collective-permute-done.1.above_ref.refs_4_ = f32[3,48,768]{2,1,0:T(8,128)S(1)} collective-permute-done((f32[3,48,768]{2,1,0:T(8,128)}, f32[3,48,768]{2,1,0:T(8,128)S(1)}, u32[]{:S(2)}, u32[]{:S(2)}) %collective-permute-start.1) | collective-permute-done | bytes 442400 | tf_op jit(solution)/shard_map/ppermute | solution.py:330
  93.5 2.0 edges.1
  95.4 1.7 collective-permute-start.3
  97.2 9.8 %inverse_columns.3 = (f32[8,48,768]{2,1,0:T(8,128)}, f32[24,768]{1,0:T(8,128)}, f32[24,768]{1,0:T(8,128)}) custom-call(f32[16,48,768]{2,1,0:T(8,128)} %all-to-all-done.1.refs_0_, f32[2,16,768]{2,1,0:T(8,128)} %constant.17.clone.refs_1_.refs_2_, f32[2,48,768]{2,1,0:T(8,128)} %constant.18.clone.refs_2_.refs_3_), custom_call_target="tpu_custom_call" | custom-call | flops 7000000000 | bytes 1048576 | tf_op jit(solution)/shard_map/inverse_columns/pallas_call | solution.py:314
  107.0 0.8 collective-permute-start.4
  107.8 1.0 collective-permute-start.5
  108.8 2.2 collective-permute-done.4.refs_7_
  111.9 20.4 %potential.3 = f32[16,48,768]{2,1,0:T(8,128)} custom-call(s32[3]{0:T(128)} %add_convert_fusion.refs_2_.refs_0_, f32[3,48,768]{2,1,0:T(8,128)} %copy-done, f32[8,48,768]{2,1,0:T(8,128)} %get-tuple-element.19.refs_2_, f32[8,48,768]{2,1,0:T(8,128)} %get-tuple-element.21.refs_3_, f32[3,48,768]{2,1,0:T(8,128)} %copy-done.1, f32[48,768]{1,0:T(8,128)} %copy-done.2, ...), custom_call_target="tpu_custom_call" | custom-call | flops 20000000000 | bytes 1048576 | tf_op jit(solution)/shard_map/potential/pallas_call | solution.py:560
  132.3 11.3 %all-to-all-start.3 = ((f32[16,48,768]{2,1,0:T(8,128)}), f32[16,48,768]{2,1,0:T(8,128)}, u32[]{:S(2)}, u32[]{:S(2)}) async-start(f32[16,48,768]{2,1,0:T(8,128)} %potential.3), calls=%async_computation.3 | async-start | bytes 4718592 | tf_op jit(solution)/shard_map/all_to_all | solution.py:638
  143.6 20.4 %potential.2 = f32[16,48,768]{2,1,0:T(8,128)} custom-call(s32[3]{0:T(128)} %add_convert_fusion.refs_2_.refs_0_, f32[3,48,768]{2,1,0:T(8,128)} %copy-done, f32[8,48,768]{2,1,0:T(8,128)} %get-tuple-element.19.refs_2_, f32[8,48,768]{2,1,0:T(8,128)} %get-tuple-element.21.refs_3_, f32[3,48,768]{2,1,0:T(8,128)} %copy-done.1, f32[48,768]{1,0:T(8,128)} %copy-done.2, ...), custom_call_target="tpu_custom_call" | custom-call | flops 20000000000 | bytes 1048576 | tf_op jit(solution)/shard_map/potential/pallas_call | solution.py:560
  164.1 12.0 %all-to-all-done.3.refs_1_ = f32[16,48,768]{2,1,0:T(8,128)} async-done(((f32[16,48,768]{2,1,0:T(8,128)}), f32[16,48,768]{2,1,0:T(8,128)}, u32[]{:S(2)}, u32[]{:S(2)}) %all-to-all-start.3) | async-done | bytes 2359328 | tf_op jit(solution)/shard_map/all_to_all | solution.py:638
  176.0 4.6 %all-to-all-start.2 = ((f32[16,48,768]{2,1,0:T(8,128)}), f32[16,48,768]{2,1,0:T(8,128)}, u32[]{:S(2)}, u32[]{:S(2)}) async-start(f32[16,48,768]{2,1,0:T(8,128)} %potential.2), calls=%async_computation.2 | async-start | bytes 4718592 | tf_op jit(solution)/shard_map/all_to_all | solution.py:638
  180.6 12.5 %forward_rows.2.refs_4_ = f32[2,16,48,768]{3,2,1,0:T(8,128)} custom-call(s32[3]{0:T(128)} %add_convert_fusion.refs_2_.refs_0_, f32[16,48,768]{2,1,0:T(8,128)} %all-to-all-done.3.refs_1_, f32[2,16,768]{2,1,0:T(8,128)} %constant.17.clone.refs_1_.refs_2_, f32[2,48,768]{2,1,0:T(8,128)} %constant.18.clone.refs_2_.refs_3_), custom_call_target="tpu_custom_call" | custom-call | flops 10000000000 | bytes 1048576 | tf_op jit(solution)/shard_map/forward_rows/pallas_call | solution.py:624
  193.1 19.0 %all-to-all-done.2.refs_1_ = f32[16,48,768]{2,1,0:T(8,128)} async-done(((f32[16,48,768]{2,1,0:T(8,128)}), f32[16,48,768]{2,1,0:T(8,128)}, u32[]{:S(2)}, u32[]{:S(2)}) %all-to-all-start.2) | async-done | bytes 2359328 | tf_op jit(solution)/shard_map/all_to_all | solution.py:638
  212.1 12.5 %forward_rows.3 = f32[2,16,48,768]{3,2,1,0:T(8,128)} custom-call(s32[3]{0:T(128)} %add_convert_fusion.refs_2_.refs_0_, f32[16,48,768]{2,1,0:T(8,128)} %all-to-all-done.2.refs_1_, f32[2,16,768]{2,1,0:T(8,128)} %constant.17.clone.refs_1_.refs_2_, f32[2,48,768]{2,1,0:T(8,128)} %constant.18.clone.refs_2_.refs_3_, ...), custom_call_target="tpu_custom_call", output_to_operand_aliasing={{}: (4, {})} | custom-call | flops 10000000000 | bytes 1048576 | tf_op jit(solution)/shard_map/forward_rows/pallas_call | solution.py:624
  (18 shorter events, 2.2 us)
Async XLA Ops:
  10.9 38.7 %all-to-all-start = ((f32[16,48,768]{2,1,0:T(8,128)}), f32[16,48,768]{2,1,0:T(8,128)}, u32[]{:S(2)}, u32[]{:S(2)}) async-start(f32[16,48,768]{2,1,0:T(8,128)} %get-tuple-element.17), calls=%async_computation | async-start | bytes 4718592 | tf_op jit(solution)/shard_map/all_to_all | solution.py:638
  49.6 47.6 %all-to-all-start.1 = ((f32[16,48,768]{2,1,0:T(8,128)}), f32[16,48,768]{2,1,0:T(8,128)}, u32[]{:S(2)}, u32[]{:S(2)}) async-start(f32[16,48,768]{2,1,0:T(8,128)} %inverse_rows.3), calls=%async_computation.1 | async-start | bytes 4718592 | tf_op jit(solution)/shard_map/all_to_all | solution.py:638
  64.2 22.3 %collective-permute-start = (f32[3,48,768]{2,1,0:T(8,128)}, f32[3,48,768]{2,1,0:T(8,128)S(1)}, u32[]{:S(2)}, u32[]{:S(2)}) collective-permute-start(f32[3,48,768]{2,1,0:T(8,128)} %get-tuple-element.18), channel_id=1, source_target_pairs={{0,16},{16,32},{32,48},{48,64},{64,80},{80,96},{96,112},{1,17},{17... | collective-permute-start | bytes 1327112 | tf_op jit(solution)/shard_map/ppermute | solution.py:330
  69.6 23.1 %collective-permute-start.1 = (f32[3,48,768]{2,1,0:T(8,128)}, f32[3,48,768]{2,1,0:T(8,128)S(1)}, u32[]{:S(2)}, u32[]{:S(2)}) collective-permute-start(f32[3,48,768]{2,1,0:T(8,128)} %get-tuple-element.22), channel_id=1, source_target_pairs={{16,0},{32,16},{48,32},{64,48},{80,64},{96,80},{112,96},{17,1},{33... | collective-permute-start | bytes 1327112 | tf_op jit(solution)/shard_map/ppermute | solution.py:330
  86.5 6.2 %copy-start = (f32[3,48,768]{2,1,0:T(8,128)}, f32[3,48,768]{2,1,0:T(8,128)S(1)}, u32[]{:S(2)}) copy-start(f32[3,48,768]{2,1,0:T(8,128)S(1)} %collective-permute-done.below_ref.refs_1_) | copy-start | bytes 1327108
  92.7 0.8 copy-start.1
  95.4 15.7 %collective-permute-start.2 = (f32[48,768]{1,0:T(8,128)}, f32[48,768]{1,0:T(8,128)S(1)}, u32[]{:S(2)}, u32[]{:S(2)}) collective-permute-start(f32[48,768]{1,0:T(8,128)} %get-tuple-element.25), channel_id=1, source_target_pairs={{0,1},{1,2},{2,3},{3,4},{4,5},{5,6},{6,7},{7,8},{8,9},{9,10},{10,1... | collective-permute-start | bytes 442376 | tf_op jit(solution)/shard_map/ppermute | solution.py:330
  95.4 15.7 %collective-permute-start.3 = (f32[48,768]{1,0:T(8,128)}, f32[48,768]{1,0:T(8,128)S(1)}, u32[]{:S(2)}, u32[]{:S(2)}) collective-permute-start(f32[48,768]{1,0:T(8,128)} %get-tuple-element.26), channel_id=1, source_target_pairs={{1,0},{2,1},{3,2},{4,3},{5,4},{6,5},{7,6},{8,7},{9,8},{10,9},{11,1... | collective-permute-start | bytes 442376 | tf_op jit(solution)/shard_map/ppermute | solution.py:330
  107.0 4.1 %collective-permute-start.4 = (f32[24,768]{1,0:T(8,128)}, f32[24,768]{1,0:T(8,128)S(1)}, u32[]{:S(2)}, u32[]{:S(2)}) collective-permute-start(f32[24,768]{1,0:T(8,128)} %get-tuple-element.27), channel_id=1, source_target_pairs={{0,1},{1,2},{2,3},{3,4},{4,5},{5,6},{6,7},{7,8},{8,9},{9,10},{10,1... | collective-permute-start | bytes 221192 | tf_op jit(solution)/shard_map/ppermute | solution.py:330
  107.8 3.3 %collective-permute-start.5 = (f32[24,768]{1,0:T(8,128)}, f32[24,768]{1,0:T(8,128)S(1)}, u32[]{:S(2)}, u32[]{:S(2)}) collective-permute-start(f32[24,768]{1,0:T(8,128)} %get-tuple-element.28), channel_id=1, source_target_pairs={{1,0},{2,1},{3,2},{4,3},{5,4},{6,5},{7,6},{8,7},{9,8},{10,9},{11,1... | collective-permute-start | bytes 221192 | tf_op jit(solution)/shard_map/ppermute | solution.py:330
  111.1 0.6 copy-start.4
  111.1 0.6 copy-start.5
  111.1 0.7 copy-start.2
  111.1 0.8 copy-start.3
  132.3 43.7 %all-to-all-start.3 = ((f32[16,48,768]{2,1,0:T(8,128)}), f32[16,48,768]{2,1,0:T(8,128)}, u32[]{:S(2)}, u32[]{:S(2)}) async-start(f32[16,48,768]{2,1,0:T(8,128)} %potential.3), calls=%async_computation.3 | async-start | bytes 4718592 | tf_op jit(solution)/shard_map/all_to_all | solution.py:638
  176.0 36.1 %all-to-all-start.2 = ((f32[16,48,768]{2,1,0:T(8,128)}), f32[16,48,768]{2,1,0:T(8,128)}, u32[]{:S(2)}, u32[]{:S(2)}) async-start(f32[16,48,768]{2,1,0:T(8,128)} %potential.2), calls=%async_computation.2 | async-start | bytes 4718592 | tf_op jit(solution)/shard_map/all_to_all | solution.py:638

commit v2 on v1

--- a/solution.py
+++ b/solution.py
@@ -22,6 +22,7 @@
 f32 = jnp.float32
 bf16 = jnp.bfloat16
 reach = 3
+gather_tile = 16
 lead = 9
 
 
@@ -107,6 +108,27 @@
 
     lax.fori_loop(0, coarse_ref.shape[1], step, 0)
 
+    tile = 16
+    width = tab_ref.shape[2]
+    quarter = width // 4
+    turn = lax.broadcasted_iota(jnp.int32, (tile, width), 1) % 4
+    turn_cos = jnp.where(turn == 0, 1.0, jnp.where(turn == 2, -1.0, 0.0)).astype(bf16)
+    turn_sin = jnp.where(turn == 1, 1.0, jnp.where(turn == 3, -1.0, 0.0)).astype(bf16)
+    flip = jnp.where(turn % 2 == 0, 1.0, -1.0).astype(bf16)
+
+    def spread(t, carry):
+        for part in range(2):
+            rows = [pl.ds(pl.multiple_of(q * quarter + t * tile, tile), tile) for q in range(4)]
+            cos, sin = tab_ref[part, rows[0]], tab_ref[2 + part, rows[0]]
+            next_cos = cos * turn_cos - sin * turn_sin
+            next_sin = sin * turn_cos + cos * turn_sin
+            tab_ref[part, rows[1]], tab_ref[2 + part, rows[1]] = next_cos, next_sin
+            tab_ref[part, rows[2]], tab_ref[2 + part, rows[2]] = cos * flip, sin * flip
+            tab_ref[part, rows[3]], tab_ref[2 + part, rows[3]] = next_cos * flip, next_sin * flip
+        return carry
+
+    lax.fori_loop(0, quarter // tile, spread, 0)
+
 
 def factor_scratch(factors):
     return [pltpu.VMEM(factor.shape, f32) for factor in factors] + [pltpu.SemaphoreType.DMA((2,))]
@@ -117,7 +139,7 @@
         angle = (np.outer(rows, np.arange(length)) % length) * (2.0 * math.pi / length)
         return np.stack([np.cos(angle), np.sin(angle)]).astype(np.float32) * np.float32(scale)
 
-    coarse = waves(np.arange(0, length, stride), 1.0)
+    coarse = waves(np.arange(0, length // 4, stride), 1.0)
     fine = waves(np.arange(stride), 1.0 / math.sqrt(length))
     return jnp.asarray(coarse), jnp.asarray(fine)
 
@@ -218,14 +240,33 @@
     )(rho_hat, tables, flags)
 
 
-def gather_blocks(in_ref, high_ref, low_ref):
+def tile_copies(hbm_ref, in_ref, sems, t):
+    group = in_ref.shape[0] // 4
+    at = pl.ds(t * gather_tile, gather_tile)
+    if not isinstance(t, int):
+        at = pl.ds(pl.multiple_of(t * gather_tile, gather_tile), gather_tile)
+    blocks = [pl.ds(g * group, group) for g in range(4)]
+    return [
+        pltpu.make_async_copy(hbm_ref.at[d, at], in_ref.at[d, at], sems.at[t, g])
+        for g, d in enumerate(blocks)
+    ]
+
+
+def fetch_blocks(hbm_ref, in_ref, sems):
+    for t in range(in_ref.shape[1] // gather_tile):
+        for copy in tile_copies(hbm_ref, in_ref, sems, t):
+            copy.start()
+
+
+def gather_blocks(hbm_ref, in_ref, sems, high_ref, low_ref):
     parts, rows, lanes = in_ref.shape
     width = high_ref.shape[2]
     local = width // parts
     planes = lanes // (2 * local)
-    tile = 16
+    tile = gather_tile
 
     def gather_rows(t, carry):
+        wait_all(tile_copies(hbm_ref, in_ref, sems, t))
         at = pl.ds(pl.multiple_of(t * tile, tile), tile)
         lane = lax.broadcasted_iota(jnp.int32, (tile, 128), 1)
         for piece in range(2 * planes):
@@ -255,24 +296,16 @@
     lax.fori_loop(0, rows // tile, gather_rows, 0)
 
 
-def fetch_blocks(hbm_ref, in_ref, sems):
-    parts = in_ref.shape[0]
-    return copy_all([(hbm_ref.at[pl.ds(d, 1)], in_ref.at[pl.ds(d, 1)]) for d in range(parts)], sems)
-
-
 def inverse_columns_body(sends, blocks_ref, coarse_hbm_ref, fine_hbm_ref, *refs):
     coarse_ref, fine_ref, factor_sems = refs[-3:]
     refs = refs[:-3]
     out_ref, head_ref, tail_ref = refs[:3]
     tab_ref, in_ref, stage_ref, high_ref, low_ref, in_sems, out_sems, send_sems = refs[-8:]
     planes, rows, width = stage_ref.shape
-    arriving = fetch_blocks(blocks_ref, in_ref, in_sems)
+    fetch_blocks(blocks_ref, in_ref, in_sems)
     fill_tables((coarse_hbm_ref, fine_hbm_ref), coarse_ref, fine_ref, tab_ref, factor_sems)
-    wait_all(arriving)
-    gather_blocks(in_ref, high_ref, low_ref)
-    field = triple(dot_nn, high_ref[0], low_ref[0], tab_ref[0], tab_ref[1])
-    field = field - triple(dot_nn, high_ref[1], low_ref[1], tab_ref[2], tab_ref[3])
-    stage_ref[...] = field.reshape(planes, rows, width)
+    gather_blocks(blocks_ref, in_ref, in_sems, high_ref, low_ref)
+    half = planes // 2
 
     def finish(z, carry):
         value = stage_ref[z]
@@ -281,7 +314,15 @@
         pltpu.make_async_copy(stage_ref.at[z], out_ref.at[z], out_sems.at[z]).start()
         return carry
 
-    lax.fori_loop(0, planes, finish, 0)
+    def step(m, carry):
+        at = pl.ds(pl.multiple_of(m * half * rows, half * rows), half * rows)
+        field = triple(dot_nn, high_ref[0, at], low_ref[0, at], tab_ref[0], tab_ref[1])
+        field = field - triple(dot_nn, high_ref[1, at], low_ref[1, at], tab_ref[2], tab_ref[3])
+        stage_ref[pl.ds(m * half, half)] = field.reshape(half, rows, width)
+        lax.fori_loop(m * half, (m + 1) * half, finish, 0)
+        return carry
+
+    lax.fori_loop(0, 2, step, 0)
     leaving = [
         pltpu.make_async_copy(stage_ref.at[z], out_ref.at[z], out_sems.at[z]) for z in range(planes)
     ]
@@ -307,7 +348,7 @@
         pltpu.VMEM((planes, rows, width), f32),
         pltpu.VMEM((2, planes * rows, width), bf16),
         pltpu.VMEM((2, planes * rows, width), bf16),
-        pltpu.SemaphoreType.DMA((parts,)),
+        pltpu.SemaphoreType.DMA((rows // gather_tile, 4)),
         pltpu.SemaphoreType.DMA((planes,)),
         pltpu.SemaphoreType.DMA((2, 1)),
     ]
@@ -330,29 +371,26 @@
     return lax.ppermute(value, axis, pairs if up else [(b, a) for a, b in pairs])
 
 
-def edges_body(below_ref, head_ref, tail_ref, above_ref, head_out, tail_out):
+def edges_body(below_ref, above_ref, head_out, tail_out):
     rows = below_ref.shape[1]
-    middle = head_ref.shape[0]
     for z in range(reach):
-        for ref, first in ((below_ref, 0), (above_ref, reach * reach + middle)):
+        for ref, first in ((below_ref, 0), (above_ref, reach * reach)):
             to = slice(first + reach * z, first + reach * (z + 1))
             head_out[to], tail_out[to] = ref[z, :reach], ref[z, rows - reach :]
-    to = slice(reach * reach, reach * reach + middle)
-    head_out[to], tail_out[to] = head_ref[...], tail_ref[...]
-
-
-def edges(below, head, tail, above):
-    width = head.shape[1]
-    count = -(-(head.shape[0] + 2 * reach * reach) // 8) * 8
+
+
+def edges(below, above):
+    width = below.shape[2]
+    count = -(-2 * reach * reach // 8) * 8
     return call(
         edges_body,
         [array(count, width)] * 2,
         1.0,
         grid=(1,),
-        in_specs=[whole(value.shape) for value in (below, head, tail, above)],
+        in_specs=[whole(below.shape)] * 2,
         out_specs=[whole((count, width))] * 2,
         name="edges",
-    )(below, head, tail, above)
+    )(below, above)
 
 
 def roll_x(value, by):
@@ -413,17 +451,20 @@
     return d_rho, two_d_sigma
 
 
-def potential_body(sources, bottom, top, flag_ref, *refs):
-    tab_hbm_ref, out_ref, tab_ref, tab_sems, pot_ref, tall_ref, stage_ref = refs[-21:-14]
-    in_sems, out_sems, side_sems = refs[-14:-11]
-    side_refs = refs[-11:-7]
+def potential_body(sources, groups, flag_ref, *refs):
     ext_ref, part_ref, smooth_ref, flat_ref, fx_ref, fy_ref, fz_ref = refs[-7:]
-    depth, rows, width = pot_ref.shape
-    total = depth + 2 * reach
-    sides = copy_all(list(zip(refs[4:8], side_refs)), side_sems)
+    count = max(source[2] for source in sources) + 2
+    plane_refs = refs[: -count - 17]
+    sides_hbm = plane_refs[-count:]
+    tab_hbm_ref, out_ref, tab_ref, tab_sems, pot_ref, tall_ref, stage_ref = refs[-count - 17 : -count - 10]
+    in_sems, out_sems, side_sems = refs[-count - 10 : -count - 7]
+    side_refs = refs[-count - 7 : -7]
+    planes, rows, width = pot_ref.shape
+    each = planes // groups
+    sides = copy_all(list(zip(sides_hbm, side_refs)), side_sems)
     arriving = copy_all(
         [
-            (refs[plane].at[pl.ds(at, 1)], ext_ref.at[pl.ds(z, 1), pl.ds(lead - 1, rows)])
+            (plane_refs[plane].at[pl.ds(at, 1)], ext_ref.at[pl.ds(z, 1), pl.ds(lead - 1, rows)])
             for z, (plane, at, _, _) in enumerate(sources)
         ],
         in_sems,
@@ -431,30 +472,34 @@
     slope = 1.0 / (2.0 * grid_step)
     tiles = rows // 8 + 1
 
-    def at_end(is_end, flag):
-        return pl.when(flag_ref[flag] == 1) if is_end else lambda body: None
+    def at_end(flag):
+        return pl.when(flag_ref[flag] == 1) if groups == 2 else lambda body: None
 
     wait_all(sides)
     for z, (_, _, side, row) in enumerate(sources):
         at = slice(row, row + reach)
-        ext_ref[z, lead - 1 - reach : lead - 1] = side_refs[side - 4][at]
-        ext_ref[z, lead - 1 + rows : lead - 1 + rows + reach] = side_refs[side - 3][at]
+        ext_ref[z, lead - 1 - reach : lead - 1] = side_refs[side][at]
+        ext_ref[z, lead - 1 + rows : lead - 1 + rows + reach] = side_refs[side + 1][at]
     wait_all(arriving)
     tables = load_tables(tab_hbm_ref, tab_ref, tab_sems)
 
-    @at_end(bottom, 0)
+    def widened(z, size, margin):
+        return z + margin * (z // size) if groups > 1 else z
+
+    @at_end(0)
     def _():
         ext_ref[reach - 1] = ext_ref[reach]
 
-    @at_end(top, 1)
+    @at_end(1)
     def _():
-        ext_ref[depth + reach] = ext_ref[depth + reach - 1]
+        ext_ref[ext_ref.shape[0] - reach] = ext_ref[ext_ref.shape[0] - reach - 1]
 
     def filter_depth(z, carry):
-        part_ref[z] = 0.25 * (ext_ref[z] + ext_ref[z + 2]) + 0.5 * ext_ref[z + 1]
-        return carry
-
-    lax.fori_loop(0, total - 2, filter_depth, 0)
+        w = widened(z, each + 4, 2)
+        part_ref[z] = 0.25 * (ext_ref[w] + ext_ref[w + 2]) + 0.5 * ext_ref[w + 1]
+        return carry
+
+    lax.fori_loop(0, part_ref.shape[0], filter_depth, 0)
 
     def filter_plane(z, carry):
         for t in range(tiles):
@@ -467,23 +512,24 @@
             )
         return carry
 
-    lax.fori_loop(0, total - 2, filter_plane, 0)
-
-    @at_end(bottom, 0)
+    lax.fori_loop(0, part_ref.shape[0], filter_plane, 0)
+
+    @at_end(0)
     def _():
         smooth_ref[1] = smooth_ref[2]
 
-    @at_end(top, 1)
+    @at_end(1)
     def _():
-        smooth_ref[depth + 2] = smooth_ref[depth + 1]
+        smooth_ref[smooth_ref.shape[0] - 2] = smooth_ref[smooth_ref.shape[0] - 3]
 
     def local_terms(z, carry):
+        w = widened(z, each + 2, 2)
         for t in range(tiles):
             r = lead - 1 + 8 * t
-            center = smooth_ref[z + 1, r : r + 8]
+            center = smooth_ref[w + 1, r : r + 8]
             gx = (roll_x(center, -1) - roll_x(center, 1)) * slope
-            gy = (smooth_ref[z + 1, r + 1 : r + 9] - smooth_ref[z + 1, r - 1 : r + 7]) * slope
-            gz = (smooth_ref[z + 2, r : r + 8] - smooth_ref[z, r : r + 8]) * slope
+            gy = (smooth_ref[w + 1, r + 1 : r + 9] - smooth_ref[w + 1, r - 1 : r + 7]) * slope
+            gz = (smooth_ref[w + 2, r : r + 8] - smooth_ref[w, r : r + 8]) * slope
             d_rho, two_d_sigma = energy_slopes(center, gx * gx + gy * gy + gz * gz)
             flat_ref[z, r : r + 8] = d_rho
             fx_ref[z, r : r + 8] = two_d_sigma * gx
@@ -491,28 +537,29 @@
             fz_ref[z, r : r + 8] = two_d_sigma * gz
         return carry
 
-    lax.fori_loop(0, depth + 2, local_terms, 0)
-
-    @at_end(bottom, 0)
+    lax.fori_loop(0, flat_ref.shape[0], local_terms, 0)
+
+    @at_end(0)
     def _():
         fz_ref[0] = fz_ref[1]
 
-    @at_end(top, 1)
+    @at_end(1)
     def _():
-        fz_ref[depth + 1] = fz_ref[depth]
+        fz_ref[fz_ref.shape[0] - 1] = fz_ref[fz_ref.shape[0] - 2]
 
     def collect(z, carry):
+        w = widened(z, each, 2)
         for t in range(rows // 8):
             r = lead + 8 * t
             here = slice(r, r + 8)
-            fx = fx_ref[z + 1, here]
+            fx = fx_ref[w + 1, here]
             along_x = (roll_x(fx, -1) - roll_x(fx, 1)) * slope
-            along_y = (fy_ref[z + 1, r + 1 : r + 9] - fy_ref[z + 1, r - 1 : r + 7]) * slope
-            along_z = (fz_ref[z + 2, here] - fz_ref[z, here]) * slope
-            pot_ref[z, 8 * t : 8 * t + 8] = flat_ref[z + 1, here] - (along_x + along_y + along_z)
-        return carry
-
-    lax.fori_loop(0, depth, collect, 0)
+            along_y = (fy_ref[w + 1, r + 1 : r + 9] - fy_ref[w + 1, r - 1 : r + 7]) * slope
+            along_z = (fz_ref[w + 2, here] - fz_ref[w, here]) * slope
+            pot_ref[z, 8 * t : 8 * t + 8] = flat_ref[w + 1, here] - (along_x + along_y + along_z)
+        return carry
+
+    lax.fori_loop(0, planes, collect, 0)
     wait_all(tables)
     forward_columns(pot_ref, tab_ref, tall_ref, stage_ref, out_ref, out_sems)
 
@@ -540,55 +587,60 @@
         wait_all(group_copies(stage_ref, out_ref, out_sems, m, group))
 
 
-def potential_of(flags, arrays, sources, start, count, depth, tables, parts):
-    rows, width = arrays[0].shape[1:]
+def potential_of(flags, planes, sides, sources, groups, tables, parts):
+    rows, width = planes[0].shape[1:]
     tall = -(-(rows + lead + 8) // 8) * 8
-    planes = lambda extra: pltpu.VMEM((count + extra, tall, width), f32)
-    used = sources[start : start + count + 2 * reach]
+    count = len(sources) - 2 * reach * groups
     lanes = count * rows
     out = (parts, width // parts, 2 * lanes)
     scratch = table_scratch(width) + [
         pltpu.VMEM((count, rows, width), f32),
         pltpu.VMEM((3 * width, lanes), bf16),
         pltpu.VMEM(out, f32),
-        pltpu.SemaphoreType.DMA((len(used),)),
+        pltpu.SemaphoreType.DMA((len(sources),)),
         pltpu.SemaphoreType.DMA((2, parts // 2)),
-        pltpu.SemaphoreType.DMA((4,)),
+        pltpu.SemaphoreType.DMA((len(sides),)),
     ]
-    body = lambda *refs: potential_body(used, start == 0, start + count == depth, *refs)
-    sides = [pltpu.VMEM(side.shape, f32) for side in arrays[4:]]
+    scratch += [pltpu.VMEM(side.shape, f32) for side in sides]
+    for margin in (6, 4, 4, 2, 2, 2, 2):
+        scratch.append(pltpu.VMEM((count + margin * groups, tall, width), f32))
     return call(
-        body,
+        lambda *refs: potential_body(sources, groups, *refs),
         array(*out),
         20.0,
         grid=(1,),
-        in_specs=[pl.BlockSpec(memory_space=pltpu.SMEM)] + [in_hbm] * 9,
+        in_specs=[pl.BlockSpec(memory_space=pltpu.SMEM)]
+        + [in_hbm] * (len(planes) + len(sides) + 1),
         out_specs=in_hbm,
-        scratch_shapes=scratch + sides + [planes(extra) for extra in (6, 4, 4, 2, 2, 2, 2)],
+        scratch_shapes=scratch,
         name="potential",
-    )(flags, *arrays, tables)
-
-
-def forward_rows_body(first, flag_ref, blocks_ref, coarse_hbm_ref, fine_hbm_ref, *refs):
+    )(flags, *planes, *sides, tables)
+
+
+def forward_rows_body(starts, flag_ref, blocks_ref, coarse_hbm_ref, fine_hbm_ref, *refs):
     coarse_ref, fine_ref, factor_sems = refs[-3:]
     out_ref, tab_ref, in_ref, stage_ref, high_ref, low_ref, in_sems, out_sems = refs[-11:-3]
     _, planes, rows, width = stage_ref.shape
-    arriving = fetch_blocks(blocks_ref, in_ref, in_sems)
+    fetch_blocks(blocks_ref, in_ref, in_sems)
     fill_tables((coarse_hbm_ref, fine_hbm_ref), coarse_ref, fine_ref, tab_ref, factor_sems)
-    wait_all(arriving)
-    gather_blocks(in_ref, high_ref, low_ref)
+    gather_blocks(blocks_ref, in_ref, in_sems, high_ref, low_ref)
     high_ref[2], low_ref[2] = -high_ref[0], -low_ref[0]
 
-    def copies(c):
+    half = planes // 2
+
+    def copies(c, m):
+        to = starts[0] + m * (starts[1] - starts[0])
         return [
-            pltpu.make_async_copy(stage_ref.at[c, z], out_ref.at[c, first + z], out_sems.at[c, z])
-            for z in range(planes)
+            pltpu.make_async_copy(stage_ref.at[c, z], out_ref.at[c, to + y], out_sems.at[c, z])
+            for y, z in enumerate([m * half + y for y in range(half)])
         ]
 
-    def step(c, carry):
-        value = triple(dot_nn, high_ref[c], low_ref[c], tab_ref[0], tab_ref[1])
-        value = value + triple(dot_nn, high_ref[c + 1], low_ref[c + 1], tab_ref[2], tab_ref[3])
-        stage_ref[c] = value.reshape(planes, rows, width)
+    def step(i, carry):
+        c, m = i // 2, i % 2
+        at = pl.ds(pl.multiple_of(m * half * rows, half * rows), half * rows)
+        value = triple(dot_nn, high_ref[c, at], low_ref[c, at], tab_ref[0], tab_ref[1])
+        value = value + triple(dot_nn, high_ref[c + 1, at], low_ref[c + 1, at], tab_ref[2], tab_ref[3])
+        stage_ref[c, pl.ds(m * half, half)] = value.reshape(half, rows, width)
 
         @pl.when(flag_ref[2] == 1)
         def _():
@@ -596,18 +648,20 @@
             at_zero = (lax.broadcasted_iota(jnp.int32, tile, 0) == 0) & (
                 lax.broadcasted_iota(jnp.int32, tile, 1) == 0
             )
-            for z in range(planes):
+            for y in range(half):
+                z = m * half + y
                 stage_ref[c, z, :8, :128] = jnp.where(at_zero, 0.0, stage_ref[c, z, :8, :128])
 
-        for copy in copies(c):
+        for copy in copies(c, m):
             copy.start()
         return carry
 
-    lax.fori_loop(0, 2, step, 0)
-    wait_all(copies(0) + copies(1))
-
-
-def forward_rows(flags, blocks, factors, first, depth, before):
+    lax.fori_loop(0, 4, step, 0)
+    for c in range(2):
+        wait_all(copies(c, 0) + copies(c, 1))
+
+
+def forward_rows(flags, blocks, factors, starts, depth, before):
     parts, rows, lanes = blocks.shape
     width = factors[0].shape[2]
     planes = lanes * parts // (2 * width)
@@ -618,11 +672,11 @@
         pltpu.VMEM((2, planes, rows, width), f32),
         pltpu.VMEM((3, planes * rows, width), bf16),
         pltpu.VMEM((3, planes * rows, width), bf16),
-        pltpu.SemaphoreType.DMA((parts,)),
+        pltpu.SemaphoreType.DMA((rows // gather_tile, 4)),
         pltpu.SemaphoreType.DMA((2, planes)),
     ]
     return call(
-        lambda *refs: forward_rows_body(first, *refs),
+        lambda *refs: forward_rows_body(starts, *refs),
         array(2, depth, rows, width),
         10.0,
         grid=(1,),
@@ -652,34 +706,37 @@
     outer = exchange(outer)
     inner = exchange(inverse_rows(rho_hat, factors, tables, flags, (1, 2)))
     outer, head, tail, low_planes, high_planes = inverse_columns(outer, factors, True)
+    outer_sides = shift(tail, "py", True, True), shift(head, "py", False, True)
+    inner, head, tail = inverse_columns(inner, factors, False)
+    inner_sides = shift(tail, "py", True, True), shift(head, "py", False, True)
+
+    low_planes, high_planes, _ = lax.optimization_barrier((low_planes, high_planes, head))
     below = shift(high_planes, "px", True, False)
     above = shift(low_planes, "px", False, False)
-    head, tail = edges(below, head, tail, above)
-    head, tail = shift(tail, "py", True, True), shift(head, "py", False, True)
-    inner, inner_head, inner_tail = inverse_columns(inner, factors, False)
-    inner_head, inner_tail = shift(inner_tail, "py", True, True), shift(inner_head, "py", False, True)
-
-    arrays = [below, outer, inner, above, head, tail, inner_head, inner_tail]
-    sources = []
-    for z in range(-reach, depth + reach):
-        if z < 0:
-            sources.append((0, z + reach, 4, reach * (z + reach)))
-        elif z < unit:
-            sources.append((1, z, 4, reach * (z + reach)))
-        elif z < depth - unit:
-            sources.append((2, z - unit, 6, reach * (z - unit)))
-        elif z < depth:
-            at = z - depth + 2 * unit
-            sources.append((1, at, 4, reach * (at + reach)))
-        else:
-            at = z - depth
-            sources.append((3, at, 4, reach * (at + reach + 2 * unit)))
-
-    result = None
-    for first, count in ((0, 2), (2, 2)):
-        planes = (first * unit, count * unit)
-        spectral = potential_of(flags, arrays, sources, *planes, depth, tables, parts)
-        result = forward_rows(flags, exchange(spectral), factors, planes[0], depth, result)
+
+    def source(z):
+        if unit <= z < depth - unit:
+            return 1, z - unit, 2, reach * (z - unit)
+        if 0 <= z < depth:
+            at = z if z < unit else z - depth + 2 * unit
+            return 0, at, 0, reach * at
+        at = z + reach if z < 0 else z - depth
+        return (2 if z < 0 else 3), at, 4, reach * (at + (0 if z < 0 else reach))
+
+    inside = [source(z) for z in range(unit - reach, depth - unit + reach)]
+    outside = [source(z) for z in range(-reach, unit + reach)]
+    outside += [source(z) for z in range(depth - unit - reach, depth + reach)]
+    planes, sides = [outer, inner], [*outer_sides, *inner_sides]
+    spectral = potential_of(flags, planes, sides, inside, 1, tables, parts)
+    inner_waves = exchange(spectral)
+
+    head, tail = edges(below, above)
+    planes += [below, above]
+    sides += [shift(tail, "py", True, True), shift(head, "py", False, True)]
+    spectral = potential_of(flags, planes, sides, outside, 2, tables, parts)
+    outer_waves = exchange(spectral)
+    result = forward_rows(flags, inner_waves, factors, (unit, 2 * unit), depth, None)
+    result = forward_rows(flags, outer_waves, factors, (0, depth - unit), depth, result)
     return result
 
 

time: 225 us -> 240 us (1.067)
  waiting for transfers between devices: 75.4 us -> 89.2 us
  starting transfers between devices: 37.4 us -> 33.7 us
    all_to_all x4, waiting for transfers between devices: 52 us -> 61.3 us  [exchange(): return lax.all_to_all(value, 'py', 0, 0, tiled=True)]
    all_to_all x4, starting transfers between devices: 26.5 us -> 20.9 us  [exchange(): return lax.all_to_all(value, 'py', 0, 0, tiled=True)]
    ppermute x6 -> x8, waiting for transfers between devices: 23.5 us -> 27.9 us  [shift(): lax.ppermute(value, axis, pairs if up else [(b, a) for a, b in pairs])]
    pallas_call x4, Pallas kernels: 65.9 us -> 68.3 us  [the longest x2 44 us: potential_of(): call(lambda *refs: potential_body(sources, groups, *refs), array(*out), 2...]
    ppermute x6 -> x8, starting transfers between devices: 10.9 us -> 12.8 us  [shift(): lax.ppermute(value, axis, pairs if up else [(b, a) for a, b in pairs])]
  transfers between devices with their start and end apart: 10 -> 12, of which waited for: 7 -> 4; matrix products, arithmetic and copies ran while one was open for 0% -> 0% of each run, Pallas kernels for 29% -> 37%
where the time goes in v2:
time: 240 us; the launch traced here: 238 us
  Pallas kernels  111 us (46%)
  waiting for transfers between devices  89.2 us (37%)
  starting transfers between devices  33.7 us (14%)
  local copies, waits for them, and re-layouts  3.4 us (1%)
    all_to_all x4, waiting for transfers between devices, exchange(): return lax.all_to_all(value, 'py', 0, 0, tiled=True)  61.3 us
    pallas_call x2, Pallas kernels, potential_of(): call(lambda *refs: potential_body(sources, groups, *refs), array(*out), 2...  44 us
    ppermute x8, waiting for transfers between devices, shift(): lax.ppermute(value, axis, pairs if up else [(b, a) for a, b in pairs])  27.9 us
    pallas_call x2, Pallas kernels, forward_rows(): call(lambda *refs: forward_rows_body(starts, *refs), array(2, depth, rows...  24.3 us
    all_to_all x4, starting transfers between devices, exchange(): return lax.all_to_all(value, 'py', 0, 0, tiled=True)  20.9 us
    pallas_call x2, Pallas kernels, inverse_columns(): call(lambda *refs: inverse_columns_body(sends, *refs), [array(planes, row...  19.3 us
    ppermute x8, starting transfers between devices, shift(): lax.ppermute(value, axis, pairs if up else [(b, a) for a, b in pairs])  12.8 us
    pallas_call x1, Pallas kernels, inverse_rows(): call(body, array(*out), 10.0, grid=(1,), in_specs=[in_hbm] * 2 + [pl.Bloc...  10.9 us
  transfers between devices with their start and end apart: 12, of which 4 were waited for; matrix products, arithmetic and copies ran while one was open for 0% of the time, Pallas kernels for 37%

profile of v2, /device:TPU:14, one launch (start us, length us, event | category | flops | bytes accessed | tf_op | source)
XLA Modules:
  0.0 238.0 jit_solution(8165476786742318292)
XLA Ops:
  0.0 10.4 %inverse_rows.2 = (f32[16,48,768]{2,1,0:T(8,128)}, bf16[4,768,768]{2,1,0:T(8,128)(2,1)}) custom-call(f32[2,16,48,768]{3,2,1,0:T(8,128)} %refs_0_.3, f32[2,4,768]{2,1,0:T(4,128)} %constant.17.clone.refs_1_.refs_2_, f32[2,48,768]{2,1,0:T(8,128)} %constant.18.clone.refs_2_.refs_3_), custom_call_target="tpu_custom_call" | custom-call | flops 10000000000 | bytes 1048576 | tf_op jit(solution)/shard_map/inverse_rows/pallas_call | solution.py:221
  10.4 6.3 %all-to-all-start = ((f32[16,48,768]{2,1,0:T(8,128)}), f32[16,48,768]{2,1,0:T(8,128)}, u32[]{:S(2)}, u32[]{:S(2)}) async-start(f32[16,48,768]{2,1,0:T(8,128)} %get-tuple-element.19), calls=%async_computation | async-start | bytes 4718592 | tf_op jit(solution)/shard_map/all_to_all | solution.py:692
  17.3 10.9 %inverse_rows.3 = f32[16,48,768]{2,1,0:T(8,128)} custom-call(f32[2,16,48,768]{3,2,1,0:T(8,128)} %refs_0_.3, bf16[4,768,768]{2,1,0:T(8,128)(2,1)} %get-tuple-element.21.refs_1_.refs_11_.refs_7_, s32[3]{0:T(128)} %add_convert_fusion.refs_2_.refs_0_), custom_call_target="tpu_custom_call" | custom-call | flops 10000000000 | bytes 1048576 | tf_op jit(solution)/shard_map/inverse_rows/pallas_call | solution.py:231
  28.2 20.9 %all-to-all-done.refs_0_ = f32[16,48,768]{2,1,0:T(8,128)} async-done(((f32[16,48,768]{2,1,0:T(8,128)}), f32[16,48,768]{2,1,0:T(8,128)}, u32[]{:S(2)}, u32[]{:S(2)}) %all-to-all-start) | async-done | bytes 2359328 | tf_op jit(solution)/shard_map/all_to_all | solution.py:692
  49.1 4.3 %all-to-all-start.1 = ((f32[16,48,768]{2,1,0:T(8,128)}), f32[16,48,768]{2,1,0:T(8,128)}, u32[]{:S(2)}, u32[]{:S(2)}) async-start(f32[16,48,768]{2,1,0:T(8,128)} %inverse_rows.3), calls=%async_computation.1 | async-start | bytes 4718592 | tf_op jit(solution)/shard_map/all_to_all | solution.py:692
  53.5 9.8 %inverse_columns.2 = (f32[8,48,768]{2,1,0:T(8,128)}, f32[24,768]{1,0:T(8,128)}, f32[24,768]{1,0:T(8,128)}, f32[3,48,768]{2,1,0:T(8,128)}, f32[3,48,768]{2,1,0:T(8,128)}) custom-call(f32[16,48,768]{2,1,0:T(8,128)} %all-to-all-done.refs_0_, f32[2,4,768]{2,1,0:T(4,128)} %constant.17.clone.refs_1_.refs_2_, f32[2,48,768]{2,1,0:T(8,128)} %constant.18.clone.refs_2_.refs_3_), custom_call_target="tpu_custom_call" | custom-call | flops 7000000000 | bytes 1048576 | tf_op jit(solution)/shard_map/inverse_columns/pallas_call | solution.py:355
  63.4 1.7 collective-permute-start.3
  65.1 20.5 %all-to-all-done.1.refs_0_ = f32[16,48,768]{2,1,0:T(8,128)} async-done(((f32[16,48,768]{2,1,0:T(8,128)}), f32[16,48,768]{2,1,0:T(8,128)}, u32[]{:S(2)}, u32[]{:S(2)}) %all-to-all-start.1) | async-done | bytes 2359328 | tf_op jit(solution)/shard_map/all_to_all | solution.py:692
  85.6 9.5 %inverse_columns.3 = (f32[8,48,768]{2,1,0:T(8,128)}, f32[24,768]{1,0:T(8,128)}, f32[24,768]{1,0:T(8,128)}) custom-call(f32[16,48,768]{2,1,0:T(8,128)} %all-to-all-done.1.refs_0_, f32[2,4,768]{2,1,0:T(4,128)} %constant.17.clone.refs_1_.refs_2_, f32[2,48,768]{2,1,0:T(8,128)} %constant.18.clone.refs_2_.refs_3_), custom_call_target="tpu_custom_call" | custom-call | flops 7000000000 | bytes 1048576 | tf_op jit(solution)/shard_map/inverse_columns/pallas_call | solution.py:355
  95.1 1.7 collective-permute-start.5
  96.9 5.4 %collective-permute-start = (f32[3,48,768]{2,1,0:T(8,128)S(1)}, f32[3,48,768]{2,1,0:T(8,128)S(1)}, u32[]{:S(2)}, u32[]{:S(2)}) collective-permute-start(f32[3,48,768]{2,1,0:T(8,128)S(1)} %copy-done.2), channel_id=1, source_target_pairs={{0,16},{16,32},{32,48},{48,64},{64,80},{80,96},{96,112},{1,17},{17... | collective-permute-start | bytes 1327112 | tf_op jit(solution)/shard_map/ppermute | solution.py:371
  102.3 2.1 collective-permute-start.1
  105.1 20.4 %potential.3 = f32[16,48,768]{2,1,0:T(8,128)} custom-call(s32[3]{0:T(128)} %add_convert_fusion.refs_2_.refs_0_, f32[8,48,768]{2,1,0:T(8,128)} %get-tuple-element.20.refs_1_, f32[8,48,768]{2,1,0:T(8,128)} %get-tuple-element.22.refs_2_, f32[24,768]{1,0:T(8,128)} %copy-done.4, f32[24,768]{1,0:T(8,128)} %copy-done.5, f32[24,768]{1,0:T(8,128)} %copy-done.6, ...), custom_call_target="tpu_custom_call" | custom-call | flops 20000000000 | bytes 1048576 | tf_op jit(solution)/shard_map/potential/pallas_call | solution.py:607
  125.5 5.9 %all-to-all-start.3 = ((f32[16,48,768]{2,1,0:T(8,128)}), f32[16,48,768]{2,1,0:T(8,128)}, u32[]{:S(2)}, u32[]{:S(2)}) async-start(f32[16,48,768]{2,1,0:T(8,128)} %potential.3), calls=%async_computation.3 | async-start | bytes 4718592 | tf_op jit(solution)/shard_map/all_to_all | solution.py:692
  131.3 0.7 copy-done.1
  132.1 0.8 copy-done.3
  132.9 1.9 edges.1
  134.9 1.6 collective-permute-start.7
  136.5 27.9 %collective-permute-done.6.refs_9_ = f32[24,768]{1,0:T(8,128)S(1)} collective-permute-done((f32[24,768]{1,0:T(8,128)}, f32[24,768]{1,0:T(8,128)S(1)}, u32[]{:S(2)}, u32[]{:S(2)}) %collective-permute-start.6) | collective-permute-done | bytes 73760 | tf_op jit(solution)/shard_map/ppermute | solution.py:371
  165.6 23.7 %potential.2 = f32[16,48,768]{2,1,0:T(8,128)} custom-call(s32[3]{0:T(128)} %add_convert_fusion.refs_2_.refs_0_, f32[8,48,768]{2,1,0:T(8,128)} %get-tuple-element.20.refs_1_, f32[8,48,768]{2,1,0:T(8,128)} %get-tuple-element.22.refs_2_, f32[3,48,768]{2,1,0:T(8,128)} %copy-done.1, f32[3,48,768]{2,1,0:T(8,128)} %copy-done.3, f32[24,768]{1,0:T(8,128)} %copy-done.4, ...), custom_call_target="tpu_custom_call" | custom-call | flops 20000000000 | bytes 1048576 | tf_op jit(solution)/shard_map/potential/pallas_call | solution.py:607
  189.3 4.4 %all-to-all-start.2 = ((f32[16,48,768]{2,1,0:T(8,128)}), f32[16,48,768]{2,1,0:T(8,128)}, u32[]{:S(2)}, u32[]{:S(2)}) async-start(f32[16,48,768]{2,1,0:T(8,128)} %potential.2), calls=%async_computation.2 | async-start | bytes 4718592 | tf_op jit(solution)/shard_map/all_to_all | solution.py:692
  193.7 12.1 %forward_rows.2.refs_4_ = f32[2,16,48,768]{3,2,1,0:T(8,128)} custom-call(s32[3]{0:T(128)} %add_convert_fusion.refs_2_.refs_0_, f32[16,48,768]{2,1,0:T(8,128)} %all-to-all-done.3.refs_1_, f32[2,4,768]{2,1,0:T(4,128)} %constant.17.clone.refs_1_.refs_2_, f32[2,48,768]{2,1,0:T(8,128)} %constant.18.clone.refs_2_.refs_3_), custom_call_target="tpu_custom_call" | custom-call | flops 10000000000 | bytes 1048576 | tf_op jit(solution)/shard_map/forward_rows/pallas_call | solution.py:678
  205.8 19.9 %all-to-all-done.2.refs_1_ = f32[16,48,768]{2,1,0:T(8,128)} async-done(((f32[16,48,768]{2,1,0:T(8,128)}), f32[16,48,768]{2,1,0:T(8,128)}, u32[]{:S(2)}, u32[]{:S(2)}) %all-to-all-start.2) | async-done | bytes 2359328 | tf_op jit(solution)/shard_map/all_to_all | solution.py:692
  225.7 12.1 %forward_rows.3 = f32[2,16,48,768]{3,2,1,0:T(8,128)} custom-call(s32[3]{0:T(128)} %add_convert_fusion.refs_2_.refs_0_, f32[16,48,768]{2,1,0:T(8,128)} %all-to-all-done.2.refs_1_, f32[2,4,768]{2,1,0:T(4,128)} %constant.17.clone.refs_1_.refs_2_, f32[2,48,768]{2,1,0:T(8,128)} %constant.18.clone.refs_2_.refs_3_, ...), custom_call_target="tpu_custom_call", output_to_operand_aliasing={{}: (4, {})} | custom-call | flops 10000000000 | bytes 1048576 | tf_op jit(solution)/shard_map/forward_rows/pallas_call | solution.py:678
  (28 shorter events, 2.8 us)
Async XLA Ops:
  10.4 38.7 %all-to-all-start = ((f32[16,48,768]{2,1,0:T(8,128)}), f32[16,48,768]{2,1,0:T(8,128)}, u32[]{:S(2)}, u32[]{:S(2)}) async-start(f32[16,48,768]{2,1,0:T(8,128)} %get-tuple-element.19), calls=%async_computation | async-start | bytes 4718592 | tf_op jit(solution)/shard_map/all_to_all | solution.py:692
  49.1 36.5 %all-to-all-start.1 = ((f32[16,48,768]{2,1,0:T(8,128)}), f32[16,48,768]{2,1,0:T(8,128)}, u32[]{:S(2)}, u32[]{:S(2)}) async-start(f32[16,48,768]{2,1,0:T(8,128)} %inverse_rows.3), calls=%async_computation.1 | async-start | bytes 4718592 | tf_op jit(solution)/shard_map/all_to_all | solution.py:692
  63.3 39.0 %collective-permute-start.2 = (f32[24,768]{1,0:T(8,128)}, f32[24,768]{1,0:T(8,128)S(1)}, u32[]{:S(2)}, u32[]{:S(2)}) collective-permute-start(f32[24,768]{1,0:T(8,128)} %get-tuple-element.28), channel_id=1, source_target_pairs={{0,1},{1,2},{2,3},{3,4},{4,5},{5,6},{6,7},{7,8},{8,9},{9,10},{10,1... | collective-permute-start | bytes 221192 | tf_op jit(solution)/shard_map/ppermute | solution.py:371
  63.4 33.5 %copy-start.2 = (f32[3,48,768]{2,1,0:T(8,128)S(1)}, f32[3,48,768]{2,1,0:T(8,128)}, u32[]{:S(2)}) copy-start(f32[3,48,768]{2,1,0:T(8,128)} %get-tuple-element.26) | copy-start | bytes 1327108
  63.4 38.9 %copy-start = (f32[3,48,768]{2,1,0:T(8,128)S(1)}, f32[3,48,768]{2,1,0:T(8,128)}, u32[]{:S(2)}) copy-start(f32[3,48,768]{2,1,0:T(8,128)} %get-tuple-element.27) | copy-start | bytes 1327108
  63.4 41.0 %collective-permute-start.3 = (f32[24,768]{1,0:T(8,128)}, f32[24,768]{1,0:T(8,128)S(1)}, u32[]{:S(2)}, u32[]{:S(2)}) collective-permute-start(f32[24,768]{1,0:T(8,128)} %get-tuple-element.29), channel_id=1, source_target_pairs={{1,0},{2,1},{3,2},{4,3},{5,4},{6,5},{7,6},{8,7},{9,8},{10,9},{11,1... | collective-permute-start | bytes 221192 | tf_op jit(solution)/shard_map/ppermute | solution.py:371
  95.0 9.4 %collective-permute-start.4 = (f32[24,768]{1,0:T(8,128)}, f32[24,768]{1,0:T(8,128)S(1)}, u32[]{:S(2)}, u32[]{:S(2)}) collective-permute-start(f32[24,768]{1,0:T(8,128)} %get-tuple-element.30), channel_id=1, source_target_pairs={{0,1},{1,2},{2,3},{3,4},{4,5},{5,6},{6,7},{7,8},{8,9},{9,10},{10,1... | collective-permute-start | bytes 221192 | tf_op jit(solution)/shard_map/ppermute | solution.py:371
  95.1 9.3 %collective-permute-start.5 = (f32[24,768]{1,0:T(8,128)}, f32[24,768]{1,0:T(8,128)}, u32[]{:S(2)}, u32[]{:S(2)}) collective-permute-start(f32[24,768]{1,0:T(8,128)} %get-tuple-element.25), channel_id=1, source_target_pairs={{1,0},{2,1},{3,2},{4,3},{5,4},{6,5},{7,6},{8,7},{9,8},{10,9},{11,1... | collective-permute-start | bytes 221192 | tf_op jit(solution)/shard_map/ppermute | solution.py:371
  96.9 34.5 %collective-permute-start = (f32[3,48,768]{2,1,0:T(8,128)S(1)}, f32[3,48,768]{2,1,0:T(8,128)S(1)}, u32[]{:S(2)}, u32[]{:S(2)}) collective-permute-start(f32[3,48,768]{2,1,0:T(8,128)S(1)} %copy-done.2), channel_id=1, source_target_pairs={{0,16},{16,32},{32,48},{48,64},{64,80},{80,96},{96,112},{1,17},{17... | collective-permute-start | bytes 1327112 | tf_op jit(solution)/shard_map/ppermute | solution.py:371
  102.3 2.2 copy-start.4
  102.3 29.0 %collective-permute-start.1 = (f32[3,48,768]{2,1,0:T(8,128)S(1)}, f32[3,48,768]{2,1,0:T(8,128)S(1)}, u32[]{:S(2)}, u32[]{:S(2)}) collective-permute-start(f32[3,48,768]{2,1,0:T(8,128)S(1)} %copy-done), channel_id=1, source_target_pairs={{16,0},{32,16},{48,32},{64,48},{80,64},{96,80},{112,96},{17,1},{33... | collective-permute-start | bytes 1327112 | tf_op jit(solution)/shard_map/ppermute | solution.py:371
  104.4 0.6 copy-start.5
  104.4 0.6 copy-start.6
  125.5 63.8 %all-to-all-start.3 = ((f32[16,48,768]{2,1,0:T(8,128)}), f32[16,48,768]{2,1,0:T(8,128)}, u32[]{:S(2)}, u32[]{:S(2)}) async-start(f32[16,48,768]{2,1,0:T(8,128)} %potential.3), calls=%async_computation.3 | async-start | bytes 4718592 | tf_op jit(solution)/shard_map/all_to_all | solution.py:692
  131.3 0.8 copy-start.1
  132.1 0.8 copy-start.3
  134.7 29.6 %collective-permute-start.6 = (f32[24,768]{1,0:T(8,128)}, f32[24,768]{1,0:T(8,128)S(1)}, u32[]{:S(2)}, u32[]{:S(2)}) collective-permute-start(f32[24,768]{1,0:T(8,128)} %get-tuple-element.31), channel_id=1, source_target_pairs={{0,1},{1,2},{2,3},{3,4},{4,5},{5,6},{6,7},{7,8},{8,9},{9,10},{10,1... | collective-permute-start | bytes 221192 | tf_op jit(solution)/shard_map/ppermute | solution.py:371
  134.9 29.5 %collective-permute-start.7 = (f32[24,768]{1,0:T(8,128)}, f32[24,768]{1,0:T(8,128)S(1)}, u32[]{:S(2)}, u32[]{:S(2)}) collective-permute-start(f32[24,768]{1,0:T(8,128)} %get-tuple-element.32), channel_id=1, source_target_pairs={{1,0},{2,1},{3,2},{4,3},{5,4},{6,5},{7,6},{8,7},{9,8},{10,9},{11,1... | collective-permute-start | bytes 221192 | tf_op jit(solution)/shard_map/ppermute | solution.py:371
  164.4 0.6 copy-start.7
  165.0 0.6 copy-start.8
  189.3 36.4 %all-to-all-start.2 = ((f32[16,48,768]{2,1,0:T(8,128)}), f32[16,48,768]{2,1,0:T(8,128)}, u32[]{:S(2)}, u32[]{:S(2)}) async-start(f32[16,48,768]{2,1,0:T(8,128)} %potential.2), calls=%async_computation.2 | async-start | bytes 4718592 | tf_op jit(solution)/shard_map/all_to_all | solution.py:692

commit v3 on v2

--- a/solution.py
+++ b/solution.py
@@ -371,26 +371,28 @@
     return lax.ppermute(value, axis, pairs if up else [(b, a) for a, b in pairs])
 
 
-def edges_body(below_ref, above_ref, head_out, tail_out):
-    rows = below_ref.shape[1]
-    for z in range(reach):
-        for ref, first in ((below_ref, 0), (above_ref, reach * reach)):
-            to = slice(first + reach * z, first + reach * (z + 1))
-            head_out[to], tail_out[to] = ref[z, :reach], ref[z, rows - reach :]
-
-
-def edges(below, above):
-    width = below.shape[2]
-    count = -(-2 * reach * reach // 8) * 8
+def halo_body(low_ref, high_ref, head_ref, tail_ref, down_ref, up_ref):
+    count, rows, width = low_ref.shape
+    side = reach * count
+    held = head_ref.shape[0]
+    for planes_ref, first, out_ref in ((low_ref, 0, down_ref), (high_ref, held - side, up_ref)):
+        out_ref[: count * rows] = planes_ref[...].reshape(count * rows, width)
+        out_ref[count * rows : count * rows + side] = head_ref[first : first + side]
+        out_ref[count * rows + side : count * rows + 2 * side] = tail_ref[first : first + side]
+
+
+def halo_slabs(*inputs):
+    count, rows, width = inputs[0].shape
+    total = -(-count * (rows + 2 * reach) // 8) * 8
     return call(
-        edges_body,
-        [array(count, width)] * 2,
+        halo_body,
+        [array(total, width)] * 2,
         1.0,
         grid=(1,),
-        in_specs=[whole(below.shape)] * 2,
-        out_specs=[whole((count, width))] * 2,
-        name="edges",
-    )(below, above)
+        in_specs=[whole(value.shape) for value in inputs],
+        out_specs=[whole((total, width))] * 2,
+        name="halo_slabs",
+    )(*inputs)
 
 
 def roll_x(value, by):
@@ -453,7 +455,7 @@
 
 def potential_body(sources, groups, flag_ref, *refs):
     ext_ref, part_ref, smooth_ref, flat_ref, fx_ref, fy_ref, fz_ref = refs[-7:]
-    count = max(source[2] for source in sources) + 2
+    count = 6 if groups == 2 else 4
     plane_refs = refs[: -count - 17]
     sides_hbm = plane_refs[-count:]
     tab_hbm_ref, out_ref, tab_ref, tab_sems, pot_ref, tall_ref, stage_ref = refs[-count - 17 : -count - 10]
@@ -461,11 +463,22 @@
     side_refs = refs[-count - 7 : -7]
     planes, rows, width = pot_ref.shape
     each = planes // groups
-    sides = copy_all(list(zip(sides_hbm, side_refs)), side_sems)
+    sides = copy_all(
+        [
+            (hbm.at[pl.ds(hbm.shape[0] - ref.shape[0], ref.shape[0])], ref)
+            for hbm, ref in zip(sides_hbm, side_refs)
+        ],
+        side_sems,
+    )
+
+    def plane_of(plane, at):
+        ref = plane_refs[plane]
+        return ref.at[at] if len(ref.shape) == 3 else ref.at[pl.ds(at * rows, rows)]
+
     arriving = copy_all(
         [
-            (plane_refs[plane].at[pl.ds(at, 1)], ext_ref.at[pl.ds(z, 1), pl.ds(lead - 1, rows)])
-            for z, (plane, at, _, _) in enumerate(sources)
+            (plane_of(plane, at), ext_ref.at[z, pl.ds(lead - 1, rows)])
+            for z, (plane, at, *_) in enumerate(sources)
         ],
         in_sems,
     )
@@ -476,10 +489,10 @@
         return pl.when(flag_ref[flag] == 1) if groups == 2 else lambda body: None
 
     wait_all(sides)
-    for z, (_, _, side, row) in enumerate(sources):
-        at = slice(row, row + reach)
-        ext_ref[z, lead - 1 - reach : lead - 1] = side_refs[side][at]
-        ext_ref[z, lead - 1 + rows : lead - 1 + rows + reach] = side_refs[side + 1][at]
+    for z, (_, _, head, head_row, tail, tail_row) in enumerate(sources):
+        ext_ref[z, lead - 1 - reach : lead - 1] = side_refs[head][head_row : head_row + reach]
+        after = side_refs[tail][tail_row : tail_row + reach]
+        ext_ref[z, lead - 1 + rows : lead - 1 + rows + reach] = after
     wait_all(arriving)
     tables = load_tables(tab_hbm_ref, tab_ref, tab_sems)
 
@@ -601,7 +614,7 @@
         pltpu.SemaphoreType.DMA((2, parts // 2)),
         pltpu.SemaphoreType.DMA((len(sides),)),
     ]
-    scratch += [pltpu.VMEM(side.shape, f32) for side in sides]
+    scratch += [pltpu.VMEM((min(side.shape[0], sides[0].shape[0]), width), f32) for side in sides]
     for margin in (6, 4, 4, 2, 2, 2, 2):
         scratch.append(pltpu.VMEM((count + margin * groups, tall, width), f32))
     return call(
@@ -710,30 +723,28 @@
     inner, head, tail = inverse_columns(inner, factors, False)
     inner_sides = shift(tail, "py", True, True), shift(head, "py", False, True)
 
-    low_planes, high_planes, _ = lax.optimization_barrier((low_planes, high_planes, head))
-    below = shift(high_planes, "px", True, False)
-    above = shift(low_planes, "px", False, False)
+    down, up = halo_slabs(low_planes, high_planes, *outer_sides)
+    down, up, _ = lax.optimization_barrier((down, up, head))
+    below, above = shift(up, "px", True, False), shift(down, "px", False, False)
 
     def source(z):
         if unit <= z < depth - unit:
-            return 1, z - unit, 2, reach * (z - unit)
+            row = reach * (z - unit)
+            return 1, z - unit, 2, row, 3, row
         if 0 <= z < depth:
             at = z if z < unit else z - depth + 2 * unit
-            return 0, at, 0, reach * at
+            return 0, at, 0, reach * at, 1, reach * at
         at = z + reach if z < 0 else z - depth
-        return (2 if z < 0 else 3), at, 4, reach * (at + (0 if z < 0 else reach))
+        side = 2 if z < 0 else 3
+        return side, at, side + 2, reach * at, side + 2, reach * (reach + at)
 
     inside = [source(z) for z in range(unit - reach, depth - unit + reach)]
     outside = [source(z) for z in range(-reach, unit + reach)]
     outside += [source(z) for z in range(depth - unit - reach, depth + reach)]
     planes, sides = [outer, inner], [*outer_sides, *inner_sides]
-    spectral = potential_of(flags, planes, sides, inside, 1, tables, parts)
-    inner_waves = exchange(spectral)
-
-    head, tail = edges(below, above)
-    planes += [below, above]
-    sides += [shift(tail, "py", True, True), shift(head, "py", False, True)]
-    spectral = potential_of(flags, planes, sides, outside, 2, tables, parts)
+    inner_waves = exchange(potential_of(flags, planes, sides, inside, 1, tables, parts))
+    halo = [below, above]
+    spectral = potential_of(flags, planes + halo, sides + halo, outside, 2, tables, parts)
     outer_waves = exchange(spectral)
     result = forward_rows(flags, inner_waves, factors, (unit, 2 * unit), depth, None)
     result = forward_rows(flags, outer_waves, factors, (0, depth - unit), depth, result)

time: 240 us -> 218 us (0.908)
  waiting for transfers between devices: 89.2 us -> 68.4 us
    ppermute x8 -> x6, waiting for transfers between devices: 27.9 us -> 0.02 us  [shift(): lax.ppermute(value, axis, pairs if up else [(b, a) for a, b in pairs])]
    all_to_all x4, waiting for transfers between devices: 61.3 us -> 68.4 us  [exchange(): return lax.all_to_all(value, 'py', 0, 0, tiled=True)]
    ppermute x8 -> x6, starting transfers between devices: 12.8 us -> 11.1 us  [shift(): lax.ppermute(value, axis, pairs if up else [(b, a) for a, b in pairs])]
  transfers between devices with their start and end apart: 12 -> 10, of which waited for: 4 -> 4; matrix products, arithmetic and copies ran while one was open for 0% -> 0% of each run, Pallas kernels for 37% -> 41%
where the time goes in v3:
time: 218 us; the launch traced here: 215 us
  Pallas kernels  111 us (51%)
  waiting for transfers between devices  68.4 us (31%)
  starting transfers between devices  31.9 us (15%)
  local copies, waits for them, and re-layouts  2.91 us (1%)
    all_to_all x4, waiting for transfers between devices, exchange(): return lax.all_to_all(value, 'py', 0, 0, tiled=True)  68.4 us
    pallas_call x2, Pallas kernels, potential_of(): call(lambda *refs: potential_body(sources, groups, *refs), array(*out), 2...  44 us
    pallas_call x2, Pallas kernels, forward_rows(): call(lambda *refs: forward_rows_body(starts, *refs), array(2, depth, rows...  24.3 us
    all_to_all x4, starting transfers between devices, exchange(): return lax.all_to_all(value, 'py', 0, 0, tiled=True)  20.8 us
    pallas_call x2, Pallas kernels, inverse_columns(): call(lambda *refs: inverse_columns_body(sends, *refs), [array(planes, row...  19.2 us
    ppermute x6, starting transfers between devices, shift(): lax.ppermute(value, axis, pairs if up else [(b, a) for a, b in pairs])  11.1 us
    pallas_call x1, Pallas kernels, inverse_rows(): call(body, array(*out), 10.0, grid=(1,), in_specs=[in_hbm] * 2 + [pl.Bloc...  10.9 us
    pallas_call x1, Pallas kernels, inverse_rows(): call(body, [array(*out), made], 10.0, grid=(1,), in_specs=[in_hbm] * 3, o...  10.4 us
  transfers between devices with their start and end apart: 10, of which 4 were waited for; matrix products, arithmetic and copies ran while one was open for 0% of the time, Pallas kernels for 41%

profile of v3, /device:TPU:14, one launch (start us, length us, event | category | flops | bytes accessed | tf_op | source)
XLA Modules:
  0.0 215.2 jit_solution(16913429017678515005)
XLA Ops:
  0.0 10.4 %inverse_rows.2 = (f32[16,48,768]{2,1,0:T(8,128)}, bf16[4,768,768]{2,1,0:T(8,128)(2,1)}) custom-call(f32[2,16,48,768]{3,2,1,0:T(8,128)} %refs_0_.3, f32[2,4,768]{2,1,0:T(4,128)} %constant.17.clone.refs_1_.refs_2_, f32[2,48,768]{2,1,0:T(8,128)} %constant.18.clone.refs_2_.refs_3_), custom_call_target="tpu_custom_call" | custom-call | flops 10000000000 | bytes 1048576 | tf_op jit(solution)/shard_map/inverse_rows/pallas_call | solution.py:221
  10.4 6.3 %all-to-all-start = ((f32[16,48,768]{2,1,0:T(8,128)}), f32[16,48,768]{2,1,0:T(8,128)}, u32[]{:S(2)}, u32[]{:S(2)}) async-start(f32[16,48,768]{2,1,0:T(8,128)} %get-tuple-element.19), calls=%async_computation | async-start | bytes 4718592 | tf_op jit(solution)/shard_map/all_to_all | solution.py:705
  17.3 10.9 %inverse_rows.3 = f32[16,48,768]{2,1,0:T(8,128)} custom-call(f32[2,16,48,768]{3,2,1,0:T(8,128)} %refs_0_.3, bf16[4,768,768]{2,1,0:T(8,128)(2,1)} %get-tuple-element.21.refs_1_.refs_11_.refs_7_, s32[3]{0:T(128)} %add_convert_fusion.refs_2_.refs_0_), custom_call_target="tpu_custom_call" | custom-call | flops 10000000000 | bytes 1048576 | tf_op jit(solution)/shard_map/inverse_rows/pallas_call | solution.py:231
  28.1 21.0 %all-to-all-done.refs_0_ = f32[16,48,768]{2,1,0:T(8,128)} async-done(((f32[16,48,768]{2,1,0:T(8,128)}), f32[16,48,768]{2,1,0:T(8,128)}, u32[]{:S(2)}, u32[]{:S(2)}) %all-to-all-start) | async-done | bytes 2359328 | tf_op jit(solution)/shard_map/all_to_all | solution.py:705
  49.1 4.3 %all-to-all-start.1 = ((f32[16,48,768]{2,1,0:T(8,128)}), f32[16,48,768]{2,1,0:T(8,128)}, u32[]{:S(2)}, u32[]{:S(2)}) async-start(f32[16,48,768]{2,1,0:T(8,128)} %inverse_rows.3), calls=%async_computation.1 | async-start | bytes 4718592 | tf_op jit(solution)/shard_map/all_to_all | solution.py:705
  53.5 9.8 %inverse_columns.2 = (f32[8,48,768]{2,1,0:T(8,128)}, f32[24,768]{1,0:T(8,128)}, f32[24,768]{1,0:T(8,128)}, f32[3,48,768]{2,1,0:T(8,128)}, f32[3,48,768]{2,1,0:T(8,128)}) custom-call(f32[16,48,768]{2,1,0:T(8,128)} %all-to-all-done.refs_0_, f32[2,4,768]{2,1,0:T(4,128)} %constant.17.clone.refs_1_.refs_2_, f32[2,48,768]{2,1,0:T(8,128)} %constant.18.clone.refs_2_.refs_3_), custom_call_target="tpu_custom_call" | custom-call | flops 7000000000 | bytes 1048576 | tf_op jit(solution)/shard_map/inverse_columns/pallas_call | solution.py:355
  63.3 1.7 collective-permute-start.1
  65.1 20.5 %all-to-all-done.1.refs_0_ = f32[16,48,768]{2,1,0:T(8,128)} async-done(((f32[16,48,768]{2,1,0:T(8,128)}), f32[16,48,768]{2,1,0:T(8,128)}, u32[]{:S(2)}, u32[]{:S(2)}) %all-to-all-start.1) | async-done | bytes 2359328 | tf_op jit(solution)/shard_map/all_to_all | solution.py:705
  85.6 9.5 %inverse_columns.3 = (f32[8,48,768]{2,1,0:T(8,128)}, f32[24,768]{1,0:T(8,128)}, f32[24,768]{1,0:T(8,128)}) custom-call(f32[16,48,768]{2,1,0:T(8,128)} %all-to-all-done.1.refs_0_, f32[2,4,768]{2,1,0:T(4,128)} %constant.17.clone.refs_1_.refs_2_, f32[2,48,768]{2,1,0:T(8,128)} %constant.18.clone.refs_2_.refs_3_), custom_call_target="tpu_custom_call" | custom-call | flops 7000000000 | bytes 1048576 | tf_op jit(solution)/shard_map/inverse_columns/pallas_call | solution.py:355
  95.1 1.7 collective-permute-start.5
  96.9 0.6 copy-done.2
  97.5 2.2 %halo_slabs.1 = (f32[168,768]{1,0:T(8,128)}, f32[168,768]{1,0:T(8,128)}) custom-call(f32[3,48,768]{2,1,0:T(8,128)} %get-tuple-element.23.low_ref, f32[3,48,768]{2,1,0:T(8,128)} %get-tuple-element.24.high_ref, f32[24,768]{1,0:T(8,128)} %copy-done.2, f32[24,768]{1,0:T(8,128)} %copy-done.3), custom_call_target="tpu_custom_call" | custom-call | flops 1000000000 | bytes 1048576 | tf_op jit(solution)/shard_map/halo_slabs/pallas_call | solution.py:387
  99.7 5.6 %collective-permute-start.2 = (f32[168,768]{1,0:T(8,128)}, f32[168,768]{1,0:T(8,128)S(1)}, u32[]{:S(2)}, u32[]{:S(2)}) collective-permute-start(f32[168,768]{1,0:T(8,128)} %get-tuple-element.30), channel_id=1, source_target_pairs={{0,16},{16,32},{32,48},{48,64},{64,80},{80,96},{96,112},{1,17},{17... | collective-permute-start | bytes 1548296 | tf_op jit(solution)/shard_map/ppermute | solution.py:371
  105.3 1.9 collective-permute-start.3
  107.9 20.4 %potential.3 = f32[16,48,768]{2,1,0:T(8,128)} custom-call(s32[3]{0:T(128)} %add_convert_fusion.refs_2_.refs_0_, f32[8,48,768]{2,1,0:T(8,128)} %get-tuple-element.20.refs_1_, f32[8,48,768]{2,1,0:T(8,128)} %get-tuple-element.22.refs_2_, f32[24,768]{1,0:T(8,128)} %copy-done.2, f32[24,768]{1,0:T(8,128)} %copy-done.3, f32[24,768]{1,0:T(8,128)} %copy-done.4, ...), custom_call_target="tpu_custom_call" | custom-call | flops 20000000000 | bytes 1048576 | tf_op jit(solution)/shard_map/potential/pallas_call | solution.py:620
  128.3 5.8 %all-to-all-start.3 = ((f32[16,48,768]{2,1,0:T(8,128)}), f32[16,48,768]{2,1,0:T(8,128)}, u32[]{:S(2)}, u32[]{:S(2)}) async-start(f32[16,48,768]{2,1,0:T(8,128)} %potential.3), calls=%async_computation.3 | async-start | bytes 4718592 | tf_op jit(solution)/shard_map/all_to_all | solution.py:705
  134.2 0.8 copy-done
  135.0 0.8 copy-done.1
  135.8 23.7 %potential.2 = f32[16,48,768]{2,1,0:T(8,128)} custom-call(s32[3]{0:T(128)} %add_convert_fusion.refs_2_.refs_0_, f32[8,48,768]{2,1,0:T(8,128)} %get-tuple-element.20.refs_1_, f32[8,48,768]{2,1,0:T(8,128)} %get-tuple-element.22.refs_2_, f32[168,768]{1,0:T(8,128)} %copy-done, f32[168,768]{1,0:T(8,128)} %copy-done.1, f32[24,768]{1,0:T(8,128)} %copy-done.2, ...), custom_call_target="tpu_custom_call" | custom-call | flops 20000000000 | bytes 1048576 | tf_op jit(solution)/shard_map/potential/pallas_call | solution.py:620
  159.5 7.0 %all-to-all-done.3.refs_1_ = f32[16,48,768]{2,1,0:T(8,128)} async-done(((f32[16,48,768]{2,1,0:T(8,128)}), f32[16,48,768]{2,1,0:T(8,128)}, u32[]{:S(2)}, u32[]{:S(2)}) %all-to-all-start.3) | async-done | bytes 2359328 | tf_op jit(solution)/shard_map/all_to_all | solution.py:705
  166.5 4.3 %all-to-all-start.2 = ((f32[16,48,768]{2,1,0:T(8,128)}), f32[16,48,768]{2,1,0:T(8,128)}, u32[]{:S(2)}, u32[]{:S(2)}) async-start(f32[16,48,768]{2,1,0:T(8,128)} %potential.2), calls=%async_computation.2 | async-start | bytes 4718592 | tf_op jit(solution)/shard_map/all_to_all | solution.py:705
  170.8 12.1 %forward_rows.2.refs_4_ = f32[2,16,48,768]{3,2,1,0:T(8,128)} custom-call(s32[3]{0:T(128)} %add_convert_fusion.refs_2_.refs_0_, f32[16,48,768]{2,1,0:T(8,128)} %all-to-all-done.3.refs_1_, f32[2,4,768]{2,1,0:T(4,128)} %constant.17.clone.refs_1_.refs_2_, f32[2,48,768]{2,1,0:T(8,128)} %constant.18.clone.refs_2_.refs_3_), custom_call_target="tpu_custom_call" | custom-call | flops 10000000000 | bytes 1048576 | tf_op jit(solution)/shard_map/forward_rows/pallas_call | solution.py:691
  183.0 19.9 %all-to-all-done.2.refs_1_ = f32[16,48,768]{2,1,0:T(8,128)} async-done(((f32[16,48,768]{2,1,0:T(8,128)}), f32[16,48,768]{2,1,0:T(8,128)}, u32[]{:S(2)}, u32[]{:S(2)}) %all-to-all-start.2) | async-done | bytes 2359328 | tf_op jit(solution)/shard_map/all_to_all | solution.py:705
  202.9 12.2 %forward_rows.3 = f32[2,16,48,768]{3,2,1,0:T(8,128)} custom-call(s32[3]{0:T(128)} %add_convert_fusion.refs_2_.refs_0_, f32[16,48,768]{2,1,0:T(8,128)} %all-to-all-done.2.refs_1_, f32[2,4,768]{2,1,0:T(4,128)} %constant.17.clone.refs_1_.refs_2_, f32[2,48,768]{2,1,0:T(8,128)} %constant.18.clone.refs_2_.refs_3_, ...), custom_call_target="tpu_custom_call", output_to_operand_aliasing={{}: (4, {})} | custom-call | flops 10000000000 | bytes 1048576 | tf_op jit(solution)/shard_map/forward_rows/pallas_call | solution.py:691
  (18 shorter events, 1.4 us)
Async XLA Ops:
  10.4 38.7 %all-to-all-start = ((f32[16,48,768]{2,1,0:T(8,128)}), f32[16,48,768]{2,1,0:T(8,128)}, u32[]{:S(2)}, u32[]{:S(2)}) async-start(f32[16,48,768]{2,1,0:T(8,128)} %get-tuple-element.19), calls=%async_computation | async-start | bytes 4718592 | tf_op jit(solution)/shard_map/all_to_all | solution.py:705
  49.1 36.5 %all-to-all-start.1 = ((f32[16,48,768]{2,1,0:T(8,128)}), f32[16,48,768]{2,1,0:T(8,128)}, u32[]{:S(2)}, u32[]{:S(2)}) async-start(f32[16,48,768]{2,1,0:T(8,128)} %inverse_rows.3), calls=%async_computation.1 | async-start | bytes 4718592 | tf_op jit(solution)/shard_map/all_to_all | solution.py:705
  63.2 33.6 %collective-permute-start = (f32[24,768]{1,0:T(8,128)}, f32[24,768]{1,0:T(8,128)S(1)}, u32[]{:S(2)}, u32[]{:S(2)}) collective-permute-start(f32[24,768]{1,0:T(8,128)} %get-tuple-element.25), channel_id=1, source_target_pairs={{0,1},{1,2},{2,3},{3,4},{4,5},{5,6},{6,7},{7,8},{8,9},{9,10},{10,1... | collective-permute-start | bytes 221192 | tf_op jit(solution)/shard_map/ppermute | solution.py:371
  63.3 33.5 %collective-permute-start.1 = (f32[24,768]{1,0:T(8,128)}, f32[24,768]{1,0:T(8,128)S(1)}, u32[]{:S(2)}, u32[]{:S(2)}) collective-permute-start(f32[24,768]{1,0:T(8,128)} %get-tuple-element.26), channel_id=1, source_target_pairs={{1,0},{2,1},{3,2},{4,3},{5,4},{6,5},{7,6},{8,7},{9,8},{10,9},{11,1... | collective-permute-start | bytes 221192 | tf_op jit(solution)/shard_map/ppermute | solution.py:371
  95.0 12.2 %collective-permute-start.4 = (f32[24,768]{1,0:T(8,128)}, f32[24,768]{1,0:T(8,128)S(1)}, u32[]{:S(2)}, u32[]{:S(2)}) collective-permute-start(f32[24,768]{1,0:T(8,128)} %get-tuple-element.32), channel_id=1, source_target_pairs={{0,1},{1,2},{2,3},{3,4},{4,5},{5,6},{6,7},{7,8},{8,9},{9,10},{10,1... | collective-permute-start | bytes 221192 | tf_op jit(solution)/shard_map/ppermute | solution.py:371
  95.1 12.1 %collective-permute-start.5 = (f32[24,768]{1,0:T(8,128)}, f32[24,768]{1,0:T(8,128)S(1)}, u32[]{:S(2)}, u32[]{:S(2)}) collective-permute-start(f32[24,768]{1,0:T(8,128)} %get-tuple-element.29), channel_id=1, source_target_pairs={{1,0},{2,1},{3,2},{4,3},{5,4},{6,5},{7,6},{8,7},{9,8},{10,9},{11,1... | collective-permute-start | bytes 221192 | tf_op jit(solution)/shard_map/ppermute | solution.py:371
  96.9 0.6 copy-start.2
  96.9 0.7 copy-start.3
  99.7 34.4 %collective-permute-start.2 = (f32[168,768]{1,0:T(8,128)}, f32[168,768]{1,0:T(8,128)S(1)}, u32[]{:S(2)}, u32[]{:S(2)}) collective-permute-start(f32[168,768]{1,0:T(8,128)} %get-tuple-element.30), channel_id=1, source_target_pairs={{0,16},{16,32},{32,48},{48,64},{64,80},{80,96},{96,112},{1,17},{17... | collective-permute-start | bytes 1548296 | tf_op jit(solution)/shard_map/ppermute | solution.py:371
  105.3 28.9 %collective-permute-start.3 = (f32[168,768]{1,0:T(8,128)}, f32[168,768]{1,0:T(8,128)S(1)}, u32[]{:S(2)}, u32[]{:S(2)}) collective-permute-start(f32[168,768]{1,0:T(8,128)} %get-tuple-element.31), channel_id=1, source_target_pairs={{16,0},{32,16},{48,32},{64,48},{80,64},{96,80},{112,96},{17,1},{33... | collective-permute-start | bytes 1548296 | tf_op jit(solution)/shard_map/ppermute | solution.py:371
  107.3 0.6 copy-start.4
  107.3 0.6 copy-start.5
  128.3 38.2 %all-to-all-start.3 = ((f32[16,48,768]{2,1,0:T(8,128)}), f32[16,48,768]{2,1,0:T(8,128)}, u32[]{:S(2)}, u32[]{:S(2)}) async-start(f32[16,48,768]{2,1,0:T(8,128)} %potential.3), calls=%async_computation.3 | async-start | bytes 4718592 | tf_op jit(solution)/shard_map/all_to_all | solution.py:705
  134.2 0.8 copy-start
  135.0 0.8 copy-start.1
  166.5 36.4 %all-to-all-start.2 = ((f32[16,48,768]{2,1,0:T(8,128)}), f32[16,48,768]{2,1,0:T(8,128)}, u32[]{:S(2)}, u32[]{:S(2)}) async-start(f32[16,48,768]{2,1,0:T(8,128)} %potential.2), calls=%async_computation.2 | async-start | bytes 4718592 | tf_op jit(solution)/shard_map/all_to_all | solution.py:705

commit v4 on v3

--- a/solution.py
+++ b/solution.py
@@ -106,7 +106,7 @@
         tab_ref[2, rows], tab_ref[3, rows] = split(sin_a * fine_cos + cos_a * fine_sin)
         return carry
 
-    lax.fori_loop(0, coarse_ref.shape[1], step, 0)
+    lax.fori_loop(0, tab_ref.shape[1] // 4 // stride, step, 0)
 
     tile = 16
     width = tab_ref.shape[2]
@@ -134,26 +134,28 @@
     return [pltpu.VMEM(factor.shape, f32) for factor in factors] + [pltpu.SemaphoreType.DMA((2,))]
 
 
-def phase_factors(length, stride):
-    def waves(rows, scale):
-        angle = (np.outer(rows, np.arange(length)) % length) * (2.0 * math.pi / length)
+def phase_factors(length, stride, norm):
+    def waves(rows, scale, period):
+        angle = (np.outer(rows, np.arange(length)) % period) * (2.0 * math.pi / period)
         return np.stack([np.cos(angle), np.sin(angle)]).astype(np.float32) * np.float32(scale)
 
-    coarse = waves(np.arange(0, length // 4, stride), 1.0)
-    fine = waves(np.arange(stride), 1.0 / math.sqrt(length))
+    coarse = waves(np.arange(0, length // 4, stride), 1.0, length)
+    coarse = np.concatenate([coarse, waves(np.arange(1, 2), 1.0, 2 * length)], axis=1)
+    fine = waves(np.arange(stride), 1.0 / math.sqrt(norm), length)
     return jnp.asarray(coarse), jnp.asarray(fine)
 
 
-def inverse_rows_body(blocks, fills, *refs):
-    if fills:
-        rho_ref, coarse_hbm_ref, fine_hbm_ref, out_ref, tab_out_ref = refs[:5]
-        coarse_ref, fine_ref, factor_sems = refs[-3:]
-        refs = refs[:-3]
+def inverse_rows_body(blocks, makes, *refs):
+    rho_ref, coarse_hbm_ref, fine_hbm_ref = refs[:3]
+    if makes:
+        factors_hbm, out_ref, tab_out_ref = refs[3:5], refs[6], refs[7]
+        full_ref, full_coarse_ref, full_fine_ref, full_factor_sems, full_sems = refs[-5:]
+        refs = refs[:-5]
     else:
-        rho_ref, tab_hbm_ref, _, out_ref = refs[:4]
-    tab_ref, tab_sems, x_ref, wide_ref, stage_ref, in_sems, out_sems = refs[-7:]
-    width = tab_ref.shape[1]
-    lanes = wide_ref.shape[1] // 2
+        out_ref = refs[3]
+    tab_ref, x_ref, wide_ref, stage_ref, in_sems, out_sems, coarse_ref, fine_ref, factor_sems = refs[-9:]
+    half = tab_ref.shape[1]
+    lanes = wide_ref.shape[2] // 2
     unit = x_ref.shape[1] // len(blocks)
     arriving = [
         copy_all(
@@ -165,79 +167,93 @@
         )
         for c in range(2)
     ]
-    if fills:
-        fill_tables((coarse_hbm_ref, fine_hbm_ref), coarse_ref, fine_ref, tab_ref, factor_sems)
-        tables = copy_all([(tab_ref.at[i], tab_out_ref.at[i]) for i in range(4)], tab_sems)
-    else:
-        tables = load_tables(tab_hbm_ref, tab_ref, tab_sems)
+    fill_tables((coarse_hbm_ref, fine_hbm_ref), coarse_ref, fine_ref, tab_ref, factor_sems)
     for c in range(2):
         wait_all(arriving[c])
-        high, low = split(x_ref[c].reshape(lanes, width).T)
-        cos_at = slice(c * lanes, (c + 1) * lanes)
-        sin_at = slice((1 - c) * lanes, (2 - c) * lanes)
-        for k, value in enumerate((high, high, low)):
-            wide_ref[k * width : (k + 1) * width, cos_at] = value
-            wide_ref[(k + 3) * width : (k + 4) * width, sin_at] = value if c == 0 else -value
-    if not fills:
-        wait_all(tables)
-    parts, block, out_lanes = stage_ref.shape
+    real, imag = [x_ref[c].reshape(lanes, 2 * half) for c in range(2)]
+    last = coarse_ref.shape[1] - 1
+    wave_cos, wave_sin = coarse_ref[0, last:], coarse_ref[1, last:]
+    for p in range(2):
+        if p == 0:
+            values = real[:, :half] + real[:, half:], imag[:, :half] + imag[:, half:]
+        else:
+            odd_re, odd_im = real[:, :half] - real[:, half:], imag[:, :half] - imag[:, half:]
+            values = odd_re * wave_cos - odd_im * wave_sin, odd_re * wave_sin + odd_im * wave_cos
+        for c in range(2):
+            high, low = split(values[c].T)
+            cos_at = slice(c * lanes, (c + 1) * lanes)
+            sin_at = slice((1 - c) * lanes, (2 - c) * lanes)
+            for k, value in enumerate((high, high, low)):
+                wide_ref[p, k * half : (k + 1) * half, cos_at] = value
+                turned = value if c == 0 else -value
+                wide_ref[p, (k + 3) * half : (k + 4) * half, sin_at] = turned
+    parts, _, block, _ = stage_ref.shape
+    out_lanes = 2 * lanes
     group = parts // 2
+    count = half // 2
 
     def step(m, carry):
-        at = pl.ds(pl.multiple_of(m * group * block, group * block), group * block)
+        at = pl.ds(pl.multiple_of(m * count, count), count)
         ch, sh = tab_ref[0, at], tab_ref[2, at]
         left = jnp.concatenate([ch, tab_ref[1, at], ch, sh, tab_ref[3, at], sh], axis=1)
-        product = dot_nn(left, wide_ref[...])
-        stage_ref[pl.ds(m * group, group)] = product.reshape(group, block, out_lanes)
+        for p in range(2):
+            product = dot_nn(left, wide_ref[p]).reshape(group, block // 2, out_lanes)
+            for g in range(group):
+                for i in range(out_lanes // 128):
+                    to = pl.ds(p, block // 2, stride=2)
+                    stage_ref[m * group + g, i, to, :] = product[g, :, i * 128 : (i + 1) * 128]
         send_group(stage_ref, out_ref, out_sems, m, group)
         return carry
 
     lax.fori_loop(0, 2, step, 0)
+    if makes:
+        fill_tables(factors_hbm, full_coarse_ref, full_fine_ref, full_ref, full_factor_sems)
+        wait_all(copy_all([(full_ref.at[i], tab_out_ref.at[i]) for i in range(4)], full_sems))
     for m in range(2):
         wait_all(group_copies(stage_ref, out_ref, out_sems, m, group))
-    if fills:
-        wait_all(tables)
-
-
-def inverse_rows(rho_hat, factors, tables, flags, blocks):
+
+
+def inverse_rows(rho_hat, factors, full, flags, blocks):
     _, depth, local, width = rho_hat.shape
-    parts = width // factors[1].shape[1]
+    half = factors[1].shape[2]
+    block = factors[1].shape[1]
+    parts = width // block
     unit = depth // 4
     planes = len(blocks) * unit
     lanes = planes * local
-    block = width // parts
-    out = (parts, block, 2 * lanes)
-    scratch = table_scratch(width) + [
+    out = (parts, 2 * lanes // 128, block, 128)
+    scratch = [
+        pltpu.VMEM((4, half, half), bf16),
         pltpu.VMEM((2, planes, local, width), f32),
-        pltpu.VMEM((6 * width, 2 * lanes), bf16),
+        pltpu.VMEM((2, 6 * half, 2 * lanes), bf16),
         pltpu.VMEM(out, f32),
         pltpu.SemaphoreType.DMA((2, len(blocks))),
         pltpu.SemaphoreType.DMA((2, parts // 2)),
-    ]
-    fills = tables is None
-    body = lambda *refs: inverse_rows_body(blocks, fills, *refs)
-    if fills:
-        made = jax.ShapeDtypeStruct((4, width, width), bf16)
+    ] + factor_scratch(factors)
+    makes = full is not None
+    body = lambda *refs: inverse_rows_body(blocks, makes, *refs)
+    if makes:
+        scratch += [pltpu.VMEM((4, width, width), bf16)] + factor_scratch(full)
         return call(
             body,
-            [array(*out), made],
+            [array(*out), jax.ShapeDtypeStruct((4, width, width), bf16)],
             10.0,
             grid=(1,),
-            in_specs=[in_hbm] * 3,
-            out_specs=[in_hbm, in_hbm],
-            scratch_shapes=scratch + factor_scratch(factors),
+            in_specs=[in_hbm] * 5 + [pl.BlockSpec(memory_space=pltpu.SMEM)],
+            out_specs=[in_hbm] * 2,
+            scratch_shapes=scratch + [pltpu.SemaphoreType.DMA((4,))],
             name="inverse_rows",
-        )(rho_hat, *factors)
+        )(rho_hat, *factors, *full, flags)
     return call(
         body,
         array(*out),
         10.0,
         grid=(1,),
-        in_specs=[in_hbm] * 2 + [pl.BlockSpec(memory_space=pltpu.SMEM)],
+        in_specs=[in_hbm] * 3,
         out_specs=in_hbm,
         scratch_shapes=scratch,
         name="inverse_rows",
-    )(rho_hat, tables, flags)
+    )(rho_hat, *factors)
 
 
 def tile_copies(hbm_ref, in_ref, sems, t):
@@ -247,23 +263,30 @@
         at = pl.ds(pl.multiple_of(t * gather_tile, gather_tile), gather_tile)
     blocks = [pl.ds(g * group, group) for g in range(4)]
     return [
-        pltpu.make_async_copy(hbm_ref.at[d, at], in_ref.at[d, at], sems.at[t, g])
+        pltpu.make_async_copy(hbm_ref.at[d, :, at], in_ref.at[d, :, at], sems.at[t, g])
+        if len(in_ref.shape) == 4
+        else pltpu.make_async_copy(hbm_ref.at[d, at], in_ref.at[d, at], sems.at[t, g])
         for g, d in enumerate(blocks)
     ]
 
 
 def fetch_blocks(hbm_ref, in_ref, sems):
-    for t in range(in_ref.shape[1] // gather_tile):
+    for t in range(in_ref.shape[-2] // gather_tile):
         for copy in tile_copies(hbm_ref, in_ref, sems, t):
             copy.start()
 
 
 def gather_blocks(hbm_ref, in_ref, sems, high_ref, low_ref):
-    parts, rows, lanes = in_ref.shape
+    parts, rows = in_ref.shape[0], in_ref.shape[-2]
     width = high_ref.shape[2]
     local = width // parts
-    planes = lanes // (2 * local)
+    planes = high_ref.shape[1] // rows
     tile = gather_tile
+
+    def load(p, at, block):
+        if len(in_ref.shape) == 4:
+            return in_ref[p, block, at]
+        return in_ref[p, at, block * 128 : (block + 1) * 128]
 
     def gather_rows(t, carry):
         wait_all(tile_copies(hbm_ref, in_ref, sems, t))
@@ -275,9 +298,9 @@
             block, offset = first // 128, first % 128
             turned = []
             for p in range(parts):
-                value = in_ref[p, at, block * 128 : (block + 1) * 128]
+                value = load(p, at, block)
                 if offset + local > 128:
-                    after = in_ref[p, at, (block + 1) * 128 : (block + 2) * 128]
+                    after = load(p, at, block + 1)
                     value = jnp.where(lane < offset, after, value)
                 turned.append(pltpu.roll(value, (p * local - offset) % 128, 1))
             to = pl.ds(pl.multiple_of(z * rows + t * tile, tile), tile)
@@ -327,8 +350,9 @@
         pltpu.make_async_copy(stage_ref.at[z], out_ref.at[z], out_sems.at[z]) for z in range(planes)
     ]
     for m in range(2 if sends else 0):
-        slab = (stage_ref.at[pl.ds(m * (planes - reach), reach)], refs[3 + m])
-        leaving += copy_all([slab], send_sems.at[m])
+        first = m * (planes - reach)
+        pairs = [(stage_ref.at[first + z], refs[3 + m].at[pl.ds(z * rows, rows)]) for z in range(reach)]
+        leaving += copy_all(pairs, send_sems.at[m])
     for z in range(planes):
         at = slice(reach * z, reach * (z + 1))
         head_ref[at] = stage_ref[z, :reach]
@@ -337,7 +361,8 @@
 
 
 def inverse_columns(blocks, factors, sends):
-    parts, rows, lanes = blocks.shape
+    parts, _, rows, _ = blocks.shape
+    lanes = blocks.shape[1] * blocks.shape[3]
     width = factors[0].shape[2]
     planes = lanes * parts // (2 * width)
     side = (reach * planes, width)
@@ -350,12 +375,12 @@
         pltpu.VMEM((2, planes * rows, width), bf16),
         pltpu.SemaphoreType.DMA((rows // gather_tile, 4)),
         pltpu.SemaphoreType.DMA((planes,)),
-        pltpu.SemaphoreType.DMA((2, 1)),
+        pltpu.SemaphoreType.DMA((2, reach)),
     ]
     return call(
         lambda *refs: inverse_columns_body(sends, *refs),
         [array(planes, rows, width), array(*side), array(*side)]
-        + [array(reach, rows, width)] * slabs,
+        + [array(slab_rows(rows), width)] * slabs,
         7.0,
         grid=(1,),
         in_specs=[in_hbm] * 3,
@@ -371,28 +396,37 @@
     return lax.ppermute(value, axis, pairs if up else [(b, a) for a, b in pairs])
 
 
-def halo_body(low_ref, high_ref, head_ref, tail_ref, down_ref, up_ref):
-    count, rows, width = low_ref.shape
-    side = reach * count
+def slab_rows(rows):
+    return reach * rows + -(-2 * reach * reach // 8) * 8
+
+
+def halo_body(head_ref, tail_ref, low_ref, high_ref, down_ref, up_ref, edge_ref, sems):
+    side = reach * reach
     held = head_ref.shape[0]
-    for planes_ref, first, out_ref in ((low_ref, 0, down_ref), (high_ref, held - side, up_ref)):
-        out_ref[: count * rows] = planes_ref[...].reshape(count * rows, width)
-        out_ref[count * rows : count * rows + side] = head_ref[first : first + side]
-        out_ref[count * rows + side : count * rows + 2 * side] = tail_ref[first : first + side]
-
-
-def halo_slabs(*inputs):
-    count, rows, width = inputs[0].shape
-    total = -(-count * (rows + 2 * reach) // 8) * 8
+    copies = []
+    for i, (first, out_ref) in enumerate(((0, down_ref), (held - side, up_ref))):
+        edge_ref[i, :side] = head_ref[first : first + side]
+        edge_ref[i, side : 2 * side] = tail_ref[first : first + side]
+        count = edge_ref.shape[1]
+        to = out_ref.at[pl.ds(out_ref.shape[0] - count, count)]
+        copies += copy_all([(edge_ref.at[i], to)], sems.at[i])
+    wait_all(copies)
+
+
+def halo_slabs(low, high, head, tail):
+    total, width = low.shape
+    count = -(-2 * reach * reach // 8) * 8
     return call(
         halo_body,
         [array(total, width)] * 2,
         1.0,
         grid=(1,),
-        in_specs=[whole(value.shape) for value in inputs],
-        out_specs=[whole((total, width))] * 2,
+        in_specs=[whole(head.shape), whole(tail.shape), in_hbm, in_hbm],
+        out_specs=[in_hbm] * 2,
+        scratch_shapes=[pltpu.VMEM((2, count, width), f32), pltpu.SemaphoreType.DMA((2, 1))],
+        input_output_aliases={2: 0, 3: 1},
         name="halo_slabs",
-    )(*inputs)
+    )(head, tail, low, high)
 
 
 def roll_x(value, by):
@@ -623,7 +657,9 @@
         20.0,
         grid=(1,),
         in_specs=[pl.BlockSpec(memory_space=pltpu.SMEM)]
-        + [in_hbm] * (len(planes) + len(sides) + 1),
+        + [in_hbm] * len(planes)
+        + [pl.BlockSpec(memory_space=pl.ANY)] * len(sides)
+        + [in_hbm],
         out_specs=in_hbm,
         scratch_shapes=scratch,
         name="potential",
@@ -713,11 +749,13 @@
     ).astype(jnp.int32)
     depth, width = rho_hat.shape[1], rho_hat.shape[3]
     unit = depth // 4
-    factors = phase_factors(width, width // parts)
-
-    outer, tables = inverse_rows(rho_hat, factors, None, None, (0, 3))
-    outer = exchange(outer)
-    inner = exchange(inverse_rows(rho_hat, factors, tables, flags, (1, 2)))
+    block = width // parts
+    factors = phase_factors(width, block, width)
+    half_factors = phase_factors(width // 2, block, width)
+
+    outer = exchange(inverse_rows(rho_hat, half_factors, None, None, (0, 3)))
+    inner, tables = inverse_rows(rho_hat, half_factors, factors, flags, (1, 2))
+    inner = exchange(inner)
     outer, head, tail, low_planes, high_planes = inverse_columns(outer, factors, True)
     outer_sides = shift(tail, "py", True, True), shift(head, "py", False, True)
     inner, head, tail = inverse_columns(inner, factors, False)

time: 218 us -> 214 us (0.982)
  Pallas kernels: 111 us -> 107 us
    pallas_call x2, Pallas kernels: 21.2 us -> 18 us  [the longest x1 10.9 us: inverse_rows(): call(body, [array(*out), jax.ShapeDtypeStruct((4, width, width), bf16)],...]
  transfers between devices with their start and end apart: 10 -> 10, of which waited for: 4 -> 4; matrix products, arithmetic and copies ran while one was open for 0% -> 0% of each run, Pallas kernels for 41% -> 42%
where the time goes in v4:
time: 214 us; the launch traced here: 211 us
  Pallas kernels  107 us (50%)
  waiting for transfers between devices  68.3 us (32%)
  starting transfers between devices  32 us (15%)
  local copies, waits for them, and re-layouts  2.91 us (1%)
    all_to_all x4, waiting for transfers between devices, exchange(): return lax.all_to_all(value, 'py', 0, 0, tiled=True)  68.3 us
    pallas_call x2, Pallas kernels, potential_of(): call(lambda *refs: potential_body(sources, groups, *refs), array(*out), 2...  44 us
    pallas_call x2, Pallas kernels, forward_rows(): call(lambda *refs: forward_rows_body(starts, *refs), array(2, depth, rows...  24.3 us
    all_to_all x4, starting transfers between devices, exchange(): return lax.all_to_all(value, 'py', 0, 0, tiled=True)  20.8 us
    pallas_call x2, Pallas kernels, inverse_columns(): call(lambda *refs: inverse_columns_body(sends, *refs), [array(planes, row...  19.4 us
    ppermute x6, starting transfers between devices, shift(): lax.ppermute(value, axis, pairs if up else [(b, a) for a, b in pairs])  11.1 us
    pallas_call x1, Pallas kernels, inverse_rows(): call(body, [array(*out), jax.ShapeDtypeStruct((4, width, width), bf16)],...  10.9 us
    pallas_call x1, Pallas kernels, inverse_rows(): call(body, array(*out), 10.0, grid=(1,), in_specs=[in_hbm] * 3, out_specs...  7.1 us
  transfers between devices with their start and end apart: 10, of which 4 were waited for; matrix products, arithmetic and copies ran while one was open for 0% of the time, Pallas kernels for 42%

profile of v4, /device:TPU:14, one launch (start us, length us, event | category | flops | bytes accessed | tf_op | source)
XLA Modules:
  0.0 211.4 jit_solution(6302139220959583698)
XLA Ops:
  0.0 7.1 %inverse_rows.2 = f32[16,6,48,128]{3,2,1,0:T(8,128)} custom-call(f32[2,16,48,768]{3,2,1,0:T(8,128)} %refs_0_.3, f32[2,3,384]{2,1,0:T(4,128)} %constant.23.clone.refs_1_, f32[2,48,384]{2,1,0:T(8,128)} %constant.24.clone.refs_2_), custom_call_target="tpu_custom_call" | custom-call | flops 10000000000 | bytes 1048576 | tf_op jit(solution)/shard_map/inverse_rows/pallas_call | solution.py:247
  7.1 6.3 %all-to-all-start = ((f32[16,6,48,128]{3,2,1,0:T(8,128)}), f32[16,6,48,128]{3,2,1,0:T(8,128)}, u32[]{:S(2)}, u32[]{:S(2)}) async-start(f32[16,6,48,128]{3,2,1,0:T(8,128)} %inverse_rows.2), calls=%async_computation | async-start | bytes 4718592 | tf_op jit(solution)/shard_map/all_to_all | solution.py:741
  14.0 10.9 %inverse_rows.3 = (f32[16,6,48,128]{3,2,1,0:T(8,128)}, bf16[4,768,768]{2,1,0:T(8,128)(2,1)}) custom-call(f32[2,16,48,768]{3,2,1,0:T(8,128)} %refs_0_.3, f32[2,3,384]{2,1,0:T(4,128)} %constant.23.clone.refs_1_, f32[2,48,384]{2,1,0:T(8,128)} %constant.24.clone.refs_2_, f32[2,5,768]{2,1,0:T(8,128)} %constant.21.clone.refs_1_.refs_3_.refs_2_, ...), custom_call_target="tpu_custom_call" | custom-call | flops 10000000000 | bytes 1048576 | tf_op jit(solution)/shard_map/inverse_rows/pallas_call | solution.py:237
  24.9 21.0 %all-to-all-done.refs_0_ = f32[16,6,48,128]{3,2,1,0:T(8,128)} async-done(((f32[16,6,48,128]{3,2,1,0:T(8,128)}), f32[16,6,48,128]{3,2,1,0:T(8,128)}, u32[]{:S(2)}, u32[]{:S(2)}) %all-to-all-start) | async-done | bytes 2359328 | tf_op jit(solution)/shard_map/all_to_all | solution.py:741
  45.8 4.3 %all-to-all-start.1 = ((f32[16,6,48,128]{3,2,1,0:T(8,128)}), f32[16,6,48,128]{3,2,1,0:T(8,128)}, u32[]{:S(2)}, u32[]{:S(2)}) async-start(f32[16,6,48,128]{3,2,1,0:T(8,128)} %get-tuple-element.20), calls=%async_computation.1 | async-start | bytes 4718592 | tf_op jit(solution)/shard_map/all_to_all | solution.py:741
  50.2 9.9 %inverse_columns.2 = (f32[8,48,768]{2,1,0:T(8,128)}, f32[24,768]{1,0:T(8,128)}, f32[24,768]{1,0:T(8,128)}, f32[168,768]{1,0:T(8,128)}, f32[168,768]{1,0:T(8,128)}) custom-call(f32[16,6,48,128]{3,2,1,0:T(8,128)} %all-to-all-done.refs_0_, f32[2,5,768]{2,1,0:T(8,128)} %constant.21.clone.refs_1_.refs_3_.refs_2_, f32[2,48,768]{2,1,0:T(8,128)} %constant.22.clone.refs_2_.refs_4_.refs_3_), custom_call_target="tpu_custom_call" | custom-call | flops 7000000000 | bytes 1048576 | tf_op jit(solution)/shard_map/inverse_columns/pallas_call | solution.py:380
  60.2 1.7 collective-permute-start.1
  61.9 20.4 %all-to-all-done.1.refs_0_ = f32[16,6,48,128]{3,2,1,0:T(8,128)} async-done(((f32[16,6,48,128]{3,2,1,0:T(8,128)}), f32[16,6,48,128]{3,2,1,0:T(8,128)}, u32[]{:S(2)}, u32[]{:S(2)}) %all-to-all-start.1) | async-done | bytes 2359328 | tf_op jit(solution)/shard_map/all_to_all | solution.py:741
  82.3 9.5 %inverse_columns.3 = (f32[8,48,768]{2,1,0:T(8,128)}, f32[24,768]{1,0:T(8,128)}, f32[24,768]{1,0:T(8,128)}) custom-call(f32[16,6,48,128]{3,2,1,0:T(8,128)} %all-to-all-done.1.refs_0_, f32[2,5,768]{2,1,0:T(8,128)} %constant.21.clone.refs_1_.refs_3_.refs_2_, f32[2,48,768]{2,1,0:T(8,128)} %constant.22.clone.refs_2_.refs_4_.refs_3_), custom_call_target="tpu_custom_call" | custom-call | flops 7000000000 | bytes 1048576 | tf_op jit(solution)/shard_map/inverse_columns/pallas_call | solution.py:380
  91.9 1.7 collective-permute-start.5
  93.7 0.6 copy-done.2
  94.3 1.6 halo_slabs.1
  95.9 5.4 %collective-permute-start.2 = (f32[168,768]{1,0:T(8,128)}, f32[168,768]{1,0:T(8,128)S(1)}, u32[]{:S(2)}, u32[]{:S(2)}) collective-permute-start(f32[168,768]{1,0:T(8,128)} %get-tuple-element.29), channel_id=1, source_target_pairs={{0,16},{16,32},{32,48},{48,64},{64,80},{80,96},{96,112},{1,17},{17... | collective-permute-start | bytes 1548296 | tf_op jit(solution)/shard_map/ppermute | solution.py:396
  101.4 2.1 collective-permute-start.3
  104.1 20.4 %potential.3 = f32[16,48,768]{2,1,0:T(8,128)} custom-call(s32[3]{0:T(128)} %add_convert_fusion.refs_5_.refs_0_, f32[8,48,768]{2,1,0:T(8,128)} %get-tuple-element.19.refs_1_, f32[8,48,768]{2,1,0:T(8,128)} %get-tuple-element.21.refs_2_, f32[24,768]{1,0:T(8,128)} %copy-done.2, f32[24,768]{1,0:T(8,128)} %copy-done.3, f32[24,768]{1,0:T(8,128)} %copy-done.4, ...), custom_call_target="tpu_custom_call" | custom-call | flops 20000000000 | bytes 1048576 | tf_op jit(solution)/shard_map/potential/pallas_call | solution.py:654
  124.5 5.8 %all-to-all-start.3 = ((f32[16,48,768]{2,1,0:T(8,128)}), f32[16,48,768]{2,1,0:T(8,128)}, u32[]{:S(2)}, u32[]{:S(2)}) async-start(f32[16,48,768]{2,1,0:T(8,128)} %potential.3), calls=%async_computation.3 | async-start | bytes 4718592 | tf_op jit(solution)/shard_map/all_to_all | solution.py:741
  130.4 0.8 copy-done
  131.2 0.8 copy-done.1
  132.0 23.7 %potential.2 = f32[16,48,768]{2,1,0:T(8,128)} custom-call(s32[3]{0:T(128)} %add_convert_fusion.refs_5_.refs_0_, f32[8,48,768]{2,1,0:T(8,128)} %get-tuple-element.19.refs_1_, f32[8,48,768]{2,1,0:T(8,128)} %get-tuple-element.21.refs_2_, f32[168,768]{1,0:T(8,128)} %copy-done, f32[168,768]{1,0:T(8,128)} %copy-done.1, f32[24,768]{1,0:T(8,128)} %copy-done.2, ...), custom_call_target="tpu_custom_call" | custom-call | flops 20000000000 | bytes 1048576 | tf_op jit(solution)/shard_map/potential/pallas_call | solution.py:654
  155.7 7.0 %all-to-all-done.3.refs_1_ = f32[16,48,768]{2,1,0:T(8,128)} async-done(((f32[16,48,768]{2,1,0:T(8,128)}), f32[16,48,768]{2,1,0:T(8,128)}, u32[]{:S(2)}, u32[]{:S(2)}) %all-to-all-start.3) | async-done | bytes 2359328 | tf_op jit(solution)/shard_map/all_to_all | solution.py:741
  162.7 4.3 %all-to-all-start.2 = ((f32[16,48,768]{2,1,0:T(8,128)}), f32[16,48,768]{2,1,0:T(8,128)}, u32[]{:S(2)}, u32[]{:S(2)}) async-start(f32[16,48,768]{2,1,0:T(8,128)} %potential.2), calls=%async_computation.2 | async-start | bytes 4718592 | tf_op jit(solution)/shard_map/all_to_all | solution.py:741
  167.1 12.2 %forward_rows.2.refs_4_ = f32[2,16,48,768]{3,2,1,0:T(8,128)} custom-call(s32[3]{0:T(128)} %add_convert_fusion.refs_5_.refs_0_, f32[16,48,768]{2,1,0:T(8,128)} %all-to-all-done.3.refs_1_, f32[2,5,768]{2,1,0:T(8,128)} %constant.21.clone.refs_1_.refs_3_.refs_2_, f32[2,48,768]{2,1,0:T(8,128)} %constant.22.clone.refs_2_.refs_4_.refs_3_), custom_call_target="tpu_custom_call" | custom-call | flops 10000000000 | bytes 1048576 | tf_op jit(solution)/shard_map/forward_rows/pallas_call | solution.py:727
  179.2 19.9 %all-to-all-done.2.refs_1_ = f32[16,48,768]{2,1,0:T(8,128)} async-done(((f32[16,48,768]{2,1,0:T(8,128)}), f32[16,48,768]{2,1,0:T(8,128)}, u32[]{:S(2)}, u32[]{:S(2)}) %all-to-all-start.2) | async-done | bytes 2359328 | tf_op jit(solution)/shard_map/all_to_all | solution.py:741
  199.1 12.2 %forward_rows.3 = f32[2,16,48,768]{3,2,1,0:T(8,128)} custom-call(s32[3]{0:T(128)} %add_convert_fusion.refs_5_.refs_0_, f32[16,48,768]{2,1,0:T(8,128)} %all-to-all-done.2.refs_1_, f32[2,5,768]{2,1,0:T(8,128)} %constant.21.clone.refs_1_.refs_3_.refs_2_, f32[2,48,768]{2,1,0:T(8,128)} %constant.22.clone.refs_2_.refs_4_.refs_3_, ...), custom_call_target="tpu_custom_call", output_to_operand_aliasing={{}: (4, {})} | custom-call | flops 10000000000 | bytes 1048576 | tf_op jit(solution)/shard_map/forward_rows/pallas_call | solution.py:727
  (18 shorter events, 1.4 us)
Async XLA Ops:
  7.1 38.7 %all-to-all-start = ((f32[16,6,48,128]{3,2,1,0:T(8,128)}), f32[16,6,48,128]{3,2,1,0:T(8,128)}, u32[]{:S(2)}, u32[]{:S(2)}) async-start(f32[16,6,48,128]{3,2,1,0:T(8,128)} %inverse_rows.2), calls=%async_computation | async-start | bytes 4718592 | tf_op jit(solution)/shard_map/all_to_all | solution.py:741
  45.8 36.5 %all-to-all-start.1 = ((f32[16,6,48,128]{3,2,1,0:T(8,128)}), f32[16,6,48,128]{3,2,1,0:T(8,128)}, u32[]{:S(2)}, u32[]{:S(2)}) async-start(f32[16,6,48,128]{3,2,1,0:T(8,128)} %get-tuple-element.20), calls=%async_computation.1 | async-start | bytes 4718592 | tf_op jit(solution)/shard_map/all_to_all | solution.py:741
  60.1 33.6 %collective-permute-start = (f32[24,768]{1,0:T(8,128)}, f32[24,768]{1,0:T(8,128)S(1)}, u32[]{:S(2)}, u32[]{:S(2)}) collective-permute-start(f32[24,768]{1,0:T(8,128)} %get-tuple-element.22), channel_id=1, source_target_pairs={{0,1},{1,2},{2,3},{3,4},{4,5},{5,6},{6,7},{7,8},{8,9},{9,10},{10,1... | collective-permute-start | bytes 221192 | tf_op jit(solution)/shard_map/ppermute | solution.py:396
  60.2 33.5 %collective-permute-start.1 = (f32[24,768]{1,0:T(8,128)}, f32[24,768]{1,0:T(8,128)S(1)}, u32[]{:S(2)}, u32[]{:S(2)}) collective-permute-start(f32[24,768]{1,0:T(8,128)} %get-tuple-element.23), channel_id=1, source_target_pairs={{1,0},{2,1},{3,2},{4,3},{5,4},{6,5},{7,6},{8,7},{9,8},{10,9},{11,1... | collective-permute-start | bytes 221192 | tf_op jit(solution)/shard_map/ppermute | solution.py:396
  91.8 11.6 %collective-permute-start.4 = (f32[24,768]{1,0:T(8,128)}, f32[24,768]{1,0:T(8,128)S(1)}, u32[]{:S(2)}, u32[]{:S(2)}) collective-permute-start(f32[24,768]{1,0:T(8,128)} %get-tuple-element.31), channel_id=1, source_target_pairs={{0,1},{1,2},{2,3},{3,4},{4,5},{5,6},{6,7},{7,8},{8,9},{9,10},{10,1... | collective-permute-start | bytes 221192 | tf_op jit(solution)/shard_map/ppermute | solution.py:396
  91.9 11.6 %collective-permute-start.5 = (f32[24,768]{1,0:T(8,128)}, f32[24,768]{1,0:T(8,128)S(1)}, u32[]{:S(2)}, u32[]{:S(2)}) collective-permute-start(f32[24,768]{1,0:T(8,128)} %get-tuple-element.28), channel_id=1, source_target_pairs={{1,0},{2,1},{3,2},{4,3},{5,4},{6,5},{7,6},{8,7},{9,8},{10,9},{11,1... | collective-permute-start | bytes 221192 | tf_op jit(solution)/shard_map/ppermute | solution.py:396
  93.6 0.6 copy-start.2
  93.7 0.7 copy-start.3
  95.9 34.4 %collective-permute-start.2 = (f32[168,768]{1,0:T(8,128)}, f32[168,768]{1,0:T(8,128)S(1)}, u32[]{:S(2)}, u32[]{:S(2)}) collective-permute-start(f32[168,768]{1,0:T(8,128)} %get-tuple-element.29), channel_id=1, source_target_pairs={{0,16},{16,32},{32,48},{48,64},{64,80},{80,96},{96,112},{1,17},{17... | collective-permute-start | bytes 1548296 | tf_op jit(solution)/shard_map/ppermute | solution.py:396
  101.4 29.0 %collective-permute-start.3 = (f32[168,768]{1,0:T(8,128)}, f32[168,768]{1,0:T(8,128)S(1)}, u32[]{:S(2)}, u32[]{:S(2)}) collective-permute-start(f32[168,768]{1,0:T(8,128)} %get-tuple-element.30), channel_id=1, source_target_pairs={{16,0},{32,16},{48,32},{64,48},{80,64},{96,80},{112,96},{17,1},{33... | collective-permute-start | bytes 1548296 | tf_op jit(solution)/shard_map/ppermute | solution.py:396
  103.5 0.6 copy-start.4
  103.5 0.6 copy-start.5
  124.5 38.2 %all-to-all-start.3 = ((f32[16,48,768]{2,1,0:T(8,128)}), f32[16,48,768]{2,1,0:T(8,128)}, u32[]{:S(2)}, u32[]{:S(2)}) async-start(f32[16,48,768]{2,1,0:T(8,128)} %potential.3), calls=%async_computation.3 | async-start | bytes 4718592 | tf_op jit(solution)/shard_map/all_to_all | solution.py:741
  130.4 0.8 copy-start
  131.2 0.8 copy-start.1
  162.7 36.4 %all-to-all-start.2 = ((f32[16,48,768]{2,1,0:T(8,128)}), f32[16,48,768]{2,1,0:T(8,128)}, u32[]{:S(2)}, u32[]{:S(2)}) async-start(f32[16,48,768]{2,1,0:T(8,128)} %potential.2), calls=%async_computation.2 | async-start | bytes 4718592 | tf_op jit(solution)/shard_map/all_to_all | solution.py:741

commit v5 on v4

--- a/solution.py
+++ b/solution.py
@@ -23,6 +23,7 @@
 bf16 = jnp.bfloat16
 reach = 3
 gather_tile = 16
+edge_rows = -(-2 * reach * reach // 8) * 8
 lead = 9
 
 
@@ -31,7 +32,7 @@
 
 def call(body, out, cost, **options):
     estimate = pl.CostEstimate(flops=int(cost * 1e9), bytes_accessed=1 << 20, transcendentals=0)
-    limit = pltpu.CompilerParams(vmem_limit_bytes=62 << 20)
+    limit = pltpu.CompilerParams(vmem_limit_bytes=63 << 20)
     return pl.pallas_call(body, out_shape=out, compiler_params=limit, cost_estimate=estimate, **options)
 
 
@@ -179,14 +180,14 @@
         else:
             odd_re, odd_im = real[:, :half] - real[:, half:], imag[:, :half] - imag[:, half:]
             values = odd_re * wave_cos - odd_im * wave_sin, odd_re * wave_sin + odd_im * wave_cos
-        for c in range(2):
-            high, low = split(values[c].T)
-            cos_at = slice(c * lanes, (c + 1) * lanes)
-            sin_at = slice((1 - c) * lanes, (2 - c) * lanes)
-            for k, value in enumerate((high, high, low)):
-                wide_ref[p, k * half : (k + 1) * half, cos_at] = value
-                turned = value if c == 0 else -value
-                wide_ref[p, (k + 3) * half : (k + 4) * half, sin_at] = turned
+        (high, low), (high_im, low_im) = [split(value.T) for value in values]
+        cos_high, cos_low = [jnp.concatenate(pair, axis=1) for pair in ((high, high_im), (low, low_im))]
+        sin_high, sin_low = [
+            jnp.concatenate(pair, axis=1) for pair in ((-high_im, high), (-low_im, low))
+        ]
+        stacked = (cos_high, cos_high, cos_low, sin_high, sin_high, sin_low)
+        for k, value in enumerate(stacked):
+            wide_ref[p, k * half : (k + 1) * half] = value
     parts, _, block, _ = stage_ref.shape
     out_lanes = 2 * lanes
     group = parts // 2
@@ -397,7 +398,7 @@
 
 
 def slab_rows(rows):
-    return reach * rows + -(-2 * reach * reach // 8) * 8
+    return reach * rows + edge_rows
 
 
 def halo_body(head_ref, tail_ref, low_ref, high_ref, down_ref, up_ref, edge_ref, sems):
@@ -415,7 +416,6 @@
 
 def halo_slabs(low, high, head, tail):
     total, width = low.shape
-    count = -(-2 * reach * reach // 8) * 8
     return call(
         halo_body,
         [array(total, width)] * 2,
@@ -423,7 +423,7 @@
         grid=(1,),
         in_specs=[whole(head.shape), whole(tail.shape), in_hbm, in_hbm],
         out_specs=[in_hbm] * 2,
-        scratch_shapes=[pltpu.VMEM((2, count, width), f32), pltpu.SemaphoreType.DMA((2, 1))],
+        scratch_shapes=[pltpu.VMEM((2, edge_rows, width), f32), pltpu.SemaphoreType.DMA((2, 1))],
         input_output_aliases={2: 0, 3: 1},
         name="halo_slabs",
     )(head, tail, low, high)
@@ -648,7 +648,10 @@
         pltpu.SemaphoreType.DMA((2, parts // 2)),
         pltpu.SemaphoreType.DMA((len(sides),)),
     ]
-    scratch += [pltpu.VMEM((min(side.shape[0], sides[0].shape[0]), width), f32) for side in sides]
+    scratch += [
+        pltpu.VMEM((min(side.shape[0], edge_rows if i >= 4 else 1 << 20), width), f32)
+        for i, side in enumerate(sides)
+    ]
     for margin in (6, 4, 4, 2, 2, 2, 2):
         scratch.append(pltpu.VMEM((count + margin * groups, tall, width), f32))
     return call(
@@ -753,8 +756,8 @@
     factors = phase_factors(width, block, width)
     half_factors = phase_factors(width // 2, block, width)
 
-    outer = exchange(inverse_rows(rho_hat, half_factors, None, None, (0, 3)))
-    inner, tables = inverse_rows(rho_hat, half_factors, factors, flags, (1, 2))
+    outer = exchange(inverse_rows(rho_hat, half_factors, None, None, (0, 2, 3)))
+    inner, tables = inverse_rows(rho_hat, half_factors, factors, flags, (1,))
     inner = exchange(inner)
     outer, head, tail, low_planes, high_planes = inverse_columns(outer, factors, True)
     outer_sides = shift(tail, "py", True, True), shift(head, "py", False, True)
@@ -766,11 +769,11 @@
     below, above = shift(up, "px", True, False), shift(down, "px", False, False)
 
     def source(z):
-        if unit <= z < depth - unit:
+        if unit <= z < 2 * unit:
             row = reach * (z - unit)
             return 1, z - unit, 2, row, 3, row
         if 0 <= z < depth:
-            at = z if z < unit else z - depth + 2 * unit
+            at = z if z < unit else z - unit
             return 0, at, 0, reach * at, 1, reach * at
         at = z + reach if z < 0 else z - depth
         side = 2 if z < 0 else 3

time: 214 us -> 217 us (1.014)
  starting transfers between devices: 32 us -> 35.1 us
  Pallas kernels: 107 us -> 110 us
  waiting for transfers between devices: 68.3 us -> 66.1 us
    pallas_call x1, Pallas kernels: 7.1 us -> 10.9 us  [inverse_rows(): call(body, array(*out), 10.0, grid=(1,), in_specs=[in_hbm] * 3, out_specs...]
    all_to_all x4, starting transfers between devices: 20.8 us -> 23.8 us  [exchange(): return lax.all_to_all(value, 'py', 0, 0, tiled=True)]
    all_to_all x4, waiting for transfers between devices: 68.3 us -> 66.1 us  [exchange(): return lax.all_to_all(value, 'py', 0, 0, tiled=True)]
  transfers between devices with their start and end apart: 10 -> 10, of which waited for: 4 -> 4; matrix products, arithmetic and copies ran while one was open for 0% -> 0% of each run, Pallas kernels for 42% -> 41%
where the time goes in v5:
time: 217 us; the launch traced here: 215 us
  Pallas kernels  110 us (51%)
  waiting for transfers between devices  66.1 us (30%)
  starting transfers between devices  35.1 us (16%)
    all_to_all x4, waiting for transfers between devices, exchange(): return lax.all_to_all(value, 'py', 0, 0, tiled=True)  66.1 us
    pallas_call x2, Pallas kernels, potential_of(): call(lambda *refs: potential_body(sources, groups, *refs), array(*out), 2...  44 us
    pallas_call x2, Pallas kernels, forward_rows(): call(lambda *refs: forward_rows_body(starts, *refs), array(2, depth, rows...  24.3 us
    all_to_all x4, starting transfers between devices, exchange(): return lax.all_to_all(value, 'py', 0, 0, tiled=True)  23.8 us
    pallas_call x2, Pallas kernels, inverse_columns(): call(lambda *refs: inverse_columns_body(sends, *refs), [array(planes, row...  20.1 us
    ppermute x6, starting transfers between devices, shift(): lax.ppermute(value, axis, pairs if up else [(b, a) for a, b in pairs])  11.3 us
    pallas_call x1, Pallas kernels, inverse_rows(): call(body, array(*out), 10.0, grid=(1,), in_specs=[in_hbm] * 3, out_specs...  10.9 us
    pallas_call x1, Pallas kernels, inverse_rows(): call(body, [array(*out), jax.ShapeDtypeStruct((4, width, width), bf16)],...  9.55 us
  transfers between devices with their start and end apart: 10, of which 4 were waited for; matrix products, arithmetic and copies ran while one was open for 0% of the time, Pallas kernels for 41%

profile of v5, /device:TPU:14, one launch (start us, length us, event | category | flops | bytes accessed | tf_op | source)
XLA Modules:
  0.0 214.7 jit_solution(6652483433634354281)
XLA Ops:
  0.0 10.9 %inverse_rows.2 = f32[16,9,48,128]{3,2,1,0:T(8,128)} custom-call(f32[2,16,48,768]{3,2,1,0:T(8,128)} %refs_0_.3, f32[2,3,384]{2,1,0:T(4,128)} %constant.23.clone.refs_1_, f32[2,48,384]{2,1,0:T(8,128)} %constant.24.clone.refs_2_), custom_call_target="tpu_custom_call" | custom-call | flops 10000000000 | bytes 1048576 | tf_op jit(solution)/shard_map/inverse_rows/pallas_call | solution.py:248
  10.9 6.3 %all-to-all-start = ((f32[16,9,48,128]{3,2,1,0:T(8,128)}), f32[16,9,48,128]{3,2,1,0:T(8,128)}, u32[]{:S(2)}, u32[]{:S(2)}) async-start(f32[16,9,48,128]{3,2,1,0:T(8,128)} %inverse_rows.2), calls=%async_computation | async-start | bytes 7077888 | tf_op jit(solution)/shard_map/all_to_all | solution.py:744
  17.8 9.6 %inverse_rows.3 = (f32[16,3,48,128]{3,2,1,0:T(8,128)}, bf16[4,768,768]{2,1,0:T(8,128)(2,1)}) custom-call(f32[2,16,48,768]{3,2,1,0:T(8,128)} %refs_0_.3, f32[2,3,384]{2,1,0:T(4,128)} %constant.23.clone.refs_1_, f32[2,48,384]{2,1,0:T(8,128)} %constant.24.clone.refs_2_, f32[2,5,768]{2,1,0:T(8,128)} %constant.21.clone.refs_1_.refs_3_.refs_2_, ...), custom_call_target="tpu_custom_call" | custom-call | flops 10000000000 | bytes 1048576 | tf_op jit(solution)/shard_map/inverse_rows/pallas_call | solution.py:238
  27.3 38.0 %all-to-all-done.refs_0_ = f32[16,9,48,128]{3,2,1,0:T(8,128)} async-done(((f32[16,9,48,128]{3,2,1,0:T(8,128)}), f32[16,9,48,128]{3,2,1,0:T(8,128)}, u32[]{:S(2)}, u32[]{:S(2)}) %all-to-all-start) | async-done | bytes 3538976 | tf_op jit(solution)/shard_map/all_to_all | solution.py:744
  65.3 4.3 %all-to-all-start.1 = ((f32[16,3,48,128]{3,2,1,0:T(8,128)}), f32[16,3,48,128]{3,2,1,0:T(8,128)}, u32[]{:S(2)}, u32[]{:S(2)}) async-start(f32[16,3,48,128]{3,2,1,0:T(8,128)} %get-tuple-element.20), calls=%async_computation.1 | async-start | bytes 2359296 | tf_op jit(solution)/shard_map/all_to_all | solution.py:744
  69.6 12.6 %inverse_columns.2 = (f32[12,48,768]{2,1,0:T(8,128)}, f32[36,768]{1,0:T(8,128)}, f32[36,768]{1,0:T(8,128)}, f32[168,768]{1,0:T(8,128)}, f32[168,768]{1,0:T(8,128)}) custom-call(f32[16,9,48,128]{3,2,1,0:T(8,128)} %all-to-all-done.refs_0_, f32[2,5,768]{2,1,0:T(8,128)} %constant.21.clone.refs_1_.refs_3_.refs_2_, ...), custom_call_target="tpu_custom_call" | custom-call | flops 7000000000 | bytes 1048576 | tf_op jit(solution)/shard_map/inverse_columns/pallas_call | solution.py:381
  82.3 1.7 collective-permute-start.1
  84.1 0.8 all-to-all-done.1.refs_0_
  84.8 7.4 %inverse_columns.3 = (f32[4,48,768]{2,1,0:T(8,128)}, f32[12,768]{1,0:T(8,128)}, f32[12,768]{1,0:T(8,128)}) custom-call(f32[16,3,48,128]{3,2,1,0:T(8,128)} %all-to-all-done.1.refs_0_, f32[2,5,768]{2,1,0:T(8,128)} %constant.21.clone.refs_1_.refs_3_.refs_2_, f32[2,48,768]{2,1,0:T(8,128)} %constant.22.clone.refs_2_.refs_4_.refs_3_), custom_call_target="tpu_custom_call" | custom-call | flops 7000000000 | bytes 1048576 | tf_op jit(solution)/shard_map/inverse_columns/pallas_call | solution.py:381
  92.4 2.0 collective-permute-start.5
  94.5 0.6 copy-done.1
  95.2 1.7 halo_slabs.1
  96.9 5.4 %collective-permute-start.2 = (f32[168,768]{1,0:T(8,128)}, f32[168,768]{1,0:T(8,128)S(1)}, u32[]{:S(2)}, u32[]{:S(2)}) collective-permute-start(f32[168,768]{1,0:T(8,128)} %get-tuple-element.29), channel_id=1, source_target_pairs={{0,16},{16,32},{32,48},{48,64},{64,80},{80,96},{96,112},{1,17},{17... | collective-permute-start | bytes 1548296 | tf_op jit(solution)/shard_map/ppermute | solution.py:397
  102.3 1.9 collective-permute-start.3
  104.2 0.6 copy-done.3
  104.9 20.3 %potential.3 = f32[16,48,768]{2,1,0:T(8,128)} custom-call(s32[3]{0:T(128)} %add_convert_fusion.refs_5_.refs_0_, f32[12,48,768]{2,1,0:T(8,128)} %get-tuple-element.19.refs_1_, f32[4,48,768]{2,1,0:T(8,128)} %get-tuple-element.21.refs_2_, f32[36,768]{1,0:T(8,128)} %copy-done.1, f32[36,768]{1,0:T(8,128)} %copy-done.2, f32[12,768]{1,0:T(8,128)} %copy-done.3, ...), custom_call_target="tpu_custom_call" | custom-call | flops 20000000000 | bytes 1048576 | tf_op jit(solution)/shard_map/potential/pallas_call | solution.py:657
  125.2 8.6 %all-to-all-start.3 = ((f32[16,48,768]{2,1,0:T(8,128)}), f32[16,48,768]{2,1,0:T(8,128)}, u32[]{:S(2)}, u32[]{:S(2)}) async-start(f32[16,48,768]{2,1,0:T(8,128)} %potential.3), calls=%async_computation.3 | async-start | bytes 4718592 | tf_op jit(solution)/shard_map/all_to_all | solution.py:744
  133.8 0.8 copy-done
  134.6 23.7 %potential.2 = f32[16,48,768]{2,1,0:T(8,128)} custom-call(s32[3]{0:T(128)} %add_convert_fusion.refs_5_.refs_0_, f32[12,48,768]{2,1,0:T(8,128)} %get-tuple-element.19.refs_1_, f32[4,48,768]{2,1,0:T(8,128)} %get-tuple-element.21.refs_2_, f32[168,768]{1,0:T(8,128)} %copy-done, f32[168,768]{1,0:T(8,128)} %collective-permute-done.3.refs_4_.refs_10_, ...), custom_call_target="tpu_custom_call" | custom-call | flops 20000000000 | bytes 1048576 | tf_op jit(solution)/shard_map/potential/pallas_call | solution.py:657
  158.3 7.8 %all-to-all-done.3.refs_1_ = f32[16,48,768]{2,1,0:T(8,128)} async-done(((f32[16,48,768]{2,1,0:T(8,128)}), f32[16,48,768]{2,1,0:T(8,128)}, u32[]{:S(2)}, u32[]{:S(2)}) %all-to-all-start.3) | async-done | bytes 2359328 | tf_op jit(solution)/shard_map/all_to_all | solution.py:744
  166.1 4.6 %all-to-all-start.2 = ((f32[16,48,768]{2,1,0:T(8,128)}), f32[16,48,768]{2,1,0:T(8,128)}, u32[]{:S(2)}, u32[]{:S(2)}) async-start(f32[16,48,768]{2,1,0:T(8,128)} %potential.2), calls=%async_computation.2 | async-start | bytes 4718592 | tf_op jit(solution)/shard_map/all_to_all | solution.py:744
  170.7 12.2 %forward_rows.2.refs_4_ = f32[2,16,48,768]{3,2,1,0:T(8,128)} custom-call(s32[3]{0:T(128)} %add_convert_fusion.refs_5_.refs_0_, f32[16,48,768]{2,1,0:T(8,128)} %all-to-all-done.3.refs_1_, f32[2,5,768]{2,1,0:T(8,128)} %constant.21.clone.refs_1_.refs_3_.refs_2_, f32[2,48,768]{2,1,0:T(8,128)} %constant.22.clone.refs_2_.refs_4_.refs_3_), custom_call_target="tpu_custom_call" | custom-call | flops 10000000000 | bytes 1048576 | tf_op jit(solution)/shard_map/forward_rows/pallas_call | solution.py:730
  182.9 19.5 %all-to-all-done.2.refs_1_ = f32[16,48,768]{2,1,0:T(8,128)} async-done(((f32[16,48,768]{2,1,0:T(8,128)}), f32[16,48,768]{2,1,0:T(8,128)}, u32[]{:S(2)}, u32[]{:S(2)}) %all-to-all-start.2) | async-done | bytes 2359328 | tf_op jit(solution)/shard_map/all_to_all | solution.py:744
  202.4 12.2 %forward_rows.3 = f32[2,16,48,768]{3,2,1,0:T(8,128)} custom-call(s32[3]{0:T(128)} %add_convert_fusion.refs_5_.refs_0_, f32[16,48,768]{2,1,0:T(8,128)} %all-to-all-done.2.refs_1_, f32[2,5,768]{2,1,0:T(8,128)} %constant.21.clone.refs_1_.refs_3_.refs_2_, f32[2,48,768]{2,1,0:T(8,128)} %constant.22.clone.refs_2_.refs_4_.refs_3_, ...), custom_call_target="tpu_custom_call", output_to_operand_aliasing={{}: (4, {})} | custom-call | flops 10000000000 | bytes 1048576 | tf_op jit(solution)/shard_map/forward_rows/pallas_call | solution.py:730
  (16 shorter events, 0.9 us)
Async XLA Ops:
  10.9 54.4 %all-to-all-start = ((f32[16,9,48,128]{3,2,1,0:T(8,128)}), f32[16,9,48,128]{3,2,1,0:T(8,128)}, u32[]{:S(2)}, u32[]{:S(2)}) async-start(f32[16,9,48,128]{3,2,1,0:T(8,128)} %inverse_rows.2), calls=%async_computation | async-start | bytes 7077888 | tf_op jit(solution)/shard_map/all_to_all | solution.py:744
  65.3 19.5 %all-to-all-start.1 = ((f32[16,3,48,128]{3,2,1,0:T(8,128)}), f32[16,3,48,128]{3,2,1,0:T(8,128)}, u32[]{:S(2)}, u32[]{:S(2)}) async-start(f32[16,3,48,128]{3,2,1,0:T(8,128)} %get-tuple-element.20), calls=%async_computation.1 | async-start | bytes 2359296 | tf_op jit(solution)/shard_map/all_to_all | solution.py:744
  82.3 12.2 %collective-permute-start = (f32[36,768]{1,0:T(8,128)}, f32[36,768]{1,0:T(8,128)S(1)}, u32[]{:S(2)}, u32[]{:S(2)}) collective-permute-start(f32[36,768]{1,0:T(8,128)} %get-tuple-element.22), channel_id=1, source_target_pairs={{0,1},{1,2},{2,3},{3,4},{4,5},{5,6},{6,7},{7,8},{8,9},{9,10},{10,1... | collective-permute-start | bytes 331784 | tf_op jit(solution)/shard_map/ppermute | solution.py:397
  82.3 12.1 %collective-permute-start.1 = (f32[36,768]{1,0:T(8,128)}, f32[36,768]{1,0:T(8,128)S(1)}, u32[]{:S(2)}, u32[]{:S(2)}) collective-permute-start(f32[36,768]{1,0:T(8,128)} %get-tuple-element.23), channel_id=1, source_target_pairs={{1,0},{2,1},{3,2},{4,3},{5,4},{6,5},{7,6},{8,7},{9,8},{10,9},{11,1... | collective-permute-start | bytes 331784 | tf_op jit(solution)/shard_map/ppermute | solution.py:397
  92.3 11.9 %collective-permute-start.4 = (f32[12,768]{1,0:T(8,128)}, f32[12,768]{1,0:T(8,128)S(1)}, u32[]{:S(2)}, u32[]{:S(2)}) collective-permute-start(f32[12,768]{1,0:T(8,128)} %get-tuple-element.31), channel_id=1, source_target_pairs={{0,1},{1,2},{2,3},{3,4},{4,5},{5,6},{6,7},{7,8},{8,9},{9,10},{10,1... | collective-permute-start | bytes 110600 | tf_op jit(solution)/shard_map/ppermute | solution.py:397
  92.4 11.8 %collective-permute-start.5 = (f32[12,768]{1,0:T(8,128)}, f32[12,768]{1,0:T(8,128)S(1)}, u32[]{:S(2)}, u32[]{:S(2)}) collective-permute-start(f32[12,768]{1,0:T(8,128)} %get-tuple-element.28), channel_id=1, source_target_pairs={{1,0},{2,1},{3,2},{4,3},{5,4},{6,5},{7,6},{8,7},{9,8},{10,9},{11,1... | collective-permute-start | bytes 110600 | tf_op jit(solution)/shard_map/ppermute | solution.py:397
  94.5 0.7 copy-start.1
  94.5 0.7 copy-start.2
  96.9 36.9 %collective-permute-start.2 = (f32[168,768]{1,0:T(8,128)}, f32[168,768]{1,0:T(8,128)S(1)}, u32[]{:S(2)}, u32[]{:S(2)}) collective-permute-start(f32[168,768]{1,0:T(8,128)} %get-tuple-element.29), channel_id=1, source_target_pairs={{0,16},{16,32},{32,48},{48,64},{64,80},{80,96},{96,112},{1,17},{17... | collective-permute-start | bytes 1548296 | tf_op jit(solution)/shard_map/ppermute | solution.py:397
  102.3 31.5 %collective-permute-start.3 = (f32[168,768]{1,0:T(8,128)}, f32[168,768]{1,0:T(8,128)}, u32[]{:S(2)}, u32[]{:S(2)}) collective-permute-start(f32[168,768]{1,0:T(8,128)} %get-tuple-element.30), channel_id=1, source_target_pairs={{16,0},{32,16},{48,32},{64,48},{80,64},{96,80},{112,96},{17,1},{33... | collective-permute-start | bytes 1548296 | tf_op jit(solution)/shard_map/ppermute | solution.py:397
  104.2 0.6 copy-start.3
  104.2 0.6 copy-start.4
  125.2 40.9 %all-to-all-start.3 = ((f32[16,48,768]{2,1,0:T(8,128)}), f32[16,48,768]{2,1,0:T(8,128)}, u32[]{:S(2)}, u32[]{:S(2)}) async-start(f32[16,48,768]{2,1,0:T(8,128)} %potential.3), calls=%async_computation.3 | async-start | bytes 4718592 | tf_op jit(solution)/shard_map/all_to_all | solution.py:744
  133.8 0.8 copy-start
  166.1 36.3 %all-to-all-start.2 = ((f32[16,48,768]{2,1,0:T(8,128)}), f32[16,48,768]{2,1,0:T(8,128)}, u32[]{:S(2)}, u32[]{:S(2)}) async-start(f32[16,48,768]{2,1,0:T(8,128)} %potential.2), calls=%async_computation.2 | async-start | bytes 4718592 | tf_op jit(solution)/shard_map/all_to_all | solution.py:744

commit v6 on v4

--- a/solution.py
+++ b/solution.py
@@ -93,8 +93,7 @@
     return dot(left_high, right_high) + (dot(left_low, right_high) + dot(left_high, right_low))
 
 
-def fill_tables(hbm_refs, coarse_ref, fine_ref, tab_ref, sems):
-    arriving = copy_all(list(zip(hbm_refs, (coarse_ref, fine_ref))), sems)
+def fill_tables(arriving, coarse_ref, fine_ref, tab_ref):
     wait_all(arriving)
     stride = fine_ref.shape[1]
 
@@ -157,6 +156,7 @@
     half = tab_ref.shape[1]
     lanes = wide_ref.shape[2] // 2
     unit = x_ref.shape[1] // len(blocks)
+    small = copy_all([(coarse_hbm_ref, coarse_ref), (fine_hbm_ref, fine_ref)], factor_sems)
     arriving = [
         copy_all(
             [
@@ -167,7 +167,7 @@
         )
         for c in range(2)
     ]
-    fill_tables((coarse_hbm_ref, fine_hbm_ref), coarse_ref, fine_ref, tab_ref, factor_sems)
+    fill_tables(small, coarse_ref, fine_ref, tab_ref)
     for c in range(2):
         wait_all(arriving[c])
     real, imag = [x_ref[c].reshape(lanes, 2 * half) for c in range(2)]
@@ -207,7 +207,9 @@
 
     lax.fori_loop(0, 2, step, 0)
     if makes:
-        fill_tables(factors_hbm, full_coarse_ref, full_fine_ref, full_ref, full_factor_sems)
+        pairs = zip(factors_hbm, (full_coarse_ref, full_fine_ref))
+        small = copy_all(list(pairs), full_factor_sems)
+        fill_tables(small, full_coarse_ref, full_fine_ref, full_ref)
         wait_all(copy_all([(full_ref.at[i], tab_out_ref.at[i]) for i in range(4)], full_sems))
     for m in range(2):
         wait_all(group_copies(stage_ref, out_ref, out_sems, m, group))
@@ -320,13 +322,14 @@
 
 
 def inverse_columns_body(sends, blocks_ref, coarse_hbm_ref, fine_hbm_ref, *refs):
-    coarse_ref, fine_ref, factor_sems = refs[-3:]
-    refs = refs[:-3]
+    edge_ref, edge_sems, coarse_ref, fine_ref, factor_sems = refs[-5:]
+    refs = refs[:-5]
     out_ref, head_ref, tail_ref = refs[:3]
     tab_ref, in_ref, stage_ref, high_ref, low_ref, in_sems, out_sems, send_sems = refs[-8:]
     planes, rows, width = stage_ref.shape
+    small = copy_all([(coarse_hbm_ref, coarse_ref), (fine_hbm_ref, fine_ref)], factor_sems)
     fetch_blocks(blocks_ref, in_ref, in_sems)
-    fill_tables((coarse_hbm_ref, fine_hbm_ref), coarse_ref, fine_ref, tab_ref, factor_sems)
+    fill_tables(small, coarse_ref, fine_ref, tab_ref)
     gather_blocks(blocks_ref, in_ref, in_sems, high_ref, low_ref)
     half = planes // 2
 
@@ -355,8 +358,9 @@
         leaving += copy_all(pairs, send_sems.at[m])
     for z in range(planes):
         at = slice(reach * z, reach * (z + 1))
-        head_ref[at] = stage_ref[z, :reach]
-        tail_ref[at] = stage_ref[z, rows - reach :]
+        edge_ref[0, at] = stage_ref[z, :reach]
+        edge_ref[1, at] = stage_ref[z, rows - reach :]
+    leaving += copy_all([(edge_ref.at[0], head_ref), (edge_ref.at[1], tail_ref)], edge_sems)
     wait_all(leaving)
 
 
@@ -377,6 +381,7 @@
         pltpu.SemaphoreType.DMA((planes,)),
         pltpu.SemaphoreType.DMA((2, reach)),
     ]
+    edges = [pltpu.VMEM((2, *side), f32), pltpu.SemaphoreType.DMA((2,))]
     return call(
         lambda *refs: inverse_columns_body(sends, *refs),
         [array(planes, rows, width), array(*side), array(*side)]
@@ -384,8 +389,8 @@
         7.0,
         grid=(1,),
         in_specs=[in_hbm] * 3,
-        out_specs=[in_hbm, whole(side), whole(side)] + [in_hbm] * slabs,
-        scratch_shapes=scratch + factor_scratch(factors),
+        out_specs=[in_hbm] * (3 + slabs),
+        scratch_shapes=scratch + edges + factor_scratch(factors),
         name="inverse_columns",
     )(blocks, *factors)
 
@@ -670,8 +675,9 @@
     coarse_ref, fine_ref, factor_sems = refs[-3:]
     out_ref, tab_ref, in_ref, stage_ref, high_ref, low_ref, in_sems, out_sems = refs[-11:-3]
     _, planes, rows, width = stage_ref.shape
+    small = copy_all([(coarse_hbm_ref, coarse_ref), (fine_hbm_ref, fine_ref)], factor_sems)
     fetch_blocks(blocks_ref, in_ref, in_sems)
-    fill_tables((coarse_hbm_ref, fine_hbm_ref), coarse_ref, fine_ref, tab_ref, factor_sems)
+    fill_tables(small, coarse_ref, fine_ref, tab_ref)
     gather_blocks(blocks_ref, in_ref, in_sems, high_ref, low_ref)
     high_ref[2], low_ref[2] = -high_ref[0], -low_ref[0]
 

time: 214 us -> 213 us (level)
  transfers between devices with their start and end apart: 10 -> 10, of which waited for: 4 -> 4; matrix products, arithmetic and copies ran while one was open for 0% -> 0% of each run, Pallas kernels for 42% -> 41%
where the time goes in v6:
time: 213 us; the launch traced here: 211 us
  Pallas kernels  106 us (50%)
  waiting for transfers between devices  69.1 us (32%)
  starting transfers between devices  32 us (15%)
  local copies, waits for them, and re-layouts  2.91 us (1%)
    all_to_all x4, waiting for transfers between devices, exchange(): return lax.all_to_all(value, 'py', 0, 0, tiled=True)  69.1 us
    pallas_call x2, Pallas kernels, potential_of(): call(lambda *refs: potential_body(sources, groups, *refs), array(*out), 2...  44 us
    pallas_call x2, Pallas kernels, forward_rows(): call(lambda *refs: forward_rows_body(starts, *refs), array(2, depth, rows...  24.2 us
    all_to_all x4, starting transfers between devices, exchange(): return lax.all_to_all(value, 'py', 0, 0, tiled=True)  20.8 us
    pallas_call x2, Pallas kernels, inverse_columns(): call(lambda *refs: inverse_columns_body(sends, *refs), [array(planes, row...  18.1 us
    ppermute x6, starting transfers between devices, shift(): lax.ppermute(value, axis, pairs if up else [(b, a) for a, b in pairs])  11.1 us
    pallas_call x1, Pallas kernels, inverse_rows(): call(body, [array(*out), jax.ShapeDtypeStruct((4, width, width), bf16)],...  10.7 us
    pallas_call x1, Pallas kernels, inverse_rows(): call(body, array(*out), 10.0, grid=(1,), in_specs=[in_hbm] * 3, out_specs...  6.92 us
  transfers between devices with their start and end apart: 10, of which 4 were waited for; matrix products, arithmetic and copies ran while one was open for 0% of the time, Pallas kernels for 41%

profile of v6, /device:TPU:14, one launch (start us, length us, event | category | flops | bytes accessed | tf_op | source)
XLA Modules:
  0.0 210.6 jit_solution(15215422972049718553)
XLA Ops:
  0.0 6.9 %inverse_rows.2 = f32[16,6,48,128]{3,2,1,0:T(8,128)} custom-call(f32[2,16,48,768]{3,2,1,0:T(8,128)} %refs_0_.3, f32[2,3,384]{2,1,0:T(4,128)} %constant.23.clone.refs_1_, f32[2,48,384]{2,1,0:T(8,128)} %constant.24.clone.refs_2_), custom_call_target="tpu_custom_call" | custom-call | flops 10000000000 | bytes 1048576 | tf_op jit(solution)/shard_map/inverse_rows/pallas_call | solution.py:249
  6.9 6.3 %all-to-all-start = ((f32[16,6,48,128]{3,2,1,0:T(8,128)}), f32[16,6,48,128]{3,2,1,0:T(8,128)}, u32[]{:S(2)}, u32[]{:S(2)}) async-start(f32[16,6,48,128]{3,2,1,0:T(8,128)} %inverse_rows.2), calls=%async_computation | async-start | bytes 4718592 | tf_op jit(solution)/shard_map/all_to_all | solution.py:747
  13.8 10.7 %inverse_rows.3 = (f32[16,6,48,128]{3,2,1,0:T(8,128)}, bf16[4,768,768]{2,1,0:T(8,128)(2,1)}) custom-call(f32[2,16,48,768]{3,2,1,0:T(8,128)} %refs_0_.3, f32[2,3,384]{2,1,0:T(4,128)} %constant.23.clone.refs_1_, f32[2,48,384]{2,1,0:T(8,128)} %constant.24.clone.refs_2_, f32[2,5,768]{2,1,0:T(8,128)} %constant.21.clone.refs_1_.refs_3_.refs_2_, ...), custom_call_target="tpu_custom_call" | custom-call | flops 10000000000 | bytes 1048576 | tf_op jit(solution)/shard_map/inverse_rows/pallas_call | solution.py:239
  24.5 21.1 %all-to-all-done.refs_0_ = f32[16,6,48,128]{3,2,1,0:T(8,128)} async-done(((f32[16,6,48,128]{3,2,1,0:T(8,128)}), f32[16,6,48,128]{3,2,1,0:T(8,128)}, u32[]{:S(2)}, u32[]{:S(2)}) %all-to-all-start) | async-done | bytes 2359328 | tf_op jit(solution)/shard_map/all_to_all | solution.py:747
  45.6 4.3 %all-to-all-start.1 = ((f32[16,6,48,128]{3,2,1,0:T(8,128)}), f32[16,6,48,128]{3,2,1,0:T(8,128)}, u32[]{:S(2)}, u32[]{:S(2)}) async-start(f32[16,6,48,128]{3,2,1,0:T(8,128)} %get-tuple-element.20), calls=%async_computation.1 | async-start | bytes 4718592 | tf_op jit(solution)/shard_map/all_to_all | solution.py:747
  50.0 9.3 %inverse_columns.2 = (f32[8,48,768]{2,1,0:T(8,128)}, f32[24,768]{1,0:T(8,128)}, f32[24,768]{1,0:T(8,128)}, f32[168,768]{1,0:T(8,128)}, f32[168,768]{1,0:T(8,128)}) custom-call(f32[16,6,48,128]{3,2,1,0:T(8,128)} %all-to-all-done.refs_0_, f32[2,5,768]{2,1,0:T(8,128)} %constant.21.clone.refs_1_.refs_3_.refs_2_, f32[2,48,768]{2,1,0:T(8,128)} %constant.22.clone.refs_2_.refs_4_.refs_3_), custom_call_target="tpu_custom_call" | custom-call | flops 7000000000 | bytes 1048576 | tf_op jit(solution)/shard_map/inverse_columns/pallas_call | solution.py:385
  59.3 1.7 collective-permute-start.1
  61.1 21.0 %all-to-all-done.1.refs_0_ = f32[16,6,48,128]{3,2,1,0:T(8,128)} async-done(((f32[16,6,48,128]{3,2,1,0:T(8,128)}), f32[16,6,48,128]{3,2,1,0:T(8,128)}, u32[]{:S(2)}, u32[]{:S(2)}) %all-to-all-start.1) | async-done | bytes 2359328 | tf_op jit(solution)/shard_map/all_to_all | solution.py:747
  82.1 8.9 %inverse_columns.3 = (f32[8,48,768]{2,1,0:T(8,128)}, f32[24,768]{1,0:T(8,128)}, f32[24,768]{1,0:T(8,128)}) custom-call(f32[16,6,48,128]{3,2,1,0:T(8,128)} %all-to-all-done.1.refs_0_, f32[2,5,768]{2,1,0:T(8,128)} %constant.21.clone.refs_1_.refs_3_.refs_2_, f32[2,48,768]{2,1,0:T(8,128)} %constant.22.clone.refs_2_.refs_4_.refs_3_), custom_call_target="tpu_custom_call" | custom-call | flops 7000000000 | bytes 1048576 | tf_op jit(solution)/shard_map/inverse_columns/pallas_call | solution.py:385
  91.1 1.7 collective-permute-start.5
  92.8 0.6 copy-done.2
  93.5 1.6 halo_slabs.1
  95.1 5.4 %collective-permute-start.2 = (f32[168,768]{1,0:T(8,128)}, f32[168,768]{1,0:T(8,128)S(1)}, u32[]{:S(2)}, u32[]{:S(2)}) collective-permute-start(f32[168,768]{1,0:T(8,128)} %get-tuple-element.29), channel_id=1, source_target_pairs={{0,16},{16,32},{32,48},{48,64},{64,80},{80,96},{96,112},{1,17},{17... | collective-permute-start | bytes 1548296 | tf_op jit(solution)/shard_map/ppermute | solution.py:401
  100.5 2.1 collective-permute-start.3
  103.3 20.4 %potential.3 = f32[16,48,768]{2,1,0:T(8,128)} custom-call(s32[3]{0:T(128)} %add_convert_fusion.refs_5_.refs_0_, f32[8,48,768]{2,1,0:T(8,128)} %get-tuple-element.19.refs_1_, f32[8,48,768]{2,1,0:T(8,128)} %get-tuple-element.21.refs_2_, f32[24,768]{1,0:T(8,128)} %copy-done.2, f32[24,768]{1,0:T(8,128)} %copy-done.3, f32[24,768]{1,0:T(8,128)} %copy-done.4, ...), custom_call_target="tpu_custom_call" | custom-call | flops 20000000000 | bytes 1048576 | tf_op jit(solution)/shard_map/potential/pallas_call | solution.py:659
  123.7 5.8 %all-to-all-start.3 = ((f32[16,48,768]{2,1,0:T(8,128)}), f32[16,48,768]{2,1,0:T(8,128)}, u32[]{:S(2)}, u32[]{:S(2)}) async-start(f32[16,48,768]{2,1,0:T(8,128)} %potential.3), calls=%async_computation.3 | async-start | bytes 4718592 | tf_op jit(solution)/shard_map/all_to_all | solution.py:747
  129.6 0.8 copy-done
  130.4 0.8 copy-done.1
  131.2 23.7 %potential.2 = f32[16,48,768]{2,1,0:T(8,128)} custom-call(s32[3]{0:T(128)} %add_convert_fusion.refs_5_.refs_0_, f32[8,48,768]{2,1,0:T(8,128)} %get-tuple-element.19.refs_1_, f32[8,48,768]{2,1,0:T(8,128)} %get-tuple-element.21.refs_2_, f32[168,768]{1,0:T(8,128)} %copy-done, f32[168,768]{1,0:T(8,128)} %copy-done.1, f32[24,768]{1,0:T(8,128)} %copy-done.2, ...), custom_call_target="tpu_custom_call" | custom-call | flops 20000000000 | bytes 1048576 | tf_op jit(solution)/shard_map/potential/pallas_call | solution.py:659
  154.9 7.0 %all-to-all-done.3.refs_1_ = f32[16,48,768]{2,1,0:T(8,128)} async-done(((f32[16,48,768]{2,1,0:T(8,128)}), f32[16,48,768]{2,1,0:T(8,128)}, u32[]{:S(2)}, u32[]{:S(2)}) %all-to-all-start.3) | async-done | bytes 2359328 | tf_op jit(solution)/shard_map/all_to_all | solution.py:747
  161.9 4.3 %all-to-all-start.2 = ((f32[16,48,768]{2,1,0:T(8,128)}), f32[16,48,768]{2,1,0:T(8,128)}, u32[]{:S(2)}, u32[]{:S(2)}) async-start(f32[16,48,768]{2,1,0:T(8,128)} %potential.2), calls=%async_computation.2 | async-start | bytes 4718592 | tf_op jit(solution)/shard_map/all_to_all | solution.py:747
  166.2 12.1 %forward_rows.2.refs_4_ = f32[2,16,48,768]{3,2,1,0:T(8,128)} custom-call(s32[3]{0:T(128)} %add_convert_fusion.refs_5_.refs_0_, f32[16,48,768]{2,1,0:T(8,128)} %all-to-all-done.3.refs_1_, f32[2,5,768]{2,1,0:T(8,128)} %constant.21.clone.refs_1_.refs_3_.refs_2_, f32[2,48,768]{2,1,0:T(8,128)} %constant.22.clone.refs_2_.refs_4_.refs_3_), custom_call_target="tpu_custom_call" | custom-call | flops 10000000000 | bytes 1048576 | tf_op jit(solution)/shard_map/forward_rows/pallas_call | solution.py:733
  178.4 19.9 %all-to-all-done.2.refs_1_ = f32[16,48,768]{2,1,0:T(8,128)} async-done(((f32[16,48,768]{2,1,0:T(8,128)}), f32[16,48,768]{2,1,0:T(8,128)}, u32[]{:S(2)}, u32[]{:S(2)}) %all-to-all-start.2) | async-done | bytes 2359328 | tf_op jit(solution)/shard_map/all_to_all | solution.py:747
  198.3 12.1 %forward_rows.3 = f32[2,16,48,768]{3,2,1,0:T(8,128)} custom-call(s32[3]{0:T(128)} %add_convert_fusion.refs_5_.refs_0_, f32[16,48,768]{2,1,0:T(8,128)} %all-to-all-done.2.refs_1_, f32[2,5,768]{2,1,0:T(8,128)} %constant.21.clone.refs_1_.refs_3_.refs_2_, f32[2,48,768]{2,1,0:T(8,128)} %constant.22.clone.refs_2_.refs_4_.refs_3_, ...), custom_call_target="tpu_custom_call", output_to_operand_aliasing={{}: (4, {})} | custom-call | flops 10000000000 | bytes 1048576 | tf_op jit(solution)/shard_map/forward_rows/pallas_call | solution.py:733
  (18 shorter events, 1.4 us)
Async XLA Ops:
  6.9 38.7 %all-to-all-start = ((f32[16,6,48,128]{3,2,1,0:T(8,128)}), f32[16,6,48,128]{3,2,1,0:T(8,128)}, u32[]{:S(2)}, u32[]{:S(2)}) async-start(f32[16,6,48,128]{3,2,1,0:T(8,128)} %inverse_rows.2), calls=%async_computation | async-start | bytes 4718592 | tf_op jit(solution)/shard_map/all_to_all | solution.py:747
  45.6 36.5 %all-to-all-start.1 = ((f32[16,6,48,128]{3,2,1,0:T(8,128)}), f32[16,6,48,128]{3,2,1,0:T(8,128)}, u32[]{:S(2)}, u32[]{:S(2)}) async-start(f32[16,6,48,128]{3,2,1,0:T(8,128)} %get-tuple-element.20), calls=%async_computation.1 | async-start | bytes 4718592 | tf_op jit(solution)/shard_map/all_to_all | solution.py:747
  59.3 33.6 %collective-permute-start = (f32[24,768]{1,0:T(8,128)}, f32[24,768]{1,0:T(8,128)S(1)}, u32[]{:S(2)}, u32[]{:S(2)}) collective-permute-start(f32[24,768]{1,0:T(8,128)} %get-tuple-element.22), channel_id=1, source_target_pairs={{0,1},{1,2},{2,3},{3,4},{4,5},{5,6},{6,7},{7,8},{8,9},{9,10},{10,1... | collective-permute-start | bytes 221192 | tf_op jit(solution)/shard_map/ppermute | solution.py:401
  59.3 33.5 %collective-permute-start.1 = (f32[24,768]{1,0:T(8,128)}, f32[24,768]{1,0:T(8,128)S(1)}, u32[]{:S(2)}, u32[]{:S(2)}) collective-permute-start(f32[24,768]{1,0:T(8,128)} %get-tuple-element.23), channel_id=1, source_target_pairs={{1,0},{2,1},{3,2},{4,3},{5,4},{6,5},{7,6},{8,7},{9,8},{10,9},{11,1... | collective-permute-start | bytes 221192 | tf_op jit(solution)/shard_map/ppermute | solution.py:401
  91.0 11.6 %collective-permute-start.4 = (f32[24,768]{1,0:T(8,128)}, f32[24,768]{1,0:T(8,128)S(1)}, u32[]{:S(2)}, u32[]{:S(2)}) collective-permute-start(f32[24,768]{1,0:T(8,128)} %get-tuple-element.31), channel_id=1, source_target_pairs={{0,1},{1,2},{2,3},{3,4},{4,5},{5,6},{6,7},{7,8},{8,9},{9,10},{10,1... | collective-permute-start | bytes 221192 | tf_op jit(solution)/shard_map/ppermute | solution.py:401
  91.1 11.6 %collective-permute-start.5 = (f32[24,768]{1,0:T(8,128)}, f32[24,768]{1,0:T(8,128)S(1)}, u32[]{:S(2)}, u32[]{:S(2)}) collective-permute-start(f32[24,768]{1,0:T(8,128)} %get-tuple-element.28), channel_id=1, source_target_pairs={{1,0},{2,1},{3,2},{4,3},{5,4},{6,5},{7,6},{8,7},{9,8},{10,9},{11,1... | collective-permute-start | bytes 221192 | tf_op jit(solution)/shard_map/ppermute | solution.py:401
  92.8 0.6 copy-start.2
  92.8 0.7 copy-start.3
  95.1 34.4 %collective-permute-start.2 = (f32[168,768]{1,0:T(8,128)}, f32[168,768]{1,0:T(8,128)S(1)}, u32[]{:S(2)}, u32[]{:S(2)}) collective-permute-start(f32[168,768]{1,0:T(8,128)} %get-tuple-element.29), channel_id=1, source_target_pairs={{0,16},{16,32},{32,48},{48,64},{64,80},{80,96},{96,112},{1,17},{17... | collective-permute-start | bytes 1548296 | tf_op jit(solution)/shard_map/ppermute | solution.py:401
  100.5 29.0 %collective-permute-start.3 = (f32[168,768]{1,0:T(8,128)}, f32[168,768]{1,0:T(8,128)S(1)}, u32[]{:S(2)}, u32[]{:S(2)}) collective-permute-start(f32[168,768]{1,0:T(8,128)} %get-tuple-element.30), channel_id=1, source_target_pairs={{16,0},{32,16},{48,32},{64,48},{80,64},{96,80},{112,96},{17,1},{33... | collective-permute-start | bytes 1548296 | tf_op jit(solution)/shard_map/ppermute | solution.py:401
  102.7 0.6 copy-start.4
  102.7 0.6 copy-start.5
  123.7 38.2 %all-to-all-start.3 = ((f32[16,48,768]{2,1,0:T(8,128)}), f32[16,48,768]{2,1,0:T(8,128)}, u32[]{:S(2)}, u32[]{:S(2)}) async-start(f32[16,48,768]{2,1,0:T(8,128)} %potential.3), calls=%async_computation.3 | async-start | bytes 4718592 | tf_op jit(solution)/shard_map/all_to_all | solution.py:747
  129.6 0.8 copy-start
  130.4 0.8 copy-start.1
  161.9 36.4 %all-to-all-start.2 = ((f32[16,48,768]{2,1,0:T(8,128)}), f32[16,48,768]{2,1,0:T(8,128)}, u32[]{:S(2)}, u32[]{:S(2)}) async-start(f32[16,48,768]{2,1,0:T(8,128)} %potential.2), calls=%async_computation.2 | async-start | bytes 4718592 | tf_op jit(solution)/shard_map/all_to_all | solution.py:747

commit v7 on v6

--- a/solution.py
+++ b/solution.py
@@ -139,7 +139,7 @@
         return np.stack([np.cos(angle), np.sin(angle)]).astype(np.float32) * np.float32(scale)
 
     coarse = waves(np.arange(0, length // 4, stride), 1.0, length)
-    coarse = np.concatenate([coarse, waves(np.arange(1, 2), 1.0, 2 * length)], axis=1)
+    coarse = np.concatenate([coarse, waves(np.array([1, stride - 1]), 1.0, 2 * length)], axis=1)
     fine = waves(np.arange(stride), 1.0 / math.sqrt(norm), length)
     return jnp.asarray(coarse), jnp.asarray(fine)
 
@@ -171,8 +171,8 @@
     for c in range(2):
         wait_all(arriving[c])
     real, imag = [x_ref[c].reshape(lanes, 2 * half) for c in range(2)]
-    last = coarse_ref.shape[1] - 1
-    wave_cos, wave_sin = coarse_ref[0, last:], coarse_ref[1, last:]
+    first = coarse_ref.shape[1] - 2
+    wave_cos, wave_sin = [coarse_ref[i, first : first + 1] for i in range(2)]
     for p in range(2):
         if p == 0:
             values = real[:, :half] + real[:, half:], imag[:, :half] + imag[:, half:]
@@ -278,7 +278,7 @@
             copy.start()
 
 
-def gather_blocks(hbm_ref, in_ref, sems, high_ref, low_ref):
+def gather_blocks(hbm_ref, in_ref, sems, high_ref, low_ref, ways):
     parts, rows = in_ref.shape[0], in_ref.shape[-2]
     width = high_ref.shape[2]
     local = width // parts
@@ -304,15 +304,17 @@
                 if offset + local > 128:
                     after = load(p, at, block + 1)
                     value = jnp.where(lane < offset, after, value)
-                turned.append(pltpu.roll(value, (p * local - offset) % 128, 1))
+                turned.append(pltpu.roll(value, (p * (local // ways) - offset) % 128, 1))
             to = pl.ds(pl.multiple_of(z * rows + t * tile, tile), tile)
             for out in range(width // 128):
-                start = out * 128 // local
-                value = turned[start]
+                way, within = out * ways // (width // 128), out % (width // 128 // ways)
+                short = local // ways
+                start = within * 128 // short
+                value = turned[(start - way) % parts]
                 for p in range(start + 1, parts):
-                    edge = p * local - out * 128
+                    edge = p * short - within * 128
                     if edge < 128:
-                        value = jnp.where(lane < edge, value, turned[p])
+                        value = jnp.where(lane < edge, value, turned[(p - way) % parts])
                 high, low = split(value)
                 high_ref[c, to, out * 128 : (out + 1) * 128] = high
                 low_ref[c, to, out * 128 : (out + 1) * 128] = low
@@ -330,7 +332,7 @@
     small = copy_all([(coarse_hbm_ref, coarse_ref), (fine_hbm_ref, fine_ref)], factor_sems)
     fetch_blocks(blocks_ref, in_ref, in_sems)
     fill_tables(small, coarse_ref, fine_ref, tab_ref)
-    gather_blocks(blocks_ref, in_ref, in_sems, high_ref, low_ref)
+    gather_blocks(blocks_ref, in_ref, in_sems, high_ref, low_ref, 1)
     half = planes // 2
 
     def finish(z, carry):
@@ -500,7 +502,7 @@
     tab_hbm_ref, out_ref, tab_ref, tab_sems, pot_ref, tall_ref, stage_ref = refs[-count - 17 : -count - 10]
     in_sems, out_sems, side_sems = refs[-count - 10 : -count - 7]
     side_refs = refs[-count - 7 : -7]
-    planes, rows, width = pot_ref.shape
+    planes, blocks, rows, _ = pot_ref.shape
     each = planes // groups
     sides = copy_all(
         [
@@ -608,7 +610,9 @@
             along_x = (roll_x(fx, -1) - roll_x(fx, 1)) * slope
             along_y = (fy_ref[w + 1, r + 1 : r + 9] - fy_ref[w + 1, r - 1 : r + 7]) * slope
             along_z = (fz_ref[w + 2, here] - fz_ref[w, here]) * slope
-            pot_ref[z, 8 * t : 8 * t + 8] = flat_ref[w + 1, here] - (along_x + along_y + along_z)
+            value = flat_ref[w + 1, here] - (along_x + along_y + along_z)
+            for i in range(blocks):
+                pot_ref[z, i, 8 * t : 8 * t + 8, :] = value[:, i * 128 : (i + 1) * 128]
         return carry
 
     lax.fori_loop(0, planes, collect, 0)
@@ -617,10 +621,15 @@
 
 
 def forward_columns(x_ref, tab_ref, tall_ref, stage_ref, out_ref, out_sems):
-    planes, rows, width = x_ref.shape
-    high, low = split(x_ref[...].reshape(planes * rows, width).T)
-    for k, value in enumerate((high, high, low)):
-        tall_ref[k * width : (k + 1) * width] = value
+    planes, blocks, rows, _ = x_ref.shape
+    width = blocks * 128
+    for i in range(blocks):
+        pieces = [
+            x_ref[z, i, pl.ds(p, rows // 2, stride=2), :] for z in range(planes) for p in range(2)
+        ]
+        high, low = split(jnp.concatenate(pieces, axis=0).T)
+        for k, value in enumerate((high, high, low)):
+            tall_ref[k * width + i * 128 : k * width + (i + 1) * 128] = value
     parts, block, out_lanes = stage_ref.shape
     group = parts // 2
 
@@ -646,7 +655,7 @@
     lanes = count * rows
     out = (parts, width // parts, 2 * lanes)
     scratch = table_scratch(width) + [
-        pltpu.VMEM((count, rows, width), f32),
+        pltpu.VMEM((count, width // 128, rows, 128), f32),
         pltpu.VMEM((3 * width, lanes), bf16),
         pltpu.VMEM(out, f32),
         pltpu.SemaphoreType.DMA((len(sources),)),
@@ -673,14 +682,20 @@
 
 def forward_rows_body(starts, flag_ref, blocks_ref, coarse_hbm_ref, fine_hbm_ref, *refs):
     coarse_ref, fine_ref, factor_sems = refs[-3:]
-    out_ref, tab_ref, in_ref, stage_ref, high_ref, low_ref, in_sems, out_sems = refs[-11:-3]
+    out_ref, tab_ref, wide_ref, in_ref, stage_ref, high_ref, low_ref, in_sems, out_sems = refs[-12:-3]
     _, planes, rows, width = stage_ref.shape
     small = copy_all([(coarse_hbm_ref, coarse_ref), (fine_hbm_ref, fine_ref)], factor_sems)
     fetch_blocks(blocks_ref, in_ref, in_sems)
     fill_tables(small, coarse_ref, fine_ref, tab_ref)
-    gather_blocks(blocks_ref, in_ref, in_sems, high_ref, low_ref)
-    high_ref[2], low_ref[2] = -high_ref[0], -low_ref[0]
-
+    length = tab_ref.shape[1]
+    for k, part in enumerate((0, 0, 1)):
+        re_at = slice(k * length, (k + 1) * length)
+        im_at = slice((k + 3) * length, (k + 4) * length)
+        wide_ref[re_at, :length], wide_ref[re_at, length:] = tab_ref[part], -tab_ref[2 + part]
+        wide_ref[im_at, :length], wide_ref[im_at, length:] = tab_ref[2 + part], tab_ref[part]
+    gather_blocks(blocks_ref, in_ref, in_sems, high_ref, low_ref, 2)
+    last = coarse_ref.shape[1] - 1
+    wave_cos, wave_sin = coarse_ref[0, last:], coarse_ref[1, last:]
     half = planes // 2
 
     def copies(c, m):
@@ -690,12 +705,24 @@
             for y, z in enumerate([m * half + y for y in range(half)])
         ]
 
-    def step(i, carry):
-        c, m = i // 2, i % 2
+    def step(m, carry):
         at = pl.ds(pl.multiple_of(m * half * rows, half * rows), half * rows)
-        value = triple(dot_nn, high_ref[c, at], low_ref[c, at], tab_ref[0], tab_ref[1])
-        value = value + triple(dot_nn, high_ref[c + 1, at], low_ref[c + 1, at], tab_ref[2], tab_ref[3])
-        stage_ref[c, pl.ds(m * half, half)] = value.reshape(half, rows, width)
+        to = pl.ds(m * half, half)
+
+        def product(way):
+            lanes = slice(way * length, (way + 1) * length)
+            pairs = [(high_ref[c, at, lanes], low_ref[c, at, lanes]) for c in range(2)]
+            left = [value for high, low in pairs for value in (high, low, high)]
+            both = dot_nn(jnp.concatenate(left, axis=1), wide_ref[...])
+            return both[:, :length], both[:, length:]
+
+        even = product(0)
+        odd_re, odd_im = product(1)
+        odd = odd_re * wave_cos - odd_im * wave_sin, odd_re * wave_sin + odd_im * wave_cos
+        for c in range(2):
+            shape = (half, rows, length)
+            stage_ref[c, to, :, :length] = (even[c] + odd[c]).reshape(shape)
+            stage_ref[c, to, :, length:] = (even[c] - odd[c]).reshape(shape)
 
         @pl.when(flag_ref[2] == 1)
         def _():
@@ -703,30 +730,34 @@
             at_zero = (lax.broadcasted_iota(jnp.int32, tile, 0) == 0) & (
                 lax.broadcasted_iota(jnp.int32, tile, 1) == 0
             )
-            for y in range(half):
-                z = m * half + y
-                stage_ref[c, z, :8, :128] = jnp.where(at_zero, 0.0, stage_ref[c, z, :8, :128])
-
-        for copy in copies(c, m):
+            for c in range(2):
+                for y in range(half):
+                    z = m * half + y
+                    corner = stage_ref[c, z, :8, :128]
+                    stage_ref[c, z, :8, :128] = jnp.where(at_zero, 0.0, corner)
+
+        for copy in copies(0, m) + copies(1, m):
             copy.start()
         return carry
 
-    lax.fori_loop(0, 4, step, 0)
+    lax.fori_loop(0, 2, step, 0)
     for c in range(2):
         wait_all(copies(c, 0) + copies(c, 1))
 
 
 def forward_rows(flags, blocks, factors, starts, depth, before):
     parts, rows, lanes = blocks.shape
-    width = factors[0].shape[2]
+    length = factors[0].shape[2]
+    width = 2 * length
     planes = lanes * parts // (2 * width)
     earlier = [] if before is None else [before]
     scratch = [
-        pltpu.VMEM((4, width, width), bf16),
+        pltpu.VMEM((4, length, length), bf16),
+        pltpu.VMEM((6 * length, width), bf16),
         pltpu.VMEM(blocks.shape, f32),
         pltpu.VMEM((2, planes, rows, width), f32),
-        pltpu.VMEM((3, planes * rows, width), bf16),
-        pltpu.VMEM((3, planes * rows, width), bf16),
+        pltpu.VMEM((2, planes * rows, width), bf16),
+        pltpu.VMEM((2, planes * rows, width), bf16),
         pltpu.SemaphoreType.DMA((rows // gather_tile, 4)),
         pltpu.SemaphoreType.DMA((2, planes)),
     ]
@@ -790,8 +821,8 @@
     halo = [below, above]
     spectral = potential_of(flags, planes + halo, sides + halo, outside, 2, tables, parts)
     outer_waves = exchange(spectral)
-    result = forward_rows(flags, inner_waves, factors, (unit, 2 * unit), depth, None)
-    result = forward_rows(flags, outer_waves, factors, (0, depth - unit), depth, result)
+    result = forward_rows(flags, inner_waves, half_factors, (unit, 2 * unit), depth, None)
+    result = forward_rows(flags, outer_waves, half_factors, (0, depth - unit), depth, result)
     return result
 
 

time: 213 us -> 210 us (0.986)
  Pallas kernels: 106 us -> 99.5 us
  waiting for transfers between devices: 69.1 us -> 72.2 us
    pallas_call x2, Pallas kernels: 24.2 us -> 18.2 us  [forward_rows(): call(lambda *refs: forward_rows_body(starts, *refs), array(2, depth, rows...]
    all_to_all x4, waiting for transfers between devices: 69.1 us -> 72.2 us  [exchange(): return lax.all_to_all(value, 'py', 0, 0, tiled=True)]
  transfers between devices with their start and end apart: 10 -> 10, of which waited for: 4 -> 4; matrix products, arithmetic and copies ran while one was open for 0% -> 0% of each run, Pallas kernels for 41% -> 40%
where the time goes in v7:
time: 210 us; the launch traced here: 208 us
  Pallas kernels  99.5 us (47%)
  waiting for transfers between devices  72.2 us (34%)
  starting transfers between devices  32 us (15%)
  local copies, waits for them, and re-layouts  2.91 us (1%)
    all_to_all x4, waiting for transfers between devices, exchange(): return lax.all_to_all(value, 'py', 0, 0, tiled=True)  72.2 us
    pallas_call x2, Pallas kernels, potential_of(): call(lambda *refs: potential_body(sources, groups, *refs), array(*out), 2...  43.9 us
    all_to_all x4, starting transfers between devices, exchange(): return lax.all_to_all(value, 'py', 0, 0, tiled=True)  20.8 us
    pallas_call x2, Pallas kernels, forward_rows(): call(lambda *refs: forward_rows_body(starts, *refs), array(2, depth, rows...  18.2 us
    pallas_call x2, Pallas kernels, inverse_columns(): call(lambda *refs: inverse_columns_body(sends, *refs), [array(planes, row...  18.1 us
    ppermute x6, starting transfers between devices, shift(): lax.ppermute(value, axis, pairs if up else [(b, a) for a, b in pairs])  11.1 us
    pallas_call x1, Pallas kernels, inverse_rows(): call(body, [array(*out), jax.ShapeDtypeStruct((4, width, width), bf16)],...  10.7 us
    pallas_call x1, Pallas kernels, inverse_rows(): call(body, array(*out), 10.0, grid=(1,), in_specs=[in_hbm] * 3, out_specs...  6.92 us
  transfers between devices with their start and end apart: 10, of which 4 were waited for; matrix products, arithmetic and copies ran while one was open for 0% of the time, Pallas kernels for 40%

profile of v7, /device:TPU:14, one launch (start us, length us, event | category | flops | bytes accessed | tf_op | source)
XLA Modules:
  0.0 207.5 jit_solution(9994172024481765689)
XLA Ops:
  0.0 6.9 %inverse_rows.2 = f32[16,6,48,128]{3,2,1,0:T(8,128)} custom-call(f32[2,16,48,768]{3,2,1,0:T(8,128)} %refs_0_.3, f32[2,4,384]{2,1,0:T(4,128)} %constant.23.clone.refs_1_.refs_2_, f32[2,48,384]{2,1,0:T(8,128)} %constant.24.clone.refs_2_.refs_3_), custom_call_target="tpu_custom_call" | custom-call | flops 10000000000 | bytes 1048576 | tf_op jit(solution)/shard_map/inverse_rows/pallas_call | solution.py:249
  6.9 6.3 %all-to-all-start = ((f32[16,6,48,128]{3,2,1,0:T(8,128)}), f32[16,6,48,128]{3,2,1,0:T(8,128)}, u32[]{:S(2)}, u32[]{:S(2)}) async-start(f32[16,6,48,128]{3,2,1,0:T(8,128)} %inverse_rows.2), calls=%async_computation | async-start | bytes 4718592 | tf_op jit(solution)/shard_map/all_to_all | solution.py:778
  13.8 10.7 %inverse_rows.3 = (f32[16,6,48,128]{3,2,1,0:T(8,128)}, bf16[4,768,768]{2,1,0:T(8,128)(2,1)}) custom-call(f32[2,16,48,768]{3,2,1,0:T(8,128)} %refs_0_.3, f32[2,4,384]{2,1,0:T(4,128)} %constant.23.clone.refs_1_.refs_2_, f32[2,48,384]{2,1,0:T(8,128)} %constant.24.clone.refs_2_.refs_3_, f32[2,6,768]{2,1,0:T(8,128)} %constant.21.clone.refs_1_.refs_3_, ...), custom_call_target="tpu_custom_call" | custom-call | flops 10000000000 | bytes 1048576 | tf_op jit(solution)/shard_map/inverse_rows/pallas_call | solution.py:239
  24.5 21.1 %all-to-all-done.refs_0_ = f32[16,6,48,128]{3,2,1,0:T(8,128)} async-done(((f32[16,6,48,128]{3,2,1,0:T(8,128)}), f32[16,6,48,128]{3,2,1,0:T(8,128)}, u32[]{:S(2)}, u32[]{:S(2)}) %all-to-all-start) | async-done | bytes 2359328 | tf_op jit(solution)/shard_map/all_to_all | solution.py:778
  45.6 4.3 %all-to-all-start.1 = ((f32[16,6,48,128]{3,2,1,0:T(8,128)}), f32[16,6,48,128]{3,2,1,0:T(8,128)}, u32[]{:S(2)}, u32[]{:S(2)}) async-start(f32[16,6,48,128]{3,2,1,0:T(8,128)} %get-tuple-element.20), calls=%async_computation.1 | async-start | bytes 4718592 | tf_op jit(solution)/shard_map/all_to_all | solution.py:778
  50.0 9.3 %inverse_columns.2 = (f32[8,48,768]{2,1,0:T(8,128)}, f32[24,768]{1,0:T(8,128)}, f32[24,768]{1,0:T(8,128)}, f32[168,768]{1,0:T(8,128)}, f32[168,768]{1,0:T(8,128)}) custom-call(f32[16,6,48,128]{3,2,1,0:T(8,128)} %all-to-all-done.refs_0_, f32[2,6,768]{2,1,0:T(8,128)} %constant.21.clone.refs_1_.refs_3_, f32[2,48,768]{2,1,0:T(8,128)} %constant.22.clone.refs_2_.refs_4_), custom_call_target="tpu_custom_call" | custom-call | flops 7000000000 | bytes 1048576 | tf_op jit(solution)/shard_map/inverse_columns/pallas_call | solution.py:387
  59.3 1.7 collective-permute-start.1
  61.1 21.0 %all-to-all-done.1.refs_0_ = f32[16,6,48,128]{3,2,1,0:T(8,128)} async-done(((f32[16,6,48,128]{3,2,1,0:T(8,128)}), f32[16,6,48,128]{3,2,1,0:T(8,128)}, u32[]{:S(2)}, u32[]{:S(2)}) %all-to-all-start.1) | async-done | bytes 2359328 | tf_op jit(solution)/shard_map/all_to_all | solution.py:778
  82.1 8.9 %inverse_columns.3 = (f32[8,48,768]{2,1,0:T(8,128)}, f32[24,768]{1,0:T(8,128)}, f32[24,768]{1,0:T(8,128)}) custom-call(f32[16,6,48,128]{3,2,1,0:T(8,128)} %all-to-all-done.1.refs_0_, f32[2,6,768]{2,1,0:T(8,128)} %constant.21.clone.refs_1_.refs_3_, f32[2,48,768]{2,1,0:T(8,128)} %constant.22.clone.refs_2_.refs_4_), custom_call_target="tpu_custom_call" | custom-call | flops 7000000000 | bytes 1048576 | tf_op jit(solution)/shard_map/inverse_columns/pallas_call | solution.py:387
  91.1 1.7 collective-permute-start.5
  92.8 0.6 copy-done.2
  93.5 1.6 halo_slabs.1
  95.1 5.4 %collective-permute-start.2 = (f32[168,768]{1,0:T(8,128)}, f32[168,768]{1,0:T(8,128)S(1)}, u32[]{:S(2)}, u32[]{:S(2)}) collective-permute-start(f32[168,768]{1,0:T(8,128)} %get-tuple-element.29), channel_id=1, source_target_pairs={{0,16},{16,32},{32,48},{48,64},{64,80},{80,96},{96,112},{1,17},{17... | collective-permute-start | bytes 1548296 | tf_op jit(solution)/shard_map/ppermute | solution.py:403
  100.5 2.1 %collective-permute-start.3 = (f32[168,768]{1,0:T(8,128)}, f32[168,768]{1,0:T(8,128)S(1)}, u32[]{:S(2)}, u32[]{:S(2)}) collective-permute-start(f32[168,768]{1,0:T(8,128)} %get-tuple-element.30), channel_id=1, source_target_pairs={{16,0},{32,16},{48,32},{64,48},{80,64},{96,80},{112,96},{17,1},{33... | collective-permute-start | bytes 1548296 | tf_op jit(solution)/shard_map/ppermute | solution.py:403
  103.3 20.3 %potential.3 = f32[16,48,768]{2,1,0:T(8,128)} custom-call(s32[3]{0:T(128)} %add_convert_fusion.refs_5_.refs_0_, f32[8,48,768]{2,1,0:T(8,128)} %get-tuple-element.19.refs_1_, f32[8,48,768]{2,1,0:T(8,128)} %get-tuple-element.21.refs_2_, f32[24,768]{1,0:T(8,128)} %copy-done.2, f32[24,768]{1,0:T(8,128)} %copy-done.3, f32[24,768]{1,0:T(8,128)} %copy-done.4, ...), custom_call_target="tpu_custom_call" | custom-call | flops 20000000000 | bytes 1048576 | tf_op jit(solution)/shard_map/potential/pallas_call | solution.py:668
  123.7 5.8 %all-to-all-start.3 = ((f32[16,48,768]{2,1,0:T(8,128)}), f32[16,48,768]{2,1,0:T(8,128)}, u32[]{:S(2)}, u32[]{:S(2)}) async-start(f32[16,48,768]{2,1,0:T(8,128)} %potential.3), calls=%async_computation.3 | async-start | bytes 4718592 | tf_op jit(solution)/shard_map/all_to_all | solution.py:778
  129.5 0.8 copy-done
  130.4 0.8 copy-done.1
  131.1 23.6 %potential.2 = f32[16,48,768]{2,1,0:T(8,128)} custom-call(s32[3]{0:T(128)} %add_convert_fusion.refs_5_.refs_0_, f32[8,48,768]{2,1,0:T(8,128)} %get-tuple-element.19.refs_1_, f32[8,48,768]{2,1,0:T(8,128)} %get-tuple-element.21.refs_2_, f32[168,768]{1,0:T(8,128)} %copy-done, f32[168,768]{1,0:T(8,128)} %copy-done.1, f32[24,768]{1,0:T(8,128)} %copy-done.2, ...), custom_call_target="tpu_custom_call" | custom-call | flops 20000000000 | bytes 1048576 | tf_op jit(solution)/shard_map/potential/pallas_call | solution.py:668
  154.8 7.1 %all-to-all-done.3.refs_1_ = f32[16,48,768]{2,1,0:T(8,128)} async-done(((f32[16,48,768]{2,1,0:T(8,128)}), f32[16,48,768]{2,1,0:T(8,128)}, u32[]{:S(2)}, u32[]{:S(2)}) %all-to-all-start.3) | async-done | bytes 2359328 | tf_op jit(solution)/shard_map/all_to_all | solution.py:778
  161.8 4.3 %all-to-all-start.2 = ((f32[16,48,768]{2,1,0:T(8,128)}), f32[16,48,768]{2,1,0:T(8,128)}, u32[]{:S(2)}, u32[]{:S(2)}) async-start(f32[16,48,768]{2,1,0:T(8,128)} %potential.2), calls=%async_computation.2 | async-start | bytes 4718592 | tf_op jit(solution)/shard_map/all_to_all | solution.py:778
  166.2 9.1 %forward_rows.2.refs_4_ = f32[2,16,48,768]{3,2,1,0:T(8,128)} custom-call(s32[3]{0:T(128)} %add_convert_fusion.refs_5_.refs_0_, f32[16,48,768]{2,1,0:T(8,128)} %all-to-all-done.3.refs_1_, f32[2,4,384]{2,1,0:T(4,128)} %constant.23.clone.refs_1_.refs_2_, f32[2,48,384]{2,1,0:T(8,128)} %constant.24.clone.refs_2_.refs_3_), custom_call_target="tpu_custom_call" | custom-call | flops 10000000000 | bytes 1048576 | tf_op jit(solution)/shard_map/forward_rows/pallas_call | solution.py:764
  175.3 22.9 %all-to-all-done.2.refs_1_ = f32[16,48,768]{2,1,0:T(8,128)} async-done(((f32[16,48,768]{2,1,0:T(8,128)}), f32[16,48,768]{2,1,0:T(8,128)}, u32[]{:S(2)}, u32[]{:S(2)}) %all-to-all-start.2) | async-done | bytes 2359328 | tf_op jit(solution)/shard_map/all_to_all | solution.py:778
  198.2 9.1 %forward_rows.3 = f32[2,16,48,768]{3,2,1,0:T(8,128)} custom-call(s32[3]{0:T(128)} %add_convert_fusion.refs_5_.refs_0_, f32[16,48,768]{2,1,0:T(8,128)} %all-to-all-done.2.refs_1_, f32[2,4,384]{2,1,0:T(4,128)} %constant.23.clone.refs_1_.refs_2_, f32[2,48,384]{2,1,0:T(8,128)} %constant.24.clone.refs_2_.refs_3_, ...), custom_call_target="tpu_custom_call", output_to_operand_aliasing={{}: (4, {})} | custom-call | flops 10000000000 | bytes 1048576 | tf_op jit(solution)/shard_map/forward_rows/pallas_call | solution.py:764
  (18 shorter events, 1.4 us)
Async XLA Ops:
  6.9 38.7 %all-to-all-start = ((f32[16,6,48,128]{3,2,1,0:T(8,128)}), f32[16,6,48,128]{3,2,1,0:T(8,128)}, u32[]{:S(2)}, u32[]{:S(2)}) async-start(f32[16,6,48,128]{3,2,1,0:T(8,128)} %inverse_rows.2), calls=%async_computation | async-start | bytes 4718592 | tf_op jit(solution)/shard_map/all_to_all | solution.py:778
  45.6 36.5 %all-to-all-start.1 = ((f32[16,6,48,128]{3,2,1,0:T(8,128)}), f32[16,6,48,128]{3,2,1,0:T(8,128)}, u32[]{:S(2)}, u32[]{:S(2)}) async-start(f32[16,6,48,128]{3,2,1,0:T(8,128)} %get-tuple-element.20), calls=%async_computation.1 | async-start | bytes 4718592 | tf_op jit(solution)/shard_map/all_to_all | solution.py:778
  59.3 33.6 %collective-permute-start = (f32[24,768]{1,0:T(8,128)}, f32[24,768]{1,0:T(8,128)S(1)}, u32[]{:S(2)}, u32[]{:S(2)}) collective-permute-start(f32[24,768]{1,0:T(8,128)} %get-tuple-element.22), channel_id=1, source_target_pairs={{0,1},{1,2},{2,3},{3,4},{4,5},{5,6},{6,7},{7,8},{8,9},{9,10},{10,1... | collective-permute-start | bytes 221192 | tf_op jit(solution)/shard_map/ppermute | solution.py:403
  59.3 33.5 %collective-permute-start.1 = (f32[24,768]{1,0:T(8,128)}, f32[24,768]{1,0:T(8,128)S(1)}, u32[]{:S(2)}, u32[]{:S(2)}) collective-permute-start(f32[24,768]{1,0:T(8,128)} %get-tuple-element.23), channel_id=1, source_target_pairs={{1,0},{2,1},{3,2},{4,3},{5,4},{6,5},{7,6},{8,7},{9,8},{10,9},{11,1... | collective-permute-start | bytes 221192 | tf_op jit(solution)/shard_map/ppermute | solution.py:403
  91.0 11.6 %collective-permute-start.4 = (f32[24,768]{1,0:T(8,128)}, f32[24,768]{1,0:T(8,128)S(1)}, u32[]{:S(2)}, u32[]{:S(2)}) collective-permute-start(f32[24,768]{1,0:T(8,128)} %get-tuple-element.31), channel_id=1, source_target_pairs={{0,1},{1,2},{2,3},{3,4},{4,5},{5,6},{6,7},{7,8},{8,9},{9,10},{10,1... | collective-permute-start | bytes 221192 | tf_op jit(solution)/shard_map/ppermute | solution.py:403
  91.1 11.6 %collective-permute-start.5 = (f32[24,768]{1,0:T(8,128)}, f32[24,768]{1,0:T(8,128)S(1)}, u32[]{:S(2)}, u32[]{:S(2)}) collective-permute-start(f32[24,768]{1,0:T(8,128)} %get-tuple-element.28), channel_id=1, source_target_pairs={{1,0},{2,1},{3,2},{4,3},{5,4},{6,5},{7,6},{8,7},{9,8},{10,9},{11,1... | collective-permute-start | bytes 221192 | tf_op jit(solution)/shard_map/ppermute | solution.py:403
  92.8 0.6 copy-start.2
  92.8 0.7 copy-start.3
  95.1 34.4 %collective-permute-start.2 = (f32[168,768]{1,0:T(8,128)}, f32[168,768]{1,0:T(8,128)S(1)}, u32[]{:S(2)}, u32[]{:S(2)}) collective-permute-start(f32[168,768]{1,0:T(8,128)} %get-tuple-element.29), channel_id=1, source_target_pairs={{0,16},{16,32},{32,48},{48,64},{64,80},{80,96},{96,112},{1,17},{17... | collective-permute-start | bytes 1548296 | tf_op jit(solution)/shard_map/ppermute | solution.py:403
  100.5 29.0 %collective-permute-start.3 = (f32[168,768]{1,0:T(8,128)}, f32[168,768]{1,0:T(8,128)S(1)}, u32[]{:S(2)}, u32[]{:S(2)}) collective-permute-start(f32[168,768]{1,0:T(8,128)} %get-tuple-element.30), channel_id=1, source_target_pairs={{16,0},{32,16},{48,32},{64,48},{80,64},{96,80},{112,96},{17,1},{33... | collective-permute-start | bytes 1548296 | tf_op jit(solution)/shard_map/ppermute | solution.py:403
  102.7 0.6 copy-start.4
  102.7 0.6 copy-start.5
  123.7 38.2 %all-to-all-start.3 = ((f32[16,48,768]{2,1,0:T(8,128)}), f32[16,48,768]{2,1,0:T(8,128)}, u32[]{:S(2)}, u32[]{:S(2)}) async-start(f32[16,48,768]{2,1,0:T(8,128)} %potential.3), calls=%async_computation.3 | async-start | bytes 4718592 | tf_op jit(solution)/shard_map/all_to_all | solution.py:778
  129.5 0.8 copy-start
  130.3 0.8 copy-start.1
  161.8 36.4 %all-to-all-start.2 = ((f32[16,48,768]{2,1,0:T(8,128)}), f32[16,48,768]{2,1,0:T(8,128)}, u32[]{:S(2)}, u32[]{:S(2)}) async-start(f32[16,48,768]{2,1,0:T(8,128)} %potential.2), calls=%async_computation.2 | async-start | bytes 4718592 | tf_op jit(solution)/shard_map/all_to_all | solution.py:778

commit v8 on v7

--- a/solution.py
+++ b/solution.py
@@ -795,10 +795,11 @@
     inner = exchange(inner)
     outer, head, tail, low_planes, high_planes = inverse_columns(outer, factors, True)
     outer_sides = shift(tail, "py", True, True), shift(head, "py", False, True)
+    down, up = halo_slabs(low_planes, high_planes, *outer_sides)
+    inner, down, up = lax.optimization_barrier((inner, down, up))
     inner, head, tail = inverse_columns(inner, factors, False)
     inner_sides = shift(tail, "py", True, True), shift(head, "py", False, True)
 
-    down, up = halo_slabs(low_planes, high_planes, *outer_sides)
     down, up, _ = lax.optimization_barrier((down, up, head))
     below, above = shift(up, "px", True, False), shift(down, "px", False, False)
 

time: 210 us -> 209 us (level)
    ppermute x6, waiting for transfers between devices: 0.02 us -> 21.6 us  [shift(): lax.ppermute(value, axis, pairs if up else [(b, a) for a, b in pairs])]
    all_to_all x4, waiting for transfers between devices: 72.2 us -> 51.1 us  [exchange(): return lax.all_to_all(value, 'py', 0, 0, tiled=True)]
  transfers between devices with their start and end apart: 10 -> 10, of which waited for: 4 -> 4; matrix products, arithmetic and copies ran while one was open for 0% -> 0% of each run, Pallas kernels for 40% -> 36%
where the time goes in v8:
time: 209 us; the launch traced here: 207 us
  Pallas kernels  99.5 us (48%)
  waiting for transfers between devices  72.7 us (35%)
  starting transfers between devices  30.6 us (15%)
  local copies, waits for them, and re-layouts  2.9 us (1%)
    all_to_all x4, waiting for transfers between devices, exchange(): return lax.all_to_all(value, 'py', 0, 0, tiled=True)  51.1 us
    pallas_call x2, Pallas kernels, potential_of(): call(lambda *refs: potential_body(sources, groups, *refs), array(*out), 2...  43.9 us
    ppermute x6, waiting for transfers between devices, shift(): lax.ppermute(value, axis, pairs if up else [(b, a) for a, b in pairs])  21.6 us
    all_to_all x4, starting transfers between devices, exchange(): return lax.all_to_all(value, 'py', 0, 0, tiled=True)  19.5 us
    pallas_call x2, Pallas kernels, forward_rows(): call(lambda *refs: forward_rows_body(starts, *refs), array(2, depth, rows...  18.2 us
    pallas_call x2, Pallas kernels, inverse_columns(): call(lambda *refs: inverse_columns_body(sends, *refs), [array(planes, row...  18.2 us
    ppermute x6, starting transfers between devices, shift(): lax.ppermute(value, axis, pairs if up else [(b, a) for a, b in pairs])  11.1 us
    pallas_call x1, Pallas kernels, inverse_rows(): call(body, [array(*out), jax.ShapeDtypeStruct((4, width, width), bf16)],...  10.7 us
  transfers between devices with their start and end apart: 10, of which 4 were waited for; matrix products, arithmetic and copies ran while one was open for 0% of the time, Pallas kernels for 36%

profile of v8, /device:TPU:14, one launch (start us, length us, event | category | flops | bytes accessed | tf_op | source)
XLA Modules:
  0.0 206.8 jit_solution(10974631386897202721)
XLA Ops:
  0.0 6.9 %inverse_rows.2 = f32[16,6,48,128]{3,2,1,0:T(8,128)} custom-call(f32[2,16,48,768]{3,2,1,0:T(8,128)} %refs_0_.3, f32[2,4,384]{2,1,0:T(4,128)} %constant.23.clone.refs_1_.refs_2_, f32[2,48,384]{2,1,0:T(8,128)} %constant.24.clone.refs_2_.refs_3_), custom_call_target="tpu_custom_call" | custom-call | flops 10000000000 | bytes 1048576 | tf_op jit(solution)/shard_map/inverse_rows/pallas_call | solution.py:249
  6.9 6.3 %all-to-all-start = ((f32[16,6,48,128]{3,2,1,0:T(8,128)}), f32[16,6,48,128]{3,2,1,0:T(8,128)}, u32[]{:S(2)}, u32[]{:S(2)}) async-start(f32[16,6,48,128]{3,2,1,0:T(8,128)} %inverse_rows.2), calls=%async_computation | async-start | bytes 4718592 | tf_op jit(solution)/shard_map/all_to_all | solution.py:778
  13.8 10.7 %inverse_rows.3 = (f32[16,6,48,128]{3,2,1,0:T(8,128)}, bf16[4,768,768]{2,1,0:T(8,128)(2,1)}) custom-call(f32[2,16,48,768]{3,2,1,0:T(8,128)} %refs_0_.3, f32[2,4,384]{2,1,0:T(4,128)} %constant.23.clone.refs_1_.refs_2_, f32[2,48,384]{2,1,0:T(8,128)} %constant.24.clone.refs_2_.refs_3_, f32[2,6,768]{2,1,0:T(8,128)} %constant.21.clone.refs_1_.refs_3_, ...), custom_call_target="tpu_custom_call" | custom-call | flops 10000000000 | bytes 1048576 | tf_op jit(solution)/shard_map/inverse_rows/pallas_call | solution.py:239
  24.5 21.1 %all-to-all-done.refs_0_ = f32[16,6,48,128]{3,2,1,0:T(8,128)} async-done(((f32[16,6,48,128]{3,2,1,0:T(8,128)}), f32[16,6,48,128]{3,2,1,0:T(8,128)}, u32[]{:S(2)}, u32[]{:S(2)}) %all-to-all-start) | async-done | bytes 2359328 | tf_op jit(solution)/shard_map/all_to_all | solution.py:778
  45.6 4.3 %all-to-all-start.1 = ((f32[16,6,48,128]{3,2,1,0:T(8,128)}), f32[16,6,48,128]{3,2,1,0:T(8,128)}, u32[]{:S(2)}, u32[]{:S(2)}) async-start(f32[16,6,48,128]{3,2,1,0:T(8,128)} %get-tuple-element.23), calls=%async_computation.1 | async-start | bytes 4718592 | tf_op jit(solution)/shard_map/all_to_all | solution.py:778
  50.0 9.2 %inverse_columns.2 = (f32[8,48,768]{2,1,0:T(8,128)}, f32[24,768]{1,0:T(8,128)}, f32[24,768]{1,0:T(8,128)}, f32[168,768]{1,0:T(8,128)}, f32[168,768]{1,0:T(8,128)}) custom-call(f32[16,6,48,128]{3,2,1,0:T(8,128)} %all-to-all-done.refs_0_, f32[2,6,768]{2,1,0:T(8,128)} %constant.21.clone.refs_1_.refs_3_, f32[2,48,768]{2,1,0:T(8,128)} %constant.22.clone.refs_2_.refs_4_), custom_call_target="tpu_custom_call" | custom-call | flops 7000000000 | bytes 1048576 | tf_op jit(solution)/shard_map/inverse_columns/pallas_call | solution.py:387
  59.3 1.7 collective-permute-start.1
  61.0 21.6 %collective-permute-done.head_ref.refs_5_.refs_3_ = f32[24,768]{1,0:T(8,128)S(1)} collective-permute-done((f32[24,768]{1,0:T(8,128)}, f32[24,768]{1,0:T(8,128)S(1)}, u32[]{:S(2)}, u32[]{:S(2)}) %collective-permute-start) | collective-permute-done | bytes 73760 | tf_op jit(solution)/shard_map/ppermute | solution.py:403
  82.6 0.6 copy-done.3
  83.3 1.6 halo_slabs.1
  84.9 9.0 %inverse_columns.3 = (f32[8,48,768]{2,1,0:T(8,128)}, f32[24,768]{1,0:T(8,128)}, f32[24,768]{1,0:T(8,128)}) custom-call(f32[16,6,48,128]{3,2,1,0:T(8,128)} %all-to-all-done.1.refs_0_, f32[2,6,768]{2,1,0:T(8,128)} %constant.21.clone.refs_1_.refs_3_, f32[2,48,768]{2,1,0:T(8,128)} %constant.22.clone.refs_2_.refs_4_), custom_call_target="tpu_custom_call" | custom-call | flops 7000000000 | bytes 1048576 | tf_op jit(solution)/shard_map/inverse_columns/pallas_call | solution.py:387
  94.0 1.7 collective-permute-start.5
  95.7 5.4 %collective-permute-start.2 = (f32[168,768]{1,0:T(8,128)}, f32[168,768]{1,0:T(8,128)S(1)}, u32[]{:S(2)}, u32[]{:S(2)}) collective-permute-start(f32[168,768]{1,0:T(8,128)} %get-tuple-element.35), channel_id=1, source_target_pairs={{0,16},{16,32},{32,48},{48,64},{64,80},{80,96},{96,112},{1,17},{17... | collective-permute-start | bytes 1548296 | tf_op jit(solution)/shard_map/ppermute | solution.py:403
  101.1 2.1 %collective-permute-start.3 = (f32[168,768]{1,0:T(8,128)S(1)}, f32[168,768]{1,0:T(8,128)S(1)}, u32[]{:S(2)}, u32[]{:S(2)}) collective-permute-start(f32[168,768]{1,0:T(8,128)S(1)} %copy-done.2), channel_id=1, source_target_pairs={{16,0},{32,16},{48,32},{64,48},{80,64},{96,80},{112,96},{17,1},{33... | collective-permute-start | bytes 1548296 | tf_op jit(solution)/shard_map/ppermute | solution.py:403
  103.9 20.3 %potential.3 = f32[16,48,768]{2,1,0:T(8,128)} custom-call(s32[3]{0:T(128)} %add_convert_fusion.refs_5_.refs_0_, f32[8,48,768]{2,1,0:T(8,128)} %get-tuple-element.22.refs_1_, f32[8,48,768]{2,1,0:T(8,128)} %get-tuple-element.31.refs_2_, f32[24,768]{1,0:T(8,128)} %copy-done.3, f32[24,768]{1,0:T(8,128)} %copy-done.4, f32[24,768]{1,0:T(8,128)} %copy-done.5, ...), custom_call_target="tpu_custom_call" | custom-call | flops 20000000000 | bytes 1048576 | tf_op jit(solution)/shard_map/potential/pallas_call | solution.py:668
  124.2 4.6 %all-to-all-start.3 = ((f32[16,48,768]{2,1,0:T(8,128)}), f32[16,48,768]{2,1,0:T(8,128)}, u32[]{:S(2)}, u32[]{:S(2)}) async-start(f32[16,48,768]{2,1,0:T(8,128)} %potential.3), calls=%async_computation.3 | async-start | bytes 4718592 | tf_op jit(solution)/shard_map/all_to_all | solution.py:778
  128.8 0.8 copy-done
  129.6 0.8 copy-done.1
  130.4 23.6 %potential.2 = f32[16,48,768]{2,1,0:T(8,128)} custom-call(s32[3]{0:T(128)} %add_convert_fusion.refs_5_.refs_0_, f32[8,48,768]{2,1,0:T(8,128)} %get-tuple-element.22.refs_1_, f32[8,48,768]{2,1,0:T(8,128)} %get-tuple-element.31.refs_2_, f32[168,768]{1,0:T(8,128)} %copy-done, f32[168,768]{1,0:T(8,128)} %copy-done.1, f32[24,768]{1,0:T(8,128)} %copy-done.3, ...), custom_call_target="tpu_custom_call" | custom-call | flops 20000000000 | bytes 1048576 | tf_op jit(solution)/shard_map/potential/pallas_call | solution.py:668
  154.0 7.1 %all-to-all-done.3.refs_1_ = f32[16,48,768]{2,1,0:T(8,128)} async-done(((f32[16,48,768]{2,1,0:T(8,128)}), f32[16,48,768]{2,1,0:T(8,128)}, u32[]{:S(2)}, u32[]{:S(2)}) %all-to-all-start.3) | async-done | bytes 2359328 | tf_op jit(solution)/shard_map/all_to_all | solution.py:778
  161.1 4.4 %all-to-all-start.2 = ((f32[16,48,768]{2,1,0:T(8,128)}), f32[16,48,768]{2,1,0:T(8,128)}, u32[]{:S(2)}, u32[]{:S(2)}) async-start(f32[16,48,768]{2,1,0:T(8,128)} %potential.2), calls=%async_computation.2 | async-start | bytes 4718592 | tf_op jit(solution)/shard_map/all_to_all | solution.py:778
  165.5 9.1 %forward_rows.2.refs_4_ = f32[2,16,48,768]{3,2,1,0:T(8,128)} custom-call(s32[3]{0:T(128)} %add_convert_fusion.refs_5_.refs_0_, f32[16,48,768]{2,1,0:T(8,128)} %all-to-all-done.3.refs_1_, f32[2,4,384]{2,1,0:T(4,128)} %constant.23.clone.refs_1_.refs_2_, f32[2,48,384]{2,1,0:T(8,128)} %constant.24.clone.refs_2_.refs_3_), custom_call_target="tpu_custom_call" | custom-call | flops 10000000000 | bytes 1048576 | tf_op jit(solution)/shard_map/forward_rows/pallas_call | solution.py:764
  174.6 22.9 %all-to-all-done.2.refs_1_ = f32[16,48,768]{2,1,0:T(8,128)} async-done(((f32[16,48,768]{2,1,0:T(8,128)}), f32[16,48,768]{2,1,0:T(8,128)}, u32[]{:S(2)}, u32[]{:S(2)}) %all-to-all-start.2) | async-done | bytes 2359328 | tf_op jit(solution)/shard_map/all_to_all | solution.py:778
  197.5 9.1 %forward_rows.3 = f32[2,16,48,768]{3,2,1,0:T(8,128)} custom-call(s32[3]{0:T(128)} %add_convert_fusion.refs_5_.refs_0_, f32[16,48,768]{2,1,0:T(8,128)} %all-to-all-done.2.refs_1_, f32[2,4,384]{2,1,0:T(4,128)} %constant.23.clone.refs_1_.refs_2_, f32[2,48,384]{2,1,0:T(8,128)} %constant.24.clone.refs_2_.refs_3_, ...), custom_call_target="tpu_custom_call", output_to_operand_aliasing={{}: (4, {})} | custom-call | flops 10000000000 | bytes 1048576 | tf_op jit(solution)/shard_map/forward_rows/pallas_call | solution.py:764
  (20 shorter events, 1.4 us)
Async XLA Ops:
  6.9 38.7 %all-to-all-start = ((f32[16,6,48,128]{3,2,1,0:T(8,128)}), f32[16,6,48,128]{3,2,1,0:T(8,128)}, u32[]{:S(2)}, u32[]{:S(2)}) async-start(f32[16,6,48,128]{3,2,1,0:T(8,128)} %inverse_rows.2), calls=%async_computation | async-start | bytes 4718592 | tf_op jit(solution)/shard_map/all_to_all | solution.py:778
  45.6 39.3 %all-to-all-start.1 = ((f32[16,6,48,128]{3,2,1,0:T(8,128)}), f32[16,6,48,128]{3,2,1,0:T(8,128)}, u32[]{:S(2)}, u32[]{:S(2)}) async-start(f32[16,6,48,128]{3,2,1,0:T(8,128)} %get-tuple-element.23), calls=%async_computation.1 | async-start | bytes 4718592 | tf_op jit(solution)/shard_map/all_to_all | solution.py:778
  59.2 23.4 %collective-permute-start = (f32[24,768]{1,0:T(8,128)}, f32[24,768]{1,0:T(8,128)S(1)}, u32[]{:S(2)}, u32[]{:S(2)}) collective-permute-start(f32[24,768]{1,0:T(8,128)} %get-tuple-element.24), channel_id=1, source_target_pairs={{0,1},{1,2},{2,3},{3,4},{4,5},{5,6},{6,7},{7,8},{8,9},{9,10},{10,1... | collective-permute-start | bytes 221192 | tf_op jit(solution)/shard_map/ppermute | solution.py:403
  59.3 23.3 %collective-permute-start.1 = (f32[24,768]{1,0:T(8,128)}, f32[24,768]{1,0:T(8,128)S(1)}, u32[]{:S(2)}, u32[]{:S(2)}) collective-permute-start(f32[24,768]{1,0:T(8,128)} %get-tuple-element.25), channel_id=1, source_target_pairs={{1,0},{2,1},{3,2},{4,3},{5,4},{6,5},{7,6},{8,7},{9,8},{10,9},{11,1... | collective-permute-start | bytes 221192 | tf_op jit(solution)/shard_map/ppermute | solution.py:403
  82.6 0.6 copy-start.3
  82.6 0.7 copy-start.4
  84.9 16.2 %copy-start.2 = (f32[168,768]{1,0:T(8,128)S(1)}, f32[168,768]{1,0:T(8,128)}, u32[]{:S(2)}) copy-start(f32[168,768]{1,0:T(8,128)} %get-tuple-element.36) | copy-start | bytes 1548292
  93.9 9.3 %collective-permute-start.4 = (f32[24,768]{1,0:T(8,128)}, f32[24,768]{1,0:T(8,128)S(1)}, u32[]{:S(2)}, u32[]{:S(2)}) collective-permute-start(f32[24,768]{1,0:T(8,128)} %get-tuple-element.37), channel_id=1, source_target_pairs={{0,1},{1,2},{2,3},{3,4},{4,5},{5,6},{6,7},{7,8},{8,9},{9,10},{10,1... | collective-permute-start | bytes 221192 | tf_op jit(solution)/shard_map/ppermute | solution.py:403
  94.0 9.3 %collective-permute-start.5 = (f32[24,768]{1,0:T(8,128)}, f32[24,768]{1,0:T(8,128)S(1)}, u32[]{:S(2)}, u32[]{:S(2)}) collective-permute-start(f32[24,768]{1,0:T(8,128)} %get-tuple-element.34), channel_id=1, source_target_pairs={{1,0},{2,1},{3,2},{4,3},{5,4},{6,5},{7,6},{8,7},{9,8},{10,9},{11,1... | collective-permute-start | bytes 221192 | tf_op jit(solution)/shard_map/ppermute | solution.py:403
  95.7 33.1 %collective-permute-start.2 = (f32[168,768]{1,0:T(8,128)}, f32[168,768]{1,0:T(8,128)S(1)}, u32[]{:S(2)}, u32[]{:S(2)}) collective-permute-start(f32[168,768]{1,0:T(8,128)} %get-tuple-element.35), channel_id=1, source_target_pairs={{0,16},{16,32},{32,48},{48,64},{64,80},{80,96},{96,112},{1,17},{17... | collective-permute-start | bytes 1548296 | tf_op jit(solution)/shard_map/ppermute | solution.py:403
  101.1 27.7 %collective-permute-start.3 = (f32[168,768]{1,0:T(8,128)S(1)}, f32[168,768]{1,0:T(8,128)S(1)}, u32[]{:S(2)}, u32[]{:S(2)}) collective-permute-start(f32[168,768]{1,0:T(8,128)S(1)} %copy-done.2), channel_id=1, source_target_pairs={{16,0},{32,16},{48,32},{64,48},{80,64},{96,80},{112,96},{17,1},{33... | collective-permute-start | bytes 1548296 | tf_op jit(solution)/shard_map/ppermute | solution.py:403
  103.2 0.6 copy-start.5
  103.2 0.6 copy-start.6
  124.2 36.9 %all-to-all-start.3 = ((f32[16,48,768]{2,1,0:T(8,128)}), f32[16,48,768]{2,1,0:T(8,128)}, u32[]{:S(2)}, u32[]{:S(2)}) async-start(f32[16,48,768]{2,1,0:T(8,128)} %potential.3), calls=%async_computation.3 | async-start | bytes 4718592 | tf_op jit(solution)/shard_map/all_to_all | solution.py:778
  128.8 0.8 copy-start
  129.6 0.8 copy-start.1
  161.1 36.4 %all-to-all-start.2 = ((f32[16,48,768]{2,1,0:T(8,128)}), f32[16,48,768]{2,1,0:T(8,128)}, u32[]{:S(2)}, u32[]{:S(2)}) async-start(f32[16,48,768]{2,1,0:T(8,128)} %potential.2), calls=%async_computation.2 | async-start | bytes 4718592 | tf_op jit(solution)/shard_map/all_to_all | solution.py:778

commit v9 on v8

--- a/solution.py
+++ b/solution.py
@@ -29,9 +29,9 @@
 in_hbm = pl.BlockSpec(memory_space=pltpu.HBM)
 
 
-def call(body, out, cost, **options):
+def call(body, out, cost, mib=62, **options):
     estimate = pl.CostEstimate(flops=int(cost * 1e9), bytes_accessed=1 << 20, transcendentals=0)
-    limit = pltpu.CompilerParams(vmem_limit_bytes=62 << 20)
+    limit = pltpu.CompilerParams(vmem_limit_bytes=mib << 20)
     return pl.pallas_call(body, out_shape=out, compiler_params=limit, cost_estimate=estimate, **options)
 
 
@@ -669,6 +669,7 @@
         lambda *refs: potential_body(sources, groups, *refs),
         array(*out),
         20.0,
+        52,
         grid=(1,),
         in_specs=[pl.BlockSpec(memory_space=pltpu.SMEM)]
         + [in_hbm] * len(planes)

time: 209 us -> 209 us (level)
  local copies, waits for them, and re-layouts: 2.9 us -> 0.67 us
    unnamed x14, local copies, waits for them, and re-layouts: 2.9 us -> 0.67 us
  transfers between devices with their start and end apart: 10 -> 10, of which waited for: 4 -> 4; matrix products, arithmetic and copies ran while one was open for 0% -> 0% of each run, Pallas kernels for 36% -> 37%
where the time goes in v9:
time: 209 us; the launch traced here: 207 us
  Pallas kernels  101 us (48%)
  waiting for transfers between devices  73.8 us (35%)
  starting transfers between devices  30.7 us (15%)
    all_to_all x4, waiting for transfers between devices, exchange(): return lax.all_to_all(value, 'py', 0, 0, tiled=True)  52.3 us
    pallas_call x2, Pallas kernels, potential_of(): call(lambda *refs: potential_body(sources, groups, *refs), array(*out), 2...  44.8 us
    ppermute x6, waiting for transfers between devices, shift(): lax.ppermute(value, axis, pairs if up else [(b, a) for a, b in pairs])  21.5 us
    all_to_all x4, starting transfers between devices, exchange(): return lax.all_to_all(value, 'py', 0, 0, tiled=True)  19.6 us
    pallas_call x2, Pallas kernels, inverse_columns(): call(lambda *refs: inverse_columns_body(sends, *refs), [array(planes, row...  18.3 us
    pallas_call x2, Pallas kernels, forward_rows(): call(lambda *refs: forward_rows_body(starts, *refs), array(2, depth, rows...  18.2 us
    ppermute x6, starting transfers between devices, shift(): lax.ppermute(value, axis, pairs if up else [(b, a) for a, b in pairs])  11.1 us
    pallas_call x1, Pallas kernels, inverse_rows(): call(body, [array(*out), jax.ShapeDtypeStruct((4, width, width), bf16)],...  10.7 us
  transfers between devices with their start and end apart: 10, of which 4 were waited for; matrix products, arithmetic and copies ran while one was open for 0% of the time, Pallas kernels for 37%

profile of v9, /device:TPU:14, one launch (start us, length us, event | category | flops | bytes accessed | tf_op | source)
XLA Modules:
  0.0 206.7 jit_solution(1750619916714144697)
XLA Ops:
  0.0 6.9 %inverse_rows.2 = f32[16,6,48,128]{3,2,1,0:T(8,128)} custom-call(f32[2,16,48,768]{3,2,1,0:T(8,128)} %refs_0_.3, f32[2,4,384]{2,1,0:T(4,128)} %constant.23.clone.refs_1_.refs_2_, f32[2,48,384]{2,1,0:T(8,128)} %constant.24.clone.refs_2_.refs_3_), custom_call_target="tpu_custom_call" | custom-call | flops 10000000000 | bytes 1048576 | tf_op jit(solution)/shard_map/inverse_rows/pallas_call | solution.py:249
  6.9 6.3 %all-to-all-start = ((f32[16,6,48,128]{3,2,1,0:T(8,128)}), f32[16,6,48,128]{3,2,1,0:T(8,128)}, u32[]{:S(2)}, u32[]{:S(2)}) async-start(f32[16,6,48,128]{3,2,1,0:T(8,128)} %inverse_rows.2), calls=%async_computation | async-start | bytes 4718592 | tf_op jit(solution)/shard_map/all_to_all | solution.py:779
  13.2 0.6 add_convert_fusion.refs_5_.refs_0_
  13.8 10.7 %inverse_rows.3 = (f32[16,6,48,128]{3,2,1,0:T(8,128)}, bf16[4,768,768]{2,1,0:T(8,128)(2,1)}) custom-call(f32[2,16,48,768]{3,2,1,0:T(8,128)} %refs_0_.3, f32[2,4,384]{2,1,0:T(4,128)} %constant.23.clone.refs_1_.refs_2_, f32[2,48,384]{2,1,0:T(8,128)} %constant.24.clone.refs_2_.refs_3_, f32[2,6,768]{2,1,0:T(8,128)} %constant.21.clone.refs_1_.refs_3_, ...), custom_call_target="tpu_custom_call" | custom-call | flops 10000000000 | bytes 1048576 | tf_op jit(solution)/shard_map/inverse_rows/pallas_call | solution.py:239
  24.5 21.1 %all-to-all-done.refs_0_ = f32[16,6,48,128]{3,2,1,0:T(8,128)} async-done(((f32[16,6,48,128]{3,2,1,0:T(8,128)}), f32[16,6,48,128]{3,2,1,0:T(8,128)}, u32[]{:S(2)}, u32[]{:S(2)}) %all-to-all-start) | async-done | bytes 2359328 | tf_op jit(solution)/shard_map/all_to_all | solution.py:779
  45.6 4.3 %all-to-all-start.1 = ((f32[16,6,48,128]{3,2,1,0:T(8,128)}), f32[16,6,48,128]{3,2,1,0:T(8,128)}, u32[]{:S(2)}, u32[]{:S(2)}) async-start(f32[16,6,48,128]{3,2,1,0:T(8,128)} %get-tuple-element.23), calls=%async_computation.1 | async-start | bytes 4718592 | tf_op jit(solution)/shard_map/all_to_all | solution.py:779
  50.0 9.3 %inverse_columns.2 = (f32[8,48,768]{2,1,0:T(8,128)}, f32[24,768]{1,0:T(8,128)}, f32[24,768]{1,0:T(8,128)}, f32[168,768]{1,0:T(8,128)}, f32[168,768]{1,0:T(8,128)}) custom-call(f32[16,6,48,128]{3,2,1,0:T(8,128)} %all-to-all-done.refs_0_, f32[2,6,768]{2,1,0:T(8,128)} %constant.21.clone.refs_1_.refs_3_, f32[2,48,768]{2,1,0:T(8,128)} %constant.22.clone.refs_2_.refs_4_), custom_call_target="tpu_custom_call" | custom-call | flops 7000000000 | bytes 1048576 | tf_op jit(solution)/shard_map/inverse_columns/pallas_call | solution.py:387
  59.2 0.1 collective-permute-start
  59.3 1.7 collective-permute-start.1
  61.0 21.5 %collective-permute-done.head_ref.refs_5_.refs_3_ = f32[24,768]{1,0:T(8,128)S(1)} collective-permute-done((f32[24,768]{1,0:T(8,128)}, f32[24,768]{1,0:T(8,128)S(1)}, u32[]{:S(2)}, u32[]{:S(2)}) %collective-permute-start) | collective-permute-done | bytes 73760 | tf_op jit(solution)/shard_map/ppermute | solution.py:403
  82.6 0.6 copy-done.1
  83.2 1.6 halo_slabs.1
  84.9 9.0 %inverse_columns.3 = (f32[8,48,768]{2,1,0:T(8,128)}, f32[24,768]{1,0:T(8,128)}, f32[24,768]{1,0:T(8,128)}) custom-call(f32[16,6,48,128]{3,2,1,0:T(8,128)} %all-to-all-done.1.refs_0_, f32[2,6,768]{2,1,0:T(8,128)} %constant.21.clone.refs_1_.refs_3_, f32[2,48,768]{2,1,0:T(8,128)} %constant.22.clone.refs_2_.refs_4_), custom_call_target="tpu_custom_call" | custom-call | flops 7000000000 | bytes 1048576 | tf_op jit(solution)/shard_map/inverse_columns/pallas_call | solution.py:387
  94.1 1.7 collective-permute-start.5
  95.8 5.4 %collective-permute-start.2 = (f32[168,768]{1,0:T(8,128)}, f32[168,768]{1,0:T(8,128)S(1)}, u32[]{:S(2)}, u32[]{:S(2)}) collective-permute-start(f32[168,768]{1,0:T(8,128)} %get-tuple-element.35), channel_id=1, source_target_pairs={{0,16},{16,32},{32,48},{48,64},{64,80},{80,96},{96,112},{1,17},{17... | collective-permute-start | bytes 1548296 | tf_op jit(solution)/shard_map/ppermute | solution.py:403
  101.2 2.1 %collective-permute-start.3 = (f32[168,768]{1,0:T(8,128)S(1)}, f32[168,768]{1,0:T(8,128)S(1)}, u32[]{:S(2)}, u32[]{:S(2)}) collective-permute-start(f32[168,768]{1,0:T(8,128)S(1)} %copy-done.6), channel_id=1, source_target_pairs={{16,0},{32,16},{48,32},{64,48},{80,64},{96,80},{112,96},{17,1},{33... | collective-permute-start | bytes 1548296 | tf_op jit(solution)/shard_map/ppermute | solution.py:403
  103.4 20.7 %potential.3 = f32[16,48,768]{2,1,0:T(8,128)} custom-call(s32[3]{0:T(128)S(1)} %copy-done, f32[8,48,768]{2,1,0:T(8,128)S(1)} %copy-done.5, f32[8,48,768]{2,1,0:T(8,128)} %get-tuple-element.31.refs_2_, f32[24,768]{1,0:T(8,128)S(1)} %copy-done.2, f32[24,768]{1,0:T(8,128)S(1)} %copy-done.4, f32[24,768]{1,0:T(8,128)S(1)} %collective-permute-done.4.refs_7_.refs_5_, ...), custom_call_target="tpu_custom_call" | custom-call | flops 20000000000 | bytes 1048576 | tf_op jit(solution)/shard_map/potential/pallas_call | solution.py:668
  124.1 4.6 %all-to-all-start.3 = ((f32[16,48,768]{2,1,0:T(8,128)}), f32[16,48,768]{2,1,0:T(8,128)}, u32[]{:S(2)}, u32[]{:S(2)}) async-start(f32[16,48,768]{2,1,0:T(8,128)} %potential.3), calls=%async_computation.3 | async-start | bytes 4718592 | tf_op jit(solution)/shard_map/all_to_all | solution.py:779
  128.7 24.1 %potential.2 = f32[16,48,768]{2,1,0:T(8,128)} custom-call(s32[3]{0:T(128)S(1)} %copy-done, f32[8,48,768]{2,1,0:T(8,128)} %get-tuple-element.22.refs_1_, f32[8,48,768]{2,1,0:T(8,128)} %get-tuple-element.31.refs_2_, f32[168,768]{1,0:T(8,128)S(1)} %collective-permute-done.2.refs_3_.refs_9_, f32[168,768]{1,0:T(8,128)S(1)} %collective-permute-done.3.refs_4_.refs_10_, ...), custom_call_target="tpu_custom_call" | custom-call | flops 20000000000 | bytes 1048576 | tf_op jit(solution)/shard_map/potential/pallas_call | solution.py:668
  152.8 8.2 %all-to-all-done.3.refs_1_ = f32[16,48,768]{2,1,0:T(8,128)} async-done(((f32[16,48,768]{2,1,0:T(8,128)}), f32[16,48,768]{2,1,0:T(8,128)}, u32[]{:S(2)}, u32[]{:S(2)}) %all-to-all-start.3) | async-done | bytes 2359328 | tf_op jit(solution)/shard_map/all_to_all | solution.py:779
  161.0 4.4 %all-to-all-start.2 = ((f32[16,48,768]{2,1,0:T(8,128)}), f32[16,48,768]{2,1,0:T(8,128)}, u32[]{:S(2)}, u32[]{:S(2)}) async-start(f32[16,48,768]{2,1,0:T(8,128)} %potential.2), calls=%async_computation.2 | async-start | bytes 4718592 | tf_op jit(solution)/shard_map/all_to_all | solution.py:779
  165.4 9.1 %forward_rows.2.refs_4_ = f32[2,16,48,768]{3,2,1,0:T(8,128)} custom-call(s32[3]{0:T(128)} %add_convert_fusion.refs_5_.refs_0_, f32[16,48,768]{2,1,0:T(8,128)} %all-to-all-done.3.refs_1_, f32[2,4,384]{2,1,0:T(4,128)} %constant.23.clone.refs_1_.refs_2_, f32[2,48,384]{2,1,0:T(8,128)} %constant.24.clone.refs_2_.refs_3_), custom_call_target="tpu_custom_call" | custom-call | flops 10000000000 | bytes 1048576 | tf_op jit(solution)/shard_map/forward_rows/pallas_call | solution.py:765
  174.5 22.9 %all-to-all-done.2.refs_1_ = f32[16,48,768]{2,1,0:T(8,128)} async-done(((f32[16,48,768]{2,1,0:T(8,128)}), f32[16,48,768]{2,1,0:T(8,128)}, u32[]{:S(2)}, u32[]{:S(2)}) %all-to-all-start.2) | async-done | bytes 2359328 | tf_op jit(solution)/shard_map/all_to_all | solution.py:779
  197.4 9.1 %forward_rows.3 = f32[2,16,48,768]{3,2,1,0:T(8,128)} custom-call(s32[3]{0:T(128)} %add_convert_fusion.refs_5_.refs_0_, f32[16,48,768]{2,1,0:T(8,128)} %all-to-all-done.2.refs_1_, f32[2,4,384]{2,1,0:T(4,128)} %constant.23.clone.refs_1_.refs_2_, f32[2,48,384]{2,1,0:T(8,128)} %constant.24.clone.refs_2_.refs_3_, ...), custom_call_target="tpu_custom_call", output_to_operand_aliasing={{}: (4, {})} | custom-call | flops 10000000000 | bytes 1048576 | tf_op jit(solution)/shard_map/forward_rows/pallas_call | solution.py:765
  (20 shorter events, 0.1 us)
Async XLA Ops:
  6.9 38.7 %all-to-all-start = ((f32[16,6,48,128]{3,2,1,0:T(8,128)}), f32[16,6,48,128]{3,2,1,0:T(8,128)}, u32[]{:S(2)}, u32[]{:S(2)}) async-start(f32[16,6,48,128]{3,2,1,0:T(8,128)} %inverse_rows.2), calls=%async_computation | async-start | bytes 4718592 | tf_op jit(solution)/shard_map/all_to_all | solution.py:779
  45.6 39.2 %all-to-all-start.1 = ((f32[16,6,48,128]{3,2,1,0:T(8,128)}), f32[16,6,48,128]{3,2,1,0:T(8,128)}, u32[]{:S(2)}, u32[]{:S(2)}) async-start(f32[16,6,48,128]{3,2,1,0:T(8,128)} %get-tuple-element.23), calls=%async_computation.1 | async-start | bytes 4718592 | tf_op jit(solution)/shard_map/all_to_all | solution.py:779
  59.2 23.3 %collective-permute-start = (f32[24,768]{1,0:T(8,128)}, f32[24,768]{1,0:T(8,128)S(1)}, u32[]{:S(2)}, u32[]{:S(2)}) collective-permute-start(f32[24,768]{1,0:T(8,128)} %get-tuple-element.24), channel_id=1, source_target_pairs={{0,1},{1,2},{2,3},{3,4},{4,5},{5,6},{6,7},{7,8},{8,9},{9,10},{10,1... | collective-permute-start | bytes 221192 | tf_op jit(solution)/shard_map/ppermute | solution.py:403
  59.3 23.3 %collective-permute-start.1 = (f32[24,768]{1,0:T(8,128)}, f32[24,768]{1,0:T(8,128)S(1)}, u32[]{:S(2)}, u32[]{:S(2)}) collective-permute-start(f32[24,768]{1,0:T(8,128)} %get-tuple-element.25), channel_id=1, source_target_pairs={{1,0},{2,1},{3,2},{4,3},{5,4},{6,5},{7,6},{8,7},{9,8},{10,9},{11,1... | collective-permute-start | bytes 221192 | tf_op jit(solution)/shard_map/ppermute | solution.py:403
  82.6 0.6 copy-start.1
  82.6 0.7 copy-start.3
  84.9 16.3 %copy-start.6 = (f32[168,768]{1,0:T(8,128)S(1)}, f32[168,768]{1,0:T(8,128)}, u32[]{:S(2)}) copy-start(f32[168,768]{1,0:T(8,128)} %get-tuple-element.36) | copy-start | bytes 1548292
  84.9 18.5 %copy-start = (s32[3]{0:T(128)S(1)}, s32[3]{0:T(128)}, u32[]{:S(2)}) copy-start(s32[3]{0:T(128)} %add_convert_fusion.refs_5_.refs_0_) | copy-start | bytes 40
  84.9 18.5 %copy-start.2 = (f32[24,768]{1,0:T(8,128)S(1)}, f32[24,768]{1,0:T(8,128)}, u32[]{:S(2)}) copy-start(f32[24,768]{1,0:T(8,128)} %copy-done.1) | copy-start | bytes 221188
  84.9 18.5 %copy-start.4 = (f32[24,768]{1,0:T(8,128)S(1)}, f32[24,768]{1,0:T(8,128)}, u32[]{:S(2)}) copy-start(f32[24,768]{1,0:T(8,128)} %copy-done.3) | copy-start | bytes 221188
  84.9 18.5 %copy-start.5 = (f32[8,48,768]{2,1,0:T(8,128)S(1)}, f32[8,48,768]{2,1,0:T(8,128)}, u32[]{:S(2)}) copy-start(f32[8,48,768]{2,1,0:T(8,128)} %get-tuple-element.22.refs_1_) | copy-start | bytes 3538948
  94.0 9.3 %collective-permute-start.4 = (f32[24,768]{1,0:T(8,128)}, f32[24,768]{1,0:T(8,128)S(1)}, u32[]{:S(2)}, u32[]{:S(2)}) collective-permute-start(f32[24,768]{1,0:T(8,128)} %get-tuple-element.37), channel_id=1, source_target_pairs={{0,1},{1,2},{2,3},{3,4},{4,5},{5,6},{6,7},{7,8},{8,9},{9,10},{10,1... | collective-permute-start | bytes 221192 | tf_op jit(solution)/shard_map/ppermute | solution.py:403
  94.1 9.3 %collective-permute-start.5 = (f32[24,768]{1,0:T(8,128)}, f32[24,768]{1,0:T(8,128)S(1)}, u32[]{:S(2)}, u32[]{:S(2)}) collective-permute-start(f32[24,768]{1,0:T(8,128)} %get-tuple-element.34), channel_id=1, source_target_pairs={{1,0},{2,1},{3,2},{4,3},{5,4},{6,5},{7,6},{8,7},{9,8},{10,9},{11,1... | collective-permute-start | bytes 221192 | tf_op jit(solution)/shard_map/ppermute | solution.py:403
  95.8 32.9 %collective-permute-start.2 = (f32[168,768]{1,0:T(8,128)}, f32[168,768]{1,0:T(8,128)S(1)}, u32[]{:S(2)}, u32[]{:S(2)}) collective-permute-start(f32[168,768]{1,0:T(8,128)} %get-tuple-element.35), channel_id=1, source_target_pairs={{0,16},{16,32},{32,48},{48,64},{64,80},{80,96},{96,112},{1,17},{17... | collective-permute-start | bytes 1548296 | tf_op jit(solution)/shard_map/ppermute | solution.py:403
  101.2 27.5 %collective-permute-start.3 = (f32[168,768]{1,0:T(8,128)S(1)}, f32[168,768]{1,0:T(8,128)S(1)}, u32[]{:S(2)}, u32[]{:S(2)}) collective-permute-start(f32[168,768]{1,0:T(8,128)S(1)} %copy-done.6), channel_id=1, source_target_pairs={{16,0},{32,16},{48,32},{64,48},{80,64},{96,80},{112,96},{17,1},{33... | collective-permute-start | bytes 1548296 | tf_op jit(solution)/shard_map/ppermute | solution.py:403
  124.1 36.9 %all-to-all-start.3 = ((f32[16,48,768]{2,1,0:T(8,128)}), f32[16,48,768]{2,1,0:T(8,128)}, u32[]{:S(2)}, u32[]{:S(2)}) async-start(f32[16,48,768]{2,1,0:T(8,128)} %potential.3), calls=%async_computation.3 | async-start | bytes 4718592 | tf_op jit(solution)/shard_map/all_to_all | solution.py:779
  161.0 36.4 %all-to-all-start.2 = ((f32[16,48,768]{2,1,0:T(8,128)}), f32[16,48,768]{2,1,0:T(8,128)}, u32[]{:S(2)}, u32[]{:S(2)}) async-start(f32[16,48,768]{2,1,0:T(8,128)} %potential.2), calls=%async_computation.2 | async-start | bytes 4718592 | tf_op jit(solution)/shard_map/all_to_all | solution.py:779
